TPU v7x, 32 devices: a whole 2x2x4 slice. The times are simulated.
32 devices in a mesh: fsdp: 8 (over z, x), tensor: 4 (over y, core).
Axes of the slice: x: 2, y: 2, z: 4, core: 2. Of those that a mesh axis runs over, the one named last changes fastest.
Arguments:
- hidden_in: bfloat16 [8192, 768], P(('fsdp', 'tensor')), may hold values from -6 to 6
- time_embed: bfloat16 [8, 768], P('fsdp'), may hold values from -6 to 6
- segment_ids: int32 [8, 1024], P('fsdp'), may hold values from -1 to 7, as said below
- cotangent: bfloat16 [8192, 768], P(('fsdp', 'tensor')), may hold values from -6 to 6
- query_weight: bfloat16 [2, 768, 768], P(None, 'fsdp', 'tensor'), may hold values from -0.21875 to 0.21875
- key_weight: bfloat16 [2, 768, 768], P(None, 'fsdp', 'tensor'), may hold values from -0.21875 to 0.21875
- value_weight: bfloat16 [2, 768, 768], P(None, 'fsdp', 'tensor'), may hold values from -0.21875 to 0.21875
- output_weight: bfloat16 [2, 768, 768], P(None, 'tensor', 'fsdp'), may hold values from -1.75 to 1.75
- up_weight: bfloat16 [2, 768, 3072], P(None, 'fsdp', 'tensor'), may hold values from -0.21875 to 0.21875
- down_weight: bfloat16 [2, 3072, 768], P(None, 'tensor', 'fsdp'), may hold values from -0.109375 to 0.109375
- query_bias: float32 [2, 768], P(None, 'tensor'), may hold values from -3 to 3
- value_bias: float32 [2, 768], P(None, 'tensor'), may hold values from -3 to 3
- output_bias: float32 [2, 768], replicated, may hold values from -3 to 3
- up_bias: float32 [2, 3072], P(None, 'tensor'), may hold values from -3 to 3
- down_bias: float32 [2, 768], replicated, may hold values from -3 to 3
- first_gain: float32 [2, 768], replicated, may hold values from 0.25 to 1.75
- first_shift: float32 [2, 768], replicated, may hold values from -3 to 3
- second_gain: float32 [2, 768], replicated, may hold values from 0.25 to 1.75
- second_shift: float32 [2, 768], replicated, may hold values from -3 to 3
Outputs:
- denoised: bfloat16 [8192, 768], P(('fsdp', 'tensor'))
- input_grad: float32 [8192, 768], P(('fsdp', 'tensor'))
- query_weight_grad: float32 [2, 768, 768], P(None, 'fsdp', 'tensor')
- key_weight_grad: float32 [2, 768, 768], P(None, 'fsdp', 'tensor')
- value_weight_grad: float32 [2, 768, 768], P(None, 'fsdp', 'tensor')
- output_weight_grad: float32 [2, 768, 768], P(None, 'tensor', 'fsdp')
- up_weight_grad: float32 [2, 768, 3072], P(None, 'fsdp', 'tensor')
- down_weight_grad: float32 [2, 3072, 768], P(None, 'tensor', 'fsdp')
- query_bias_grad: float32 [2, 768], P(None, 'tensor')
- value_bias_grad: float32 [2, 768], P(None, 'tensor')
- output_bias_grad: float32 [2, 768], replicated
- up_bias_grad: float32 [2, 3072], P(None, 'tensor')
- down_bias_grad: float32 [2, 768], replicated
- first_gain_grad: float32 [2, 768], replicated
- first_shift_grad: float32 [2, 768], replicated
- second_gain_grad: float32 [2, 768], replicated
- second_shift_grad: float32 [2, 768], replicated
Inputs may be any that keep to these rules, and one draw needn't show every extreme that they name: `segment_ids`: each sequence holds 8 documents of at least one token in order 0 to 7, followed by padding of at least one token.
All inputs are finite; a program needn't handle non-finite values.
Results may differ from a plain program's by a relative error of at most 0.015.
Values may be sent and summed in bfloat16 or wider, within the bound.
No kernel may reach another device: no remote copies, remote signals or barrier semaphores. Data moves between devices by JAX's collectives and lax.ppermute only.
A program may use at most 192 MiB of HBM per device.

v0:
```python
import functools

import jax
import jax.numpy as jnp
from jax import lax
from jax.experimental import pallas as pl
from jax.experimental.pallas import tpu as pltpu
from jax.sharding import PartitionSpec as P

HEAD_DIM = 64
EPSILON = 1e-05
LOW = jnp.bfloat16
WIDE = jnp.float32
ROOT = 0.7978845608028654
CUBE = 0.044715

SWAP_CORE = [(0, 1), (1, 0), (2, 3), (3, 2)]
SWAP_Y = [(0, 2), (2, 0), (1, 3), (3, 1)]


def swap_core(value):
    return lax.ppermute(value, "tensor", SWAP_CORE)


def swap_y(value):
    return lax.ppermute(value, "tensor", SWAP_Y)


def dot(a, b):
    return jnp.dot(a, b, preferred_element_type=WIDE)


def dot_nt(a, b):
    return lax.dot_general(a, b, (((1,), (1,)), ((), ())), preferred_element_type=WIDE)


def dot_tn(a, b):
    return lax.dot_general(a, b, (((0,), (0,)), ((), ())), preferred_element_type=WIDE)


def tie(*values):
    return lax.optimization_barrier(values)


def ring_order(count):
    return list(range(0, count, 2)) + list(range(count - 1, 0, -2))


class Ring:
    def __init__(self):
        self.count = lax.axis_size("fsdp")
        self.use = self.count == 8
        self.core = lax.axis_index("tensor") % 2
        if self.use:
            here = lax.axis_index("fsdp")
            self.place = jnp.where(here % 2 == 0, here // 2, self.count - 1 - here // 2)
            self.way = 1 - 2 * self.core
            self.far = self.count // 2
            order = ring_order(self.count)
            self.pairs = [
                [(order[i], order[(i + way) % self.count]) for i in range(self.count)]
                for way in (1, -1)
            ]
            self.split = [
                (here * 4 + t, there * 4 + t)
                for t in range(4)
                for here, there in self.pairs[t % 2]
            ]
            self.blocks = jnp.stack([self.block_at(step) for step in range(self.count)])

    def split_send(self, value):
        return lax.ppermute(value, ("fsdp", "tensor"), self.split)

    def send_both(self, ahead, behind):
        return lax.ppermute(ahead, "fsdp", self.pairs[0]), lax.ppermute(behind, "fsdp", self.pairs[1])

    def block_at(self, steps):
        place = (self.place + steps + 2 * self.count) % self.count
        return jnp.where(place < self.count // 2, 2 * place, 2 * (self.count - 1 - place) + 1)


class Gather:
    def __init__(self, ring, piece):
        self.ring = ring
        self.rows, self.columns = piece.shape
        self.todo = []
        self.done = 0
        if ring.use:
            self.whole = jnp.zeros((ring.count * self.rows, self.columns), piece.dtype)
            self.put(piece, lax.axis_index("fsdp"))
            self.current = piece
        else:
            self.whole = lax.all_gather(piece, "fsdp", axis=0, tiled=True)

    def put(self, value, block, offset=0):
        start = block * self.rows + offset
        self.whole = lax.dynamic_update_slice(self.whole, value, (start, 0))

    def flush(self):
        ring = self.ring
        half = self.rows // 2
        for step, value in self.todo:
            if step < ring.far:
                self.put(value, ring.block_at(-ring.way * step))
                self.put(swap_core(value), ring.block_at(ring.way * step))
            else:
                block = ring.block_at(step)
                self.put(value, block, ring.core * half)
                self.put(swap_core(value), block, (1 - ring.core) * half)
        self.todo = []

    def step(self, token=None):
        ring = self.ring
        if not ring.use or self.done == ring.far:
            return
        self.flush()
        self.done += 1
        current = self.current
        if token is not None:
            current, _ = tie(current, token)
        if self.done == ring.far:
            half = self.rows // 2
            current = lax.dynamic_slice(current, (ring.core * half, 0), (half, self.columns))
        self.current = ring.split_send(current)
        self.todo.append((self.done, self.current))

    def finish(self):
        if self.ring.use:
            while self.done < self.ring.far:
                self.step()
            self.flush()


class Scatter:
    def __init__(self, ring, owns, gots):
        self.ring = ring
        self.owns, self.gots = owns, gots
        self.done = 0
        if ring.use:
            self.rows = owns[0].shape[0] // ring.count
        else:
            total = jnp.concatenate(
                [own.astype(WIDE) + got.astype(WIDE) for own, got in zip(owns, gots)], axis=1
            )
            self.result = lax.psum_scatter(total, "fsdp", scatter_dimension=0, tiled=True)

    def step(self, main=None):
        ring = self.ring
        if not ring.use or self.done == ring.far:
            return main
        moving = self.moving if self.done else None
        ahead, behind = ring.send_both(
            *passing(ring.blocks, self.owns, self.gots, ring.far - self.done, ring.count, moving)
        )
        if main is not None:
            main, ahead, behind = tie(main, ahead, behind)
        self.moving = (ahead, behind)
        self.done += 1
        if self.done == ring.far:
            self.result = passing(ring.blocks, self.owns, self.gots, 0, ring.count, self.moving)[0]
        return main

    def finish(self):
        if self.ring.use:
            while self.done < self.ring.far:
                self.step()
        return self.result


def exchanges(count):
    moves = [swap_core, swap_y]
    bit = 1
    while bit < count:
        pairs = [(i, i ^ bit) for i in range(count)]
        moves.append(lambda value, pairs=pairs: lax.ppermute(value, "fsdp", pairs))
        bit *= 2
    return moves


ROOM = 16 << 20
NEVER = -1e30


def out(shape, dtype=LOW):
    return jax.ShapeDtypeStruct(shape, dtype)


def kernel_call(kernel, operands, outs, scratch=(), scalars=0, cost=1.0):
    inside = pl.BlockSpec(memory_space=pltpu.VMEM)
    word = pl.BlockSpec(memory_space=pltpu.SMEM)
    return pl.pallas_call(
        kernel,
        in_specs=[word] * scalars + [inside] * (len(operands) - scalars),
        out_specs=[inside] * len(outs),
        out_shape=outs,
        scratch_shapes=scratch,
        compiler_params=pltpu.CompilerParams(vmem_limit_bytes=ROOM),
        cost_estimate=pl.CostEstimate(
            flops=int(cost * 1e9), bytes_accessed=1024, transcendentals=0
        ),
    )(*operands)


def norm_parts(rows):
    center = rows - jnp.mean(rows, axis=1, keepdims=True)
    factor = lax.rsqrt(jnp.mean(center * center, axis=1, keepdims=True) + EPSILON)
    return center * factor, factor


def norm_backward(grad, rows, gain):
    normed, factor = norm_parts(rows)
    scaled = grad * gain
    through = factor * (
        scaled
        - jnp.mean(scaled, axis=1, keepdims=True)
        - normed * jnp.mean(scaled * normed, axis=1, keepdims=True)
    )
    gain_grad = jnp.sum(grad * normed, axis=0, keepdims=True)
    return gain_grad, jnp.sum(grad, axis=0, keepdims=True), through


def gelu_both(pre):
    inner = jnp.tanh(ROOT * (pre + CUBE * pre * pre * pre))
    slope = 0.5 * (1.0 + inner) + 0.5 * pre * (1.0 - inner * inner) * (
        ROOT * (1.0 + 3.0 * CUBE * pre * pre)
    )
    return 0.5 * pre * (1.0 + inner), slope


def project(layer, base, part, arrived, bias, gain, shift, weights, q_bias, v_bias):
    rows, depth = base.shape
    width = q_bias.shape[1]
    scale = HEAD_DIM ** (-0.5)
    at = slice(layer, layer + 1)

    def kernel(base_ref, part_ref, arrived_ref, bias_ref, gain_ref, shift_ref, w_ref, qb_ref, vb_ref,
               state_ref, first_ref, q_ref, kv_ref):
        state = base_ref[...] + (part_ref[...].astype(WIDE) + arrived_ref[...].astype(WIDE))
        state += bias_ref[layer - 1 : layer, :]
        first = (norm_parts(state)[0] * gain_ref[at, :] + shift_ref[at, :]).astype(LOW)
        state_ref[...] = state
        first_ref[...] = first
        query = (dot(first, w_ref[:, :width]) + qb_ref[at, :]).astype(LOW)
        q_ref[...] = query * jnp.asarray(scale, LOW)
        kv_ref[:, :width] = dot(first, w_ref[:, width : 2 * width]).astype(LOW)
        kv_ref[:, width:] = (dot(first, w_ref[:, 2 * width : 3 * width]) + vb_ref[at, :]).astype(LOW)

    return kernel_call(
        kernel,
        (base, part, arrived, bias, gain, shift, weights, q_bias, v_bias),
        [
            out((rows, depth), WIDE),
            out((rows, depth)),
            out((rows, width)),
            out((rows, 2 * width)),
        ], cost=1.2)


def feed(layer, state, part, arrived, out_bias, gain, shift, weights, up_bias, lows=None):
    rows, depth = state.shape
    hidden = up_bias.shape[1]
    back = lows is not None
    half = hidden // 2
    tile = 384
    row = slice(layer, layer + 1)

    def kernel(*refs):
        state_ref, part_ref, arrived_ref, ob_ref, gain_ref, shift_ref, w_ref, ub_ref = refs[:8]
        refs = refs[8:]
        middle = (
            state_ref[...] + (part_ref[...].astype(WIDE) + arrived_ref[...].astype(WIDE)) + ob_ref[row, :]
        )
        second = (norm_parts(middle)[0] * gain_ref[row, :] + shift_ref[row, :]).astype(LOW)
        if back:
            lows_ref, middle_ref, second_ref, act_ref, other_ref, branch_ref, ubg_ref = refs
            low = lows_ref[...]
        else:
            middle_ref, second_ref, act_ref, other_ref, branch_ref = refs
        middle_ref[...] = middle
        second_ref[...] = second
        total = None
        for start in range(0, hidden, tile):
            at = slice(start, start + tile)
            inside = start + start // half * half
            up = w_ref[:, inside : inside + tile]
            down = w_ref[:, half + inside : half + inside + tile]
            act, slope = gelu_both(dot(second, up) + ub_ref[row, at])
            act = act.astype(LOW)
            act_ref[:, at] = act
            if back:
                other = (dot(low, down) * slope).astype(LOW)
                ubg_ref[0:1, at] = jnp.sum(other.astype(WIDE), axis=0, keepdims=True)
                here = dot_nt(other, up)
            else:
                other = slope.astype(LOW)
                here = dot_nt(act, down)
            other_ref[:, at] = other
            total = here if total is None else total + here
        branch_ref[...] = total.astype(LOW)

    operands = [state, part, arrived, out_bias, gain, shift, weights, up_bias]
    outs = [
        out((rows, depth), WIDE),
        out((rows, depth)),
        out((rows, hidden)),
        out((rows, hidden)),
        out((rows, depth)),
    ]
    if back:
        operands.append(lows)
        outs.append(out((8, hidden), WIDE))
    return kernel_call(kernel, operands, outs, cost=4.0)


def feed_back(layer, g_middle, part, arrived, state, gain, slopes, weights):
    rows, depth = state.shape
    hidden = slopes.shape[1]
    half = hidden // 2
    tile = 384

    def kernel(gm_ref, part_ref, arrived_ref, state_ref, gain_ref, slope_ref, w_ref,
               grad_ref, low_ref, gpre_ref, branch_ref, sums_ref, ubg_ref):
        incoming = part_ref[...].astype(WIDE) + arrived_ref[...].astype(WIDE)
        gain_grad, shift_grad, through = norm_backward(incoming, state_ref[...], gain_ref[layer : layer + 1, :])
        grad = gm_ref[...] + through
        low = grad.astype(LOW)
        grad_ref[...] = grad
        low_ref[...] = low
        sums_ref[0:1, :] = gain_grad
        sums_ref[1:2, :] = shift_grad
        sums_ref[2:3, :] = jnp.sum(grad, axis=0, keepdims=True)
        total = None
        for start in range(0, hidden, tile):
            at = slice(start, start + tile)
            inside = start + start // half * half
            up = w_ref[:, inside : inside + tile]
            down = w_ref[:, half + inside : half + inside + tile]
            gpre = (dot(low, down) * slope_ref[:, at].astype(WIDE)).astype(LOW)
            gpre_ref[:, at] = gpre
            ubg_ref[0:1, at] = jnp.sum(gpre.astype(WIDE), axis=0, keepdims=True)
            here = dot_nt(gpre, up)
            total = here if total is None else total + here
        branch_ref[...] = total.astype(LOW)

    return kernel_call(
        kernel,
        (g_middle, part, arrived, state, gain, slopes, weights),
        [
            out((rows, depth), WIDE),
            out((rows, depth)),
            out((rows, hidden)),
            out((rows, depth)),
            out((8, depth), WIDE),
            out((8, hidden), WIDE),
        ], cost=3.8)

def turned(value):
    return value.astype(WIDE).T.astype(LOW)


def outer_feed(core, seconds, g_pres, lows, acts, which):
    depth = seconds[0].shape[1]
    size = acts[0].shape[1] // 2

    def kernel(core_ref, s0, s1, g0, g1, l0, l1, a0, a1, out_ref):
        start = jnp.where(core_ref[0] == which, 0, size)
        for index, (left_refs, right_refs) in enumerate((((s0, s1), (g0, g1)), ((l0, l1), (a0, a1)))):
            left = jnp.concatenate([turned(ref[...]) for ref in left_refs], axis=1)
            for at in range(0, size, 384):
                columns = pl.ds(pl.multiple_of(start + at, 128), 384)
                right = jnp.concatenate([ref[:, columns] for ref in right_refs])
                base = index * size + at
                out_ref[:, base : base + 384] = dot(left, right).astype(LOW)

    return kernel_call(
        kernel,
        (core, *seconds, *g_pres, *lows, *acts),
        [out((depth, 2 * size))],
        scalars=1,
        cost=2.0,
    )[0]


def outer_heads(core, firsts, g_qkv, m_lows, mixeds, which):
    depth = firsts[0].shape[1]
    width = mixeds[0].shape[1]
    size = width // 2

    def kernel(core_ref, f0, f1, g_ref, l0, l1, m0, m1, out_ref):
        low = core_ref[0] == which

        def pick(value):
            return jnp.where(low, value[:, :size], value[:, size:])

        first = jnp.concatenate([turned(f0[...]), turned(f1[...])], axis=1)
        g = g_ref[...]
        right = jnp.concatenate(
            [pick(g[:, i * width : (i + 1) * width]) for i in range(3)], axis=1
        )
        m_low = jnp.concatenate([turned(l0[...]), turned(l1[...])], axis=1)
        mixed = jnp.concatenate([pick(m0[...]), pick(m1[...])])
        out_ref[...] = jnp.concatenate([dot(first, right), dot(m_low, mixed)], axis=1).astype(LOW)

    return kernel_call(
        kernel, (core, *firsts, g_qkv, *m_lows, *mixeds), [out((depth, 4 * size))], scalars=1, cost=1.8)[0]


def passing(blocks, owns, gots, step, count, moving):
    parts = len(owns)
    rows = owns[0].shape[0] // count
    half = rows // 2
    columns = sum(own.shape[1] for own in owns)
    first = moving is None
    last = step == 0
    partial_in = not first and moving[0].shape[0] == half

    def kernel(blocks_ref, *refs):
        own_refs, got_refs = refs[:parts], refs[parts : 2 * parts]
        rest = refs[2 * parts :]
        moving_refs, out_refs = (rest[:2], rest[2:]) if not first else ((), rest)

        def here(index, offset=0, size=rows):
            start = pl.multiple_of(blocks_ref[index] * rows + offset, 16)
            at = pl.ds(start, size)
            return jnp.concatenate(
                [
                    own[at, :].astype(WIDE) + got[at, :].astype(WIDE)
                    for own, got in zip(own_refs, got_refs)
                ],
                axis=1,
            )

        if first:
            out_refs[0][...] = here(step, 0, half).astype(LOW)
            out_refs[1][...] = here(step, half, half).astype(LOW)
        elif last:
            total = here(0) + moving_refs[0][...].astype(WIDE) + moving_refs[1][...].astype(WIDE)
            out_refs[0][...] = total
        else:
            ahead, behind = here(step), here((count - step) % count)
            a, b = moving_refs[0][...].astype(WIDE), moving_refs[1][...].astype(WIDE)
            if partial_in:
                out_refs[0][:half, :] = (ahead[:half] + a).astype(LOW)
                out_refs[0][half:, :] = ahead[half:].astype(LOW)
                out_refs[1][:half, :] = behind[:half].astype(LOW)
                out_refs[1][half:, :] = (behind[half:] + b).astype(LOW)
            else:
                out_refs[0][...] = (ahead + a).astype(LOW)
                out_refs[1][...] = (behind + b).astype(LOW)

    if last:
        outs = [out((rows, columns), WIDE)]
    else:
        outs = [out((half if first else rows, columns))] * 2
    operands = (blocks, *owns, *gots) + (() if first else tuple(moving))
    return kernel_call(kernel, operands, outs, scalars=1, cost=0.8)


def pack_near(weights):
    layers, rows, size = weights[0].shape

    def kernel(q_ref, k_ref, v_ref, o_ref, out_ref):
        for layer in range(layers):
            out_ref[layer] = jnp.concatenate(
                [q_ref[layer], k_ref[layer], v_ref[layer], turned(o_ref[layer])], axis=1
            )

    return kernel_call(kernel, weights, [out((layers, rows, 4 * size))])[0]


def weave_near(core, own, peer):
    layers, rows, columns = own.shape
    size = columns // 4

    def kernel(core_ref, own_ref, peer_ref, *out_refs):
        first = core_ref[0] == 0
        for layer, out_ref in enumerate(out_refs):
            a, b = own_ref[layer], peer_ref[layer]
            low, high = jnp.where(first, a, b), jnp.where(first, b, a)
            parts = []
            for i in range(4):
                parts += [low[:, i * size : (i + 1) * size], high[:, i * size : (i + 1) * size]]
            out_ref[...] = jnp.concatenate(parts, axis=1)

    return kernel_call(
        kernel, (core, own, peer), [out((rows, 2 * columns))] * layers, scalars=1
    )


def pack_far(up, down):
    layers, rows, size = up.shape

    def kernel(up_ref, down_ref, *out_refs):
        for layer, out_ref in enumerate(out_refs):
            out_ref[:, :size] = up_ref[layer]
            out_ref[:, size:] = turned(down_ref[layer])

    return kernel_call(kernel, (up, down), [out((rows, 2 * size))] * layers)


def weave_far(core, own, peer):
    rows, columns = own[0].shape

    def kernel(core_ref, *refs):
        first = core_ref[0] == 0
        count = len(own)
        for index in range(count):
            a, b = refs[index][...], refs[count + index][...]
            refs[2 * count + index][:, :columns] = jnp.where(first, a, b)
            refs[2 * count + index][:, columns:] = jnp.where(first, b, a)

    return kernel_call(
        kernel, (core, *own, *peer), [out((rows, 2 * columns))] * len(own), scalars=1
    )


def weave_bias(core, own, peer, size):
    layers = own.shape[0]
    rest = own.shape[1] - 2 * size

    def kernel(core_ref, own_ref, peer_ref, q_ref, v_ref, u_ref):
        first = core_ref[0] == 0
        a, b = own_ref[...], peer_ref[...]
        low, high = jnp.where(first, a, b), jnp.where(first, b, a)
        q_ref[...] = jnp.concatenate([low[:, :size], high[:, :size]], axis=1)
        v_ref[...] = jnp.concatenate([low[:, size : 2 * size], high[:, size : 2 * size]], axis=1)
        u_ref[...] = jnp.concatenate([low[:, 2 * size :], high[:, 2 * size :]], axis=1)

    return kernel_call(
        kernel,
        (core, own, peer),
        [
            out((layers, 2 * size), WIDE),
            out((layers, 2 * size), WIDE),
            out((layers, 2 * rest), WIDE),
        ],
        scalars=1,
    )


def mark_documents(core, segments, rows):
    def kernel(core_ref, segment_ref, *refs):
        core = core_ref[0]
        blocks = [core, 2 + core, 1 - core, 3 - core]
        lane = lax.broadcasted_iota(jnp.int32, (128, rows), 0)
        for index, block in enumerate(blocks):
            at = pl.ds(pl.multiple_of(block * rows, 128), rows)
            mark = jnp.where(lane == segment_ref[:, at] + 1, 1.0, 0.0).T
            refs[2 + index][...] = mark.astype(LOW)
            if index < 2:
                real = lax.broadcasted_iota(jnp.int32, (rows, 128), 1) < 9
                refs[index][...] = jnp.where(real & (mark == 0.0), NEVER, 0.0).astype(LOW)

    made = kernel_call(kernel, (core, segments), [out((rows, 128))] * 6, scalars=1)
    return made[:2], made[2:]


def seed_rows(side, own, other, marks):
    rows, depth = own.shape

    def kernel(side_ref, own_ref, other_ref, m0, m1, low0, low1, sums_ref):
        total = None
        for j, (mark, low) in enumerate(((m0, low0), (m1, low1))):
            mine = side_ref[0] == j
            value = jnp.where(mine, own_ref[...], other_ref[...])
            value = jnp.where(mark[:, 0:1] > 0, jnp.zeros_like(value), value)
            low[...] = value
            here = jnp.sum(value.astype(WIDE), axis=0, keepdims=True)
            here = jnp.where(mine, here, 0.0)
            total = here if total is None else total + here
        sums_ref[0:1, :] = total

    return kernel_call(
        kernel,
        (side, own, other, *marks),
        [out((rows, depth)), out((rows, depth)), out((8, depth), WIDE)],
        scalars=1,
    )


def project_first(side, own, other, embed, gain, shift, weights, q_bias, v_bias):
    rows, depth = own.shape
    width = q_bias.shape[1]
    scale = HEAD_DIM ** (-0.5)

    def kernel(side_ref, own_ref, other_ref, embed_ref, gain_ref, shift_ref, w_ref, qb_ref, vb_ref, *refs):
        firsts = []
        for j in range(2):
            rows_in = jnp.where(side_ref[0] == j, own_ref[...], other_ref[...])
            state = rows_in.astype(WIDE) + embed_ref[...].astype(WIDE)
            refs[j][...] = state
            first = (norm_parts(state)[0] * gain_ref[0:1, :] + shift_ref[0:1, :]).astype(LOW)
            refs[2 + j][...] = first
            firsts.append(first)
        first = jnp.concatenate(firsts)
        query = (dot(first, w_ref[:, :width]) + qb_ref[0:1, :]).astype(LOW)
        query = query * jnp.asarray(scale, LOW)
        key = dot(first, w_ref[:, width : 2 * width]).astype(LOW)
        value = (dot(first, w_ref[:, 2 * width : 3 * width]) + vb_ref[0:1, :]).astype(LOW)
        for j in range(2):
            at = slice(j * rows, (j + 1) * rows)
            refs[4 + j][...] = query[at]
            refs[6 + j][:, :width] = key[at]
            refs[6 + j][:, width:] = value[at]

    made = kernel_call(
        kernel,
        (side, own, other, embed, gain, shift, weights, q_bias, v_bias),
        [out((rows, depth), WIDE)] * 2
        + [out((rows, depth))] * 2
        + [out((rows, width))] * 2
        + [out((rows, 2 * width))] * 2,
        scalars=1, cost=1.8)
    return [made[2 * i : 2 * i + 2] for i in range(4)]


def last_branch(side, acts, weights):
    rows, hidden = acts[0].shape
    depth = weights.shape[0]
    size = hidden // 2

    def kernel(side_ref, a0, a1, w_ref, away_ref, here_ref):
        for flip, ref in ((1, away_ref), (0, here_ref)):
            act = jnp.where(side_ref[0] == flip, a0[...], a1[...])
            total = dot_nt(act[:, :size], w_ref[:, size : 2 * size])
            total += dot_nt(act[:, size:], w_ref[:, 3 * size :])
            ref[...] = total.astype(ref.dtype)

    return kernel_call(
        kernel,
        (side, *acts, weights),
        [out((rows, depth)), out((rows, depth), WIDE)],
        scalars=1, cost=1.4)


def last_rows(side, middles, here, crossed, bias, layer):
    rows, depth = here.shape

    def kernel(side_ref, m0, m1, here_ref, crossed_ref, bias_ref, out_ref):
        middle = jnp.where(side_ref[0] == 0, m0[...], m1[...])
        total = here_ref[...] + crossed_ref[...].astype(WIDE)
        out_ref[...] = (middle + total + bias_ref[layer : layer + 1, :]).astype(LOW)

    return kernel_call(
        kernel, (side, *middles, here, crossed, bias), [out((rows, depth))], scalars=1
    )[0]


def project_back(side, dqs, owns, aways, weights, last):
    rows, width = dqs[0].shape
    depth = weights.shape[0]

    def kernel(side_ref, dq0, dq1, own0, own1, away0, away1, w_ref, g_ref, part0, part1, sums_ref):
        pair = (
            own0[...].astype(WIDE)
            + own1[...].astype(WIDE)
            + (away0[...].astype(WIDE) + away1[...].astype(WIDE))
        ).astype(LOW)
        g_ref[:rows, :width] = dq0[...]
        g_ref[rows:, :width] = dq1[...]
        g_ref[:, width:] = pair
        g = g_ref[...]
        total = dot_nt(g, w_ref[:, : 3 * width])
        low, high = total[:rows], total[rows:]
        if last:
            part0[...] = jnp.where(side_ref[0] == 0, high, low).astype(LOW)
            part1[...] = jnp.where(side_ref[0] == 0, low, high)
        else:
            part0[...] = low.astype(LOW)
            part1[...] = high.astype(LOW)
        sums_ref[0:1, :] = jnp.sum(g[:, :width].astype(WIDE), axis=0, keepdims=True)
        sums_ref[1:2, :] = jnp.sum(pair[:, width:].astype(WIDE), axis=0, keepdims=True)

    return kernel_call(
        kernel,
        (side, *dqs, *owns, *aways, weights),
        [
            out((2 * rows, 3 * width)),
            out((rows, depth)),
            out((rows, depth), WIDE if last else LOW),
            out((8, width), WIDE),
        ],
        scalars=1, cost=1.6)


def first_rows(side, here, arrived, states, g_middles, gain):
    rows, depth = here.shape

    def kernel(side_ref, here_ref, arrived_ref, s0, s1, g0, g1, gain_ref, out_ref, sums_ref):
        low = side_ref[0] == 0
        incoming = here_ref[...] + arrived_ref[...].astype(WIDE)
        state = jnp.where(low, s0[...], s1[...])
        gain_grad, shift_grad, through = norm_backward(incoming, state, gain_ref[0:1, :])
        out_ref[...] = jnp.where(low, g0[...], g1[...]) + through
        sums_ref[0:1, :] = gain_grad
        sums_ref[1:2, :] = shift_grad

    return kernel_call(
        kernel,
        (side, here, arrived, *states, *g_middles, gain),
        [out((rows, depth), WIDE), out((8, depth), WIDE)],
        scalars=1,
    )


def vector_rows(place, entries, layers, depth):
    arrays = [array for _, _, group in entries for array in group]

    def kernel(place_ref, *refs):
        out_ref = refs[-1]
        place = place_ref[0]
        side = place // 2
        at = 0
        for row, (take, index), group in entries:
            here = refs[at : at + len(group)]
            at += len(group)
            if take == "own":
                value = jnp.where(side == 0, here[0][index : index + 1, :], here[1][index : index + 1, :])
                out_ref[row : row + 1, :] = value
            elif take == "one":
                out_ref[row : row + 1, :] = here[0][index : index + 1, :]
            elif take == "half":
                value = here[0][index : index + 1, :]
                zero = jnp.zeros_like(value)
                out_ref[row : row + 1, :] = jnp.concatenate(
                    [jnp.where(side == 0, value, zero), jnp.where(side == 0, zero, value)], axis=1
                )
            else:
                value = here[0][0:1, :] + here[1][0:1, :]
                for t in range(4):
                    here_row = value[:, t % 2 * depth : (t % 2 + 1) * depth]
                    out_ref[row + t : row + t + 1, :] = jnp.where(side == t // 2, here_row, 0.0)

    return kernel_call(
        kernel, (place, *arrays), [out((12 * layers, depth), WIDE)], scalars=1
    )[0]


def vector_outputs(place, total, layers, size):
    depth = total.shape[1]

    def kernel(place_ref, total_ref, qb, vb, ob, ub, db, fg, fs, sg, ss):
        place = place_ref[0]

        def pick(values):
            result = values[0]
            for t in range(1, 4):
                result = jnp.where(place == t, values[t], result)
            return result

        for layer in range(layers):
            at = slice(layer, layer + 1)
            row = lambda i: total_ref[12 * layer + i : 12 * layer + i + 1, :]
            for ref, i in ((fg, 0), (fs, 1), (sg, 2), (ss, 3), (ob, 4), (db, 5)):
                ref[at, :] = row(i)
            for ref, i in ((qb, 6), (vb, 7)):
                value = row(i)
                ref[at, :] = pick([value[:, t * size : (t + 1) * size] for t in range(4)])
            ub[at, :] = pick([row(8 + t) for t in range(4)])

    small, large = out((layers, size), WIDE), out((layers, depth), WIDE)
    return kernel_call(
        kernel, (place, total), [small, small] + [large] * 7, scalars=1
    )


def matrix_outputs(results, size):
    layers = len(results)
    rows, columns = results[0].shape
    count = columns // size

    def kernel(*refs):
        for layer in range(layers):
            value = refs[layer][...].astype(WIDE)
            for i in range(count):
                part = value[:, i * size : (i + 1) * size]
                refs[layers + i][layer] = part.T if i == count - 1 else part

    return kernel_call(
        kernel,
        results,
        [out((layers, rows, size), WIDE)] * (count - 1) + [out((layers, size, rows), WIDE)],
    )


def head_lanes(half):
    lane = lax.broadcasted_iota(jnp.int32, (1, 128), 1)
    return (lane >= half * HEAD_DIM) & (lane < (half + 1) * HEAD_DIM)


def only(mask, value):
    return jnp.where(mask, value, jnp.zeros_like(value))


def fold(value, reduce):
    return reduce(value.reshape(value.shape[0] // 8, 8, value.shape[1]), axis=0)


def attend(query, q_marks, pairs, k_marks, weights):
    rows, width = query.shape
    heads = width // HEAD_DIM
    blocks = len(pairs)
    size = pairs[0].shape[0]

    def kernel(q_ref, qm_ref, *refs):
        kv_refs, km_refs = refs[:blocks], refs[blocks : 2 * blocks]
        w_ref, mixed_ref, norm_ref, part_ref, held = refs[2 * blocks :]
        parts = []
        for pair in range(heads // 2):
            at = slice(pair * 128, pair * 128 + 128)
            to = slice(width + pair * 128, width + pair * 128 + 128)
            q = q_ref[:, at]
            values = [turned(kv[:, to]) for kv in kv_refs]
            for half in range(2):
                q_one = jnp.concatenate([only(head_lanes(half), q), qm_ref[...]], axis=1)
                top = None
                for b in range(blocks):
                    key = jnp.concatenate([kv_refs[b][:, at], km_refs[b][...]], axis=1)
                    scores = dot_nt(key, q_one)
                    held[b] = scores
                    here = fold(scores, jnp.max)
                    top = here if top is None else jnp.maximum(top, here)
                top = jnp.max(top, axis=0, keepdims=True)
                total, bulk = None, None
                for b in range(blocks):
                    grown = jnp.exp(held[b] - top)
                    here = fold(grown, jnp.sum)
                    bulk = here if bulk is None else bulk + here
                    value = values[b][half * HEAD_DIM : (half + 1) * HEAD_DIM]
                    part = dot(value, grown.astype(LOW))
                    total = part if total is None else total + part
                bulk = jnp.sum(bulk, axis=0, keepdims=True)
                parts.append(total * (1.0 / bulk))
                row = pair * 2 + half
                norm_ref[row : row + 1, :] = top + jnp.log(bulk)
        mixed = jnp.concatenate(parts).T.astype(LOW)
        mixed_ref[...] = mixed
        part_ref[...] = dot_nt(mixed, w_ref[:, 3 * width :]).astype(LOW)

    return kernel_call(
        kernel,
        (query, q_marks, *pairs, *k_marks, weights),
        [out((rows, width)), out((8, rows), WIDE), out((rows, weights.shape[0]))],
        [pltpu.VMEM((blocks, size, rows), WIDE)], cost=4.0)


def attend_back(layer, grads, part, arrived, middle, gain, weights, query, q_marks, norms, pairs, k_marks):
    rows, width = query.shape
    depth = middle.shape[1]
    heads = width // HEAD_DIM
    blocks = len(pairs)
    size = pairs[0].shape[0]
    scale = HEAD_DIM ** (-0.5)
    near = blocks // 2

    def kernel(grads_ref, part_ref, arrived_ref, middle_ref, gain_ref, weight_ref, q_ref, qm_ref, norm_ref, *refs):
        kv_refs, km_refs = refs[:blocks], refs[blocks : 2 * blocks]
        gm_ref, low_ref, sums_ref, dq_ref, own_ref, away_ref, p_wide, w_wide, p_all, s_all = refs[2 * blocks :]
        incoming = part_ref[...].astype(WIDE) + arrived_ref[...].astype(WIDE)
        gain_grad, shift_grad, through = norm_backward(
            incoming, middle_ref[...], gain_ref[layer : layer + 1, :]
        )
        g_middle = grads_ref[...].astype(WIDE) + through
        low = g_middle.astype(LOW)
        gm_ref[...] = g_middle
        low_ref[...] = low
        sums_ref[0:1, :] = gain_grad
        sums_ref[1:2, :] = shift_grad
        sums_ref[2:3, :] = jnp.sum(g_middle, axis=0, keepdims=True)
        g_mixed = dot(low, weight_ref[:, 3 * width :]).astype(LOW)
        dqs = []
        for pair in range(heads // 2):
            at = slice(pair * 128, pair * 128 + 128)
            to = slice(width + pair * 128, width + pair * 128 + 128)
            q, g = q_ref[:, at], g_mixed[:, at]
            keys = [turned(kv[:, at]) for kv in kv_refs]
            q_stack, g_stack = [], []
            for half in range(2):
                lanes = head_lanes(half)
                q_stack.append(only(lanes, q))
                g_stack.append(only(lanes, g))
                q_one = jnp.concatenate([q_stack[half], qm_ref[...]], axis=1)
                row = pair * 2 + half
                norm = norm_ref[row : row + 1, :]
                total = None
                for b in range(blocks):
                    key = jnp.concatenate([kv_refs[b][:, at], km_refs[b][...]], axis=1)
                    probs = jnp.exp(dot_nt(key, q_one) - norm)
                    weighed = probs * dot_nt(kv_refs[b][:, to], g_stack[half])
                    here = fold(weighed, jnp.sum)
                    total = here if total is None else total + here
                    p_wide[b] = probs
                    w_wide[b] = weighed
                    p_all[b * size : (b + 1) * size, half * rows : (half + 1) * rows] = probs.astype(LOW)
                total = jnp.sum(total, axis=0, keepdims=True)
                dq = None
                for b in range(blocks):
                    g_scores = (w_wide[b] - p_wide[b] * total).astype(LOW)
                    s_all[b * size : (b + 1) * size, half * rows : (half + 1) * rows] = g_scores
                    part = dot(keys[b][half * HEAD_DIM : (half + 1) * HEAD_DIM], g_scores)
                    dq = part if dq is None else dq + part
                dqs.append(dq)
            dk = dot(s_all[...], jnp.concatenate(q_stack)).astype(LOW)
            dv = dot(p_all[...], jnp.concatenate(g_stack)).astype(LOW)
            own_ref[:, at] = dk[: near * size]
            away_ref[:, at] = dk[near * size :]
            own_ref[:, to] = dv[: near * size]
            away_ref[:, to] = dv[near * size :]
        dq_ref[...] = (jnp.concatenate(dqs).T * scale).astype(LOW)

    half_rows = near * size
    length = blocks * size
    return kernel_call(
        kernel,
        (grads, part, arrived, middle, gain, weights, query, q_marks, norms, *pairs, *k_marks),
        [
            out((rows, depth), WIDE),
            out((rows, depth)),
            out((8, depth), WIDE),
            out((rows, width)),
            out((half_rows, 2 * width)),
            out((half_rows, 2 * width)),
        ],
        [
            pltpu.VMEM((blocks, size, rows), WIDE),
            pltpu.VMEM((blocks, size, rows), WIDE),
            pltpu.VMEM((length, 2 * rows), LOW),
            pltpu.VMEM((length, 2 * rows), LOW),
        ], cost=6.4)


def local(
    hidden_in,
    time_embed,
    segment_ids,
    cotangent,
    query_weight,
    key_weight,
    value_weight,
    output_weight,
    up_weight,
    down_weight,
    query_bias,
    value_bias,
    output_bias,
    up_bias,
    down_bias,
    first_gain,
    first_shift,
    second_gain,
    second_shift,
):
    rows, depth = hidden_in.shape
    layers, _, head_width = query_weight.shape
    hidden_width = up_weight.shape[2]
    place = lax.axis_index("tensor")
    core = (place % 2).reshape(1)
    side = (place // 2).reshape(1)
    place = place.reshape(1)
    ring = Ring()
    last = layers - 1

    near_own = pack_near((query_weight, key_weight, value_weight, output_weight))
    near_peer = swap_core(near_own)
    hidden_other = swap_y(hidden_in)
    pieces = weave_near(core, near_own, near_peer)
    near = [Gather(ring, pieces[0])]
    near[0].step()
    if ring.use:
        (_, query_bias, value_bias, up_bias, segment_ids, cotangent, up_weight, down_weight) = tie(
            near[0].current,
            query_bias,
            value_bias,
            up_bias,
            segment_ids,
            cotangent,
            up_weight,
            down_weight,
        )
    far_own = pack_far(up_weight, down_weight)
    far_pieces = weave_far(core, far_own, [swap_core(piece) for piece in far_own])
    near[0].step()
    near[0].step()
    token = near[0].current if ring.use else None
    near[0].finish()
    far = [Gather(ring, far_pieces[0])]
    far[0].step(token)
    biases = jnp.concatenate([query_bias, value_bias, up_bias], axis=1)
    q_bias, v_bias, u_bias = weave_bias(core, biases, swap_core(biases), head_width)
    q_marks, k_marks = mark_documents(core, segment_ids, rows)
    near.append(Gather(ring, pieces[1]))
    far.append(Gather(ring, far_pieces[1]))

    def exchange(parts):
        first = swap_y(parts[0])
        second = swap_y(tie(parts[1], first)[0])
        first, _ = tie(first, parts[1])
        return [first, second]

    kept = []
    for layer in range(layers):
        w_near = near[layer].whole
        if layer == 0:
            states, firsts, queries, pairs = project_first(
                side, hidden_in, hidden_other, time_embed, first_gain, first_shift, w_near, q_bias, v_bias
            )
            seeds = None
        else:
            made = [
                project(
                    layer,
                    middles[j],
                    branches[j],
                    arrived[j],
                    down_bias,
                    first_gain,
                    first_shift,
                    w_near,
                    q_bias,
                    v_bias,
                )
                for j in range(2)
            ]
            states, firsts, queries, pairs = ([m[i] for m in made] for i in range(4))
        pairs = list(pairs) + [swap_core(pair) for pair in pairs]
        mixeds, norms, parts = [], [], []
        for j in range(2):
            mixed, norm, part = attend(queries[j], q_marks[j], pairs, k_marks, w_near)
            mixeds.append(mixed)
            norms.append(norm)
            parts.append(part)
            far[layer].step(part)
        arrived = exchange(parts)
        if layer == 0:
            token = far[0].current if ring.use else None
            near[1].step(token)
        far[layer].finish()
        w_far = far[layer].whole
        if layer == 0:
            cotangent, _ = tie(cotangent, parts[1])
            seed0, seed1, seed_sums = seed_rows(side, cotangent, swap_y(cotangent), k_marks[:2])
            seeds = [seed0, seed1]
        made = []
        for j in range(2):
            made.append(
                feed(
                    layer,
                    states[j],
                    parts[j],
                    arrived[j],
                    output_bias,
                    second_gain,
                    second_shift,
                    w_far,
                    u_bias,
                    seeds[j] if layer == last else None,
                )
            )
            if layer == 0:
                near[1].step(made[j][4])
        middles, seconds, acts, others, branches = ([m[i] for m in made] for i in range(5))
        kept.append((states, firsts, queries, pairs, norms, mixeds, middles, seconds, acts, others))
        if layer < last:
            arrived = [swap_y(branch) for branch in branches]
            arrived[0], branches[1] = tie(arrived[0], branches[1])
            token = near[1].current if ring.use else None
            near[1].finish()
            far[1].step(token)

    entries = [(12 * last + 5, ("one", 0), (seed_sums,))]
    up_sums = [m[5] for m in made]
    grads, lows, g_pres, parts = seeds, seeds, others, branches
    under_way, results = [], {}

    def advance(main):
        for scatter in under_way:
            main = scatter.step(main)
        return main

    for layer in reversed(range(layers)):
        (states, firsts, queries, pairs, norms, mixeds, middles, seconds, acts, slopes) = kept[layer]
        w_near = near[layer].whole
        w_far = far[layer].whole
        base = 12 * layer
        if layer < last:
            made = []
            for j in range(2):
                if j == 1:
                    arrived[1] = advance(arrived[1])
                made.append(feed_back(
                    layer + 1,
                    g_middles[j],
                    parts[j],
                    arrived[j],
                    above[j],
                    first_gain,
                    slopes[j],
                    w_far,
                ))
            grads, lows, g_pres, parts, sums, up_sums = ([m[i] for m in made] for i in range(6))
            entries += [
                (base + 12, ("own", 0), sums),
                (base + 13, ("own", 1), sums),
                (base + 5, ("own", 2), sums),
            ]
        entries.append((base + 8, ("up", 0), up_sums))
        arrived = exchange(parts)
        if layer < last:
            arrived[0] = advance(arrived[0])
        made = []
        for j in range(2):
            if j == 1:
                feed_away = outer_feed(core, seconds, g_pres, lows, acts, 1)
                got = swap_core(feed_away)
                feed_own = outer_feed(core, seconds, g_pres, lows, acts, 0)
                arrived[1], feed_own, got = tie(arrived[1], feed_own, got)
                arrived[1] = advance(arrived[1])
                under_way.append(Scatter(ring, [feed_own], [got]))
                results[layer, "feed"] = under_way[-1]
            made.append(
                attend_back(
                    layer,
                    grads[j],
                    parts[j],
                    arrived[j],
                    middles[j],
                    second_gain,
                    w_near,
                    queries[j],
                    q_marks[j],
                    norms[j],
                    pairs,
                    k_marks,
                )
            )
            if j == 0:
                g_pres, _ = tie(g_pres, made[0][1])
        g_middles, m_lows, sums, dqs, owns, aways = ([m[i] for m in made] for i in range(6))
        entries += [
            (base + 2, ("own", 0), sums),
            (base + 3, ("own", 1), sums),
            (base + 4, ("own", 2), sums),
        ]
        aways = [swap_core(away) for away in aways]
        aways[1] = advance(aways[1])
        g_qkv, part0, part1, sums = project_back(side, dqs, owns, aways, w_near, layer == 0)
        entries += [(base + 6, ("half", 0), (sums,)), (base + 7, ("half", 1), (sums,))]
        if layer > 0:
            parts = [part0, part1]
            arrived = exchange(parts)
            above = states
        else:
            arrived = swap_y(part0)
        near_away = outer_heads(core, firsts, g_qkv, m_lows, mixeds, 1)
        near_got = swap_core(near_away)
        near_own = outer_heads(core, firsts, g_qkv, m_lows, mixeds, 0)
        if layer == last:
            arrived[0], near_own, near_got = tie(arrived[0], near_own, near_got)
            arrived[0] = advance(arrived[0])
        under_way.append(Scatter(ring, [near_own], [near_got]))
        results[layer, "near"] = under_way[-1]
        if layer == last:
            acts_after, _ = tie(acts, near_own)
            away_rows, here_rows = last_branch(side, acts_after, w_far)
            crossed = swap_y(away_rows)
            denoised = last_rows(side, middles, here_rows, crossed, down_bias, layer)
    input_grad, sums = first_rows(side, part1, arrived, states, g_middles, first_gain)
    entries += [(0, ("one", 0), (sums,)), (1, ("one", 1), (sums,))]
    total = vector_rows(place, entries, layers, depth)
    results[0, "near"].step()
    if ring.use:
        for move_by in exchanges(ring.count):
            total = total + move_by(total)
            total = advance(total)
    else:
        total = lax.psum(total, ("fsdp", "tensor"))
    vectors = vector_outputs(place, total, layers, head_width)
    up_out, down_out = matrix_outputs(
        [results[layer, "feed"].finish() for layer in range(layers)], hidden_width
    )
    heads = matrix_outputs([results[layer, "near"].finish() for layer in range(layers)], head_width)
    return (denoised, input_grad, *heads, up_out, down_out, *vectors)


def solution(mesh):
    rows = P(("fsdp", "tensor"), None)
    inner = P(None, "fsdp", "tensor")
    outer = P(None, "tensor", "fsdp")
    cut = P(None, "tensor")
    in_specs = (
        rows,
        P("fsdp", None),
        P("fsdp", None),
        rows,
        inner,
        inner,
        inner,
        outer,
        inner,
        outer,
        cut,
        cut,
        P(),
        cut,
        P(),
        P(),
        P(),
        P(),
        P(),
    )
    out_specs = (
        rows,
        rows,
        inner,
        inner,
        inner,
        outer,
        inner,
        outer,
        cut,
        cut,
        P(),
        cut,
        P(),
        P(),
        P(),
        P(),
        P(),
    )
    return jax.shard_map(local, mesh=mesh, in_specs=in_specs, out_specs=out_specs, check_vma=False)
```

profile of v0, /device:TPU:0, one launch (start us, length us, event | category | flops | bytes accessed | tf_op | source)
XLA Modules:
  0.0 366.2 jit_solution(15071911093999351658)
XLA Ops:
  19.9 3.7 %collective-permute-done.4 = bf16[96,1536]{1,0:T(8,128)(2,1)S(1)} collective-permute-done((bf16[96,1536]{1,0:T(8,128)(2,1)}, bf16[96,1536]{1,0:T(8,128)(2,1)S(1)}, u32[]{:S(2)}, u32[]{:S(2)}) %collective-permute-start.4) | collective-permute-done | bytes 294944 | tf_op jit(solution)/shard_map/ppermute | solution.py:72
  25.4 4.9 %collective-permute-done.6 = bf16[96,1536]{1,0:T(8,128)(2,1)S(1)} collective-permute-done((bf16[96,1536]{1,0:T(8,128)(2,1)S(1)}, bf16[96,1536]{1,0:T(8,128)(2,1)S(1)}, u32[]{:S(2)}, u32[]{:S(2)}) %collective-permute-start.6) | collective-permute-done | bytes 294944 | tf_op jit(solution)/shard_map/ppermute | solution.py:72
  37.0 3.5 shard_map.317
  44.4 3.9 %shard_map.319 = (bf16[256,384]{1,0:T(8,128)(2,1)S(1)}, f32[8,256]{1,0:T(8,128)S(1)}, bf16[256,768]{1,0:T(8,128)(2,1)S(1)}) custom-call(bf16[256,384]{1,0:T(8,128)(2,1)S(1)} %get-tuple-element.276.q_ref, bf16[256,128]{1,0:T(8,128)(2,1)S(1)} %get-tuple-element.278.qm_ref, bf16[256,768]{1,0:T(8,128)(2,1)S(1)} %get-tuple-element.279.refs_0_, ...), custom_call_target="tpu_custom_call" | custom-call | flops 4000000000 | bytes 1024 | tf_op jit(solution)/shard_map/pallas_call | solution.py:191
  51.8 3.9 %shard_map.320 = (bf16[256,384]{1,0:T(8,128)(2,1)S(1)}, f32[8,256]{1,0:T(8,128)S(1)}, bf16[256,768]{1,0:T(8,128)(2,1)S(1)}) custom-call(bf16[256,384]{1,0:T(8,128)(2,1)S(1)} %get-tuple-element.286.q_ref, bf16[256,128]{1,0:T(8,128)(2,1)S(1)} %get-tuple-element.287.qm_ref, bf16[256,768]{1,0:T(8,128)(2,1)S(1)} %get-tuple-element.279.refs_0_, ...), custom_call_target="tpu_custom_call" | custom-call | flops 4000000000 | bytes 1024 | tf_op jit(solution)/shard_map/pallas_call | solution.py:191
  56.9 3.4 collective-permute-done.13.refs_2_
  63.6 8.1 %collective-permute-done.20 = bf16[96,3072]{1,0:T(8,128)(2,1)S(1)} collective-permute-done((bf16[96,3072]{1,0:T(8,128)(2,1)S(1)}, bf16[96,3072]{1,0:T(8,128)(2,1)S(1)}, u32[]{:S(2)}, u32[]{:S(2)}) %collective-permute-start.20) | collective-permute-done | bytes 589856 | tf_op jit(solution)/shard_map/ppermute | solution.py:72
  75.1 3.4 collective-permute-done.22
  78.5 3.2 collective-permute-done.26
  112.5 2.9 shard_map.326
  117.9 5.5 %shard_map.327 = (bf16[256,384]{1,0:T(8,128)(2,1)S(1)}, f32[8,256]{1,0:T(8,128)S(1)}, bf16[256,768]{1,0:T(8,128)(2,1)S(1)}) custom-call(bf16[256,384]{1,0:T(8,128)(2,1)S(1)} %get-tuple-element.310.q_ref, bf16[256,128]{1,0:T(8,128)(2,1)S(1)} %get-tuple-element.278.qm_ref, bf16[256,768]{1,0:T(8,128)(2,1)S(1)} %get-tuple-element.311.refs_0_, ...), custom_call_target="tpu_custom_call" | custom-call | flops 4000000000 | bytes 1024 | tf_op jit(solution)/shard_map/pallas_call | solution.py:191
  126.7 5.5 %shard_map.328 = (bf16[256,384]{1,0:T(8,128)(2,1)S(1)}, f32[8,256]{1,0:T(8,128)S(1)}, bf16[256,768]{1,0:T(8,128)(2,1)S(1)}) custom-call(bf16[256,384]{1,0:T(8,128)(2,1)S(1)} %get-tuple-element.316.q_ref, bf16[256,128]{1,0:T(8,128)(2,1)S(1)} %get-tuple-element.287.qm_ref, bf16[256,768]{1,0:T(8,128)(2,1)S(1)} %get-tuple-element.311.refs_0_, ...), custom_call_target="tpu_custom_call" | custom-call | flops 4000000000 | bytes 1024 | tf_op jit(solution)/shard_map/pallas_call | solution.py:191
  138.1 8.1 %collective-permute-done.42 = bf16[96,3072]{1,0:T(8,128)(2,1)S(1)} collective-permute-done((bf16[96,3072]{1,0:T(8,128)(2,1)S(1)}, bf16[96,3072]{1,0:T(8,128)(2,1)S(1)}, u32[]{:S(2)}, u32[]{:S(2)}) %collective-permute-start.42) | collective-permute-done | bytes 589856 | tf_op jit(solution)/shard_map/ppermute | solution.py:72
  148.2 5.0 %collective-permute-done.44 = bf16[48,3072]{1,0:T(8,128)(2,1)S(1)} collective-permute-done((bf16[48,3072]{1,0:T(8,128)(2,1)S(1)}, bf16[48,3072]{1,0:T(8,128)(2,1)S(1)}, u32[]{:S(2)}, u32[]{:S(2)}) %collective-permute-start.44) | collective-permute-done | bytes 294944 | tf_op jit(solution)/shard_map/ppermute | solution.py:72
  154.8 3.7 %shard_map.330 = (f32[256,768]{1,0:T(8,128)S(1)}, bf16[256,768]{1,0:T(8,128)(2,1)S(1)}, bf16[256,1536]{1,0:T(8,128)(2,1)S(1)}, bf16[256,1536]{1,0:T(8,128)(2,1)S...) custom-call(f32[256,768]{1,0:T(8,128)S(1)} %get-tuple-element.309.refs_0_.state_ref, ...), custom_call_target="tpu_custom_call" | custom-call | flops 4000000000 | bytes 1024 | tf_op jit(solution)/shard_map/pallas_call | solution.py:191
  159.1 3.7 %shard_map.331 = (f32[256,768]{1,0:T(8,128)S(1)}, bf16[256,768]{1,0:T(8,128)(2,1)S(1)}, bf16[256,1536]{1,0:T(8,128)(2,1)S(1)}, bf16[256,1536]{1,0:T(8,128)(2,1)S...) custom-call(f32[256,768]{1,0:T(8,128)S(1)} %get-tuple-element.327.refs_0_.state_ref, ...), custom_call_target="tpu_custom_call" | custom-call | flops 4000000000 | bytes 1024 | tf_op jit(solution)/shard_map/pallas_call | solution.py:191
  162.9 6.9 %collective-permute-done.48.arrived_ref = bf16[256,768]{1,0:T(8,128)(2,1)S(1)} collective-permute-done((bf16[256,768]{1,0:T(8,128)(2,1)S(1)}, bf16[256,768]{1,0:T(8,128)(2,1)S(1)}, u32[]{:S(2)}, u32[]{:S(2)}) %collective-permute-start.48) | collective-permute-done | bytes 393248 | tf_op jit(solution)/shard_map/ppermute | solution.py:26
  169.8 9.0 %shard_map.332 = (f32[256,768]{1,0:T(8,128)S(1)}, bf16[256,768]{1,0:T(8,128)(2,1)S(1)}, f32[8,768]{1,0:T(8,128)S(1)}, bf16[256,384]{1,0:T(8,128)(2,1)S(1)}, bf16...) custom-call(bf16[256,768]{1,0:T(8,128)(2,1)S(1)} %get-tuple-element.325.refs_8_.grads_ref.l0, ...), custom_call_target="tpu_custom_call" | custom-call | flops 6400000000 | bytes 1024 | tf_op jit(solution)/shard_map/pallas_call | solution.py:191
  186.3 7.6 %collective-permute-done.49.arrived_ref = bf16[256,768]{1,0:T(8,128)(2,1)S(1)} collective-permute-done((bf16[256,768]{1,0:T(8,128)(2,1)S(1)}, bf16[256,768]{1,0:T(8,128)(2,1)S(1)}, u32[]{:S(2)}, u32[]{:S(2)}) %collective-permute-start.49) | collective-permute-done | bytes 393248 | tf_op jit(solution)/shard_map/ppermute | solution.py:26
  193.9 8.8 %shard_map.335 = (f32[256,768]{1,0:T(8,128)S(1)}, bf16[256,768]{1,0:T(8,128)(2,1)S(1)}, f32[8,768]{1,0:T(8,128)S(1)}, bf16[256,384]{1,0:T(8,128)(2,1)S(1)}, bf16...) custom-call(bf16[256,768]{1,0:T(8,128)(2,1)S(1)} %get-tuple-element.329.refs_8_.l1.grads_ref, ...), custom_call_target="tpu_custom_call" | custom-call | flops 6400000000 | bytes 1024 | tf_op jit(solution)/shard_map/pallas_call | solution.py:191
  212.0 3.3 collective-permute-done.53.refs_2_
  217.1 3.8 %shard_map.337 = (bf16[512,1152]{1,0:T(8,128)(2,1)S(1)}, bf16[256,768]{1,0:T(8,128)(2,1)S(1)}, bf16[256,768]{1,0:T(8,128)(2,1)S(1)}, f32[8,384]{1,0:T(8,128)S(1)}) custom-call(s32[1]{0:T(128)} %bitcast.side_ref, bf16[256,384]{1,0:T(8,128)(2,1)S(1)} %copy-done.44, bf16[256,384]{1,0:T(8,128)(2,1)S(1)} %copy-done.46, bf16[512,768]{1,0:T(8,128)(2,1)S(1)} %copy-done.40, ...), custom_call_target="tpu_custom_call" | custom-call | flops 1600000000 | bytes 1024 | tf_op jit(solution)/shard_map/pallas_call | solution.py:191
  227.7 6.5 %collective-permute-done.55.arrived_ref = bf16[256,768]{1,0:T(8,128)(2,1)S(1)} collective-permute-done((bf16[256,768]{1,0:T(8,128)(2,1)S(1)}, bf16[256,768]{1,0:T(8,128)(2,1)S(1)}, u32[]{:S(2)}, u32[]{:S(2)}) %collective-permute-start.55) | collective-permute-done | bytes 393248 | tf_op jit(solution)/shard_map/ppermute | solution.py:26
  256.0 3.1 collective-permute-done.66.refs_2_
  260.7 6.2 %shard_map.349 = (f32[256,768]{1,0:T(8,128)S(1)}, bf16[256,768]{1,0:T(8,128)(2,1)S(1)}, f32[8,768]{1,0:T(8,128)S(1)}, bf16[256,384]{1,0:T(8,128)(2,1)S(1)}, bf16...) custom-call(f32[256,768]{1,0:T(8,128)S(1)} %get-tuple-element.380.grads_ref, ...), custom_call_target="tpu_custom_call" | custom-call | flops 6400000000 | bytes 1024 | tf_op jit(solution)/shard_map/pallas_call | solution.py:191
  275.3 5.2 %collective-permute-done.70.arrived_ref = bf16[256,768]{1,0:T(8,128)(2,1)S(1)} collective-permute-done((bf16[256,768]{1,0:T(8,128)(2,1)S(1)}, bf16[256,768]{1,0:T(8,128)(2,1)S(1)}, u32[]{:S(2)}, u32[]{:S(2)}) %collective-permute-start.70) | collective-permute-done | bytes 393248 | tf_op jit(solution)/shard_map/ppermute | solution.py:26
  280.5 6.2 %shard_map.353 = (f32[256,768]{1,0:T(8,128)S(1)}, bf16[256,768]{1,0:T(8,128)(2,1)S(1)}, f32[8,768]{1,0:T(8,128)S(1)}, bf16[256,384]{1,0:T(8,128)(2,1)S(1)}, bf16...) custom-call(f32[256,768]{1,0:T(8,128)S(1)} %get-tuple-element.408.grads_ref, ...), custom_call_target="tpu_custom_call" | custom-call | flops 6400000000 | bytes 1024 | tf_op jit(solution)/shard_map/pallas_call | solution.py:191
  297.0 3.1 collective-permute-done.79.refs_3_
  309.9 5.5 %collective-permute-done.80.arrived_ref = bf16[256,768]{1,0:T(8,128)(2,1)S(1)} collective-permute-done((bf16[256,768]{1,0:T(8,128)(2,1)S(1)}, bf16[256,768]{1,0:T(8,128)(2,1)S(1)}, u32[]{:S(2)}, u32[]{:S(2)}) %collective-permute-start.80) | collective-permute-done | bytes 393248 | tf_op jit(solution)/shard_map/ppermute | solution.py:26
  328.1 6.3 %collective-permute-done.87.refs_2_ = bf16[96,768]{1,0:T(8,128)(2,1)S(1)} collective-permute-done((bf16[96,768]{1,0:T(8,128)(2,1)S(1)}, bf16[96,768]{1,0:T(8,128)(2,1)S(1)}, u32[]{:S(2)}, u32[]{:S(2)}) %collective-permute-start.87) | collective-permute-done | bytes 147488 | tf_op jit(solution)/shard_map/ppermute | solution.py:75
  351.2 3.2 collective-permute-done.94
  362.0 3.1 collective-permute-done.100
  (530 shorter events, 202.6 us)
Async XLA Ops:
  4.9 32.0 %collective-permute-start = (bf16[256,768]{1,0:T(8,128)(2,1)}, bf16[256,768]{1,0:T(8,128)(2,1)}, u32[]{:S(2)}, u32[]{:S(2)}) collective-permute-start(bf16[256,768]{1,0:T(8,128)(2,1)} %own_ref.1), channel_id=1, source_target_pairs={{0,2},{2,0},{1,3},{3,1},{4,6},{6,4},{5,7},{7,5},{8,10},{10,8},{9,1... | collective-permute-start | bytes 1179656 | tf_op jit(solution)/shard_map/ppermute | solution.py:26
  32.0 11.5 %collective-permute-start.16 = (bf16[96,3072]{1,0:T(8,128)(2,1)S(1)}, bf16[96,3072]{1,0:T(8,128)(2,1)S(1)}, u32[]{:S(2)}, u32[]{:S(2)}) collective-permute-start(bf16[96,3072]{1,0:T(8,128)(2,1)S(1)} %get-tuple-element.295), channel_id=1, source_target_pairs={{0,8},{8,16},{16,24},{24,28},{28,20},{20,12},{12,4},{4,0},{1,5},{9... | collective-permute-start | bytes 1769480 | tf_op jit(solution)/shard_map/ppermute | solution.py:72
  43.5 20.0 %collective-permute-start.17 = (bf16[96,3072]{1,0:T(8,128)(2,1)S(1)}, bf16[96,3072]{1,0:T(8,128)(2,1)S(1)}, u32[]{:S(2)}, u32[]{:S(2)}) collective-permute-start(bf16[96,3072]{1,0:T(8,128)(2,1)S(1)} %collective-permute-done.16), channel_id=1, source_target_pairs={{0,1},{1,0},{2,3},{3,2},{4,5},{5,4},{6,7},{7,6},{8,9},{9,8},{10,11... | collective-permute-start | bytes 1769480 | tf_op jit(solution)/shard_map/ppermute | solution.py:22
  48.3 12.0 %collective-permute-start.13 = (bf16[256,768]{1,0:T(8,128)(2,1)S(1)}, bf16[256,768]{1,0:T(8,128)(2,1)S(1)}, u32[]{:S(2)}, u32[]{:S(2)}) collective-permute-start(bf16[256,768]{1,0:T(8,128)(2,1)S(1)} %get-tuple-element.285.refs_1_), channel_id=1, source_target_pairs={{0,2},{2,0},{1,3},{3,1},{4,6},{6,4},{5,7},{7,5},{8,10},{10,8},{9,1... | collective-permute-start | bytes 1179656 | tf_op jit(solution)/shard_map/ppermute | solution.py:26
  49.9 12.0 %collective-permute-start.18 = (bf16[96,3072]{1,0:T(8,128)(2,1)S(1)}, bf16[96,3072]{1,0:T(8,128)(2,1)S(1)}, u32[]{:S(2)}, u32[]{:S(2)}) collective-permute-start(bf16[96,3072]{1,0:T(8,128)(2,1)S(1)} %collective-permute-done.16), channel_id=1, source_target_pairs={{0,8},{8,16},{16,24},{24,28},{28,20},{20,12},{12,4},{4,0},{1,5},{9... | collective-permute-start | bytes 1769480 | tf_op jit(solution)/shard_map/ppermute | solution.py:72
  56.4 60.7 %collective-permute-start.46 = (bf16[256,768]{1,0:T(8,128)(2,1)S(1)}, bf16[256,768]{1,0:T(8,128)(2,1)S(1)}, u32[]{:S(2)}, u32[]{:S(2)}) collective-permute-start(bf16[256,768]{1,0:T(8,128)(2,1)S(1)} %copy-done.16), channel_id=1, source_target_pairs={{0,2},{2,0},{1,3},{3,1},{4,6},{6,4},{5,7},{7,5},{8,10},{10,8},{9,1... | collective-permute-start | bytes 1179656 | tf_op jit(solution)/shard_map/ppermute | solution.py:26
  60.3 29.0 %collective-permute-start.25 = (bf16[256,768]{1,0:T(8,128)(2,1)S(1)}, bf16[256,768]{1,0:T(8,128)(2,1)S(1)}, u32[]{:S(2)}, u32[]{:S(2)}) collective-permute-start(bf16[256,768]{1,0:T(8,128)(2,1)S(1)} %get-tuple-element.302.refs_1_), channel_id=1, source_target_pairs={{0,2},{2,0},{1,3},{3,1},{4,6},{6,4},{5,7},{7,5},{8,10},{10,8},{9,1... | collective-permute-start | bytes 1179656 | tf_op jit(solution)/shard_map/ppermute | solution.py:26
  63.5 11.5 %collective-permute-start.19 = (bf16[96,3072]{1,0:T(8,128)(2,1)S(1)}, bf16[96,3072]{1,0:T(8,128)(2,1)S(1)}, u32[]{:S(2)}, u32[]{:S(2)}) collective-permute-start(bf16[96,3072]{1,0:T(8,128)(2,1)S(1)} %collective-permute-done.18), channel_id=1, source_target_pairs={{0,1},{1,0},{2,3},{3,2},{4,5},{5,4},{6,7},{7,6},{8,9},{9,8},{10,11... | collective-permute-start | bytes 1769480 | tf_op jit(solution)/shard_map/ppermute | solution.py:22
  81.7 14.3 %collective-permute-start.27 = (bf16[96,1536]{1,0:T(8,128)(2,1)S(1)}, bf16[96,1536]{1,0:T(8,128)(2,1)S(1)}, u32[]{:S(2)}, u32[]{:S(2)}) collective-permute-start(bf16[96,1536]{1,0:T(8,128)(2,1)S(1)} %collective-permute-done.26), channel_id=1, source_target_pairs={{0,1},{1,0},{2,3},{3,2},{4,5},{5,4},{6,7},{7,6},{8,9},{9,8},{10,11... | collective-permute-start | bytes 884744 | tf_op jit(solution)/shard_map/ppermute | solution.py:22
  87.2 11.9 %collective-permute-start.24 = (bf16[256,768]{1,0:T(8,128)(2,1)S(1)}, bf16[256,768]{1,0:T(8,128)(2,1)S(1)}, u32[]{:S(2)}, u32[]{:S(2)}) collective-permute-start(bf16[256,768]{1,0:T(8,128)(2,1)S(1)} %get-tuple-element.300.part_ref), channel_id=1, source_target_pairs={{0,2},{2,0},{1,3},{3,1},{4,6},{6,4},{5,7},{7,5},{8,10},{10,8},{9,1... | collective-permute-start | bytes 1179656 | tf_op jit(solution)/shard_map/ppermute | solution.py:26
  92.2 20.3 %collective-permute-start.34 = (bf16[256,768]{1,0:T(8,128)(2,1)S(1)}, bf16[256,768]{1,0:T(8,128)(2,1)S(1)}, u32[]{:S(2)}, u32[]{:S(2)}) collective-permute-start(bf16[256,768]{1,0:T(8,128)(2,1)S(1)} %get-tuple-element.313.part_ref), channel_id=1, source_target_pairs={{0,2},{2,0},{1,3},{3,1},{4,6},{6,4},{5,7},{7,5},{8,10},{10,8},{9,1... | collective-permute-start | bytes 1179656 | tf_op jit(solution)/shard_map/ppermute | solution.py:26
  102.8 14.6 %collective-permute-start.38 = (bf16[96,3072]{1,0:T(8,128)(2,1)S(1)}, bf16[96,3072]{1,0:T(8,128)(2,1)S(1)}, u32[]{:S(2)}, u32[]{:S(2)}) collective-permute-start(bf16[96,3072]{1,0:T(8,128)(2,1)S(1)} %get-tuple-element.320), channel_id=1, source_target_pairs={{0,8},{8,16},{16,24},{24,28},{28,20},{20,12},{12,4},{4,0},{1,5},{9... | collective-permute-start | bytes 1769480 | tf_op jit(solution)/shard_map/ppermute | solution.py:72
  117.4 20.5 %collective-permute-start.39 = (bf16[96,3072]{1,0:T(8,128)(2,1)S(1)}, bf16[96,3072]{1,0:T(8,128)(2,1)S(1)}, u32[]{:S(2)}, u32[]{:S(2)}) collective-permute-start(bf16[96,3072]{1,0:T(8,128)(2,1)S(1)} %collective-permute-done.38), channel_id=1, source_target_pairs={{0,1},{1,0},{2,3},{3,2},{4,5},{5,4},{6,7},{7,6},{8,9},{9,8},{10,11... | collective-permute-start | bytes 1769480 | tf_op jit(solution)/shard_map/ppermute | solution.py:22
  123.5 11.3 %collective-permute-start.37 = (bf16[256,768]{1,0:T(8,128)(2,1)S(1)}, bf16[256,768]{1,0:T(8,128)(2,1)S(1)}, u32[]{:S(2)}, u32[]{:S(2)}) collective-permute-start(bf16[256,768]{1,0:T(8,128)(2,1)S(1)} %get-tuple-element.315.refs_1_), channel_id=1, source_target_pairs={{0,2},{2,0},{1,3},{3,1},{4,6},{6,4},{5,7},{7,5},{8,10},{10,8},{9,1... | collective-permute-start | bytes 1179656 | tf_op jit(solution)/shard_map/ppermute | solution.py:26
  125.0 11.3 %collective-permute-start.40 = (bf16[96,3072]{1,0:T(8,128)(2,1)S(1)}, bf16[96,3072]{1,0:T(8,128)(2,1)S(1)}, u32[]{:S(2)}, u32[]{:S(2)}) collective-permute-start(bf16[96,3072]{1,0:T(8,128)(2,1)S(1)} %collective-permute-done.38), channel_id=1, source_target_pairs={{0,8},{8,16},{16,24},{24,28},{28,20},{20,12},{12,4},{4,0},{1,5},{9... | collective-permute-start | bytes 1769480 | tf_op jit(solution)/shard_map/ppermute | solution.py:72
  134.8 24.3 %collective-permute-start.47 = (bf16[256,768]{1,0:T(8,128)(2,1)S(1)}, bf16[256,768]{1,0:T(8,128)(2,1)S(1)}, u32[]{:S(2)}, u32[]{:S(2)}) collective-permute-start(bf16[256,768]{1,0:T(8,128)(2,1)S(1)} %get-tuple-element.328.refs_1_), channel_id=1, source_target_pairs={{0,2},{2,0},{1,3},{3,1},{4,6},{6,4},{5,7},{7,5},{8,10},{10,8},{9,1... | collective-permute-start | bytes 1179656 | tf_op jit(solution)/shard_map/ppermute | solution.py:26
  182.3 11.6 %collective-permute-start.50 = (bf16[768,1536]{1,0:T(8,128)(2,1)S(1)}, bf16[768,1536]{1,0:T(8,128)(2,1)S(1)}, u32[]{:S(2)}, u32[]{:S(2)}) collective-permute-start(bf16[768,1536]{1,0:T(8,128)(2,1)S(1)} %shard_map.334), channel_id=1, source_target_pairs={{0,1},{1,0},{2,3},{3,2},{4,5},{5,4},{6,7},{7,6},{8,9},{9,8},{10,11... | collective-permute-start | bytes 7077896 | tf_op jit(solution)/shard_map/ppermute | solution.py:22
  182.4 11.5 %collective-permute-start.49 = (bf16[256,768]{1,0:T(8,128)(2,1)S(1)}, bf16[256,768]{1,0:T(8,128)(2,1)S(1)}, u32[]{:S(2)}, u32[]{:S(2)}) collective-permute-start(bf16[256,768]{1,0:T(8,128)(2,1)S(1)} %get-tuple-element.338.part_ref), channel_id=1, source_target_pairs={{0,2},{2,0},{1,3},{3,1},{4,6},{6,4},{5,7},{7,5},{8,10},{10,8},{9,1... | collective-permute-start | bytes 1179656 | tf_op jit(solution)/shard_map/ppermute | solution.py:26
  222.7 12.1 %collective-permute-start.56 = (bf16[768,768]{1,0:T(8,128)(2,1)S(1)}, bf16[768,768]{1,0:T(8,128)(2,1)S(1)}, u32[]{:S(2)}, u32[]{:S(2)}) collective-permute-start(bf16[768,768]{1,0:T(8,128)(2,1)S(1)} %shard_map.339), channel_id=1, source_target_pairs={{0,1},{1,0},{2,3},{3,2},{4,5},{5,4},{6,7},{7,6},{8,9},{9,8},{10,11... | collective-permute-start | bytes 3538952 | tf_op jit(solution)/shard_map/ppermute | solution.py:22
  222.7 11.5 %collective-permute-start.55 = (bf16[256,768]{1,0:T(8,128)(2,1)S(1)}, bf16[256,768]{1,0:T(8,128)(2,1)S(1)}, u32[]{:S(2)}, u32[]{:S(2)}) collective-permute-start(bf16[256,768]{1,0:T(8,128)(2,1)S(1)} %get-tuple-element.358.part_ref), channel_id=1, source_target_pairs={{0,2},{2,0},{1,3},{3,1},{4,6},{6,4},{5,7},{7,5},{8,10},{10,8},{9,1... | collective-permute-start | bytes 1179656 | tf_op jit(solution)/shard_map/ppermute | solution.py:26
  235.4 12.2 %collective-permute-start.64 = (bf16[48,768]{1,0:T(8,128)(2,1)S(1)}, bf16[48,768]{1,0:T(8,128)(2,1)S(1)}, u32[]{:S(2)}, u32[]{:S(2)}) collective-permute-start(bf16[48,768]{1,0:T(8,128)(2,1)S(1)} %get-tuple-element.390), channel_id=1, source_target_pairs={{0,8},{8,16},{16,24},{24,28},{28,20},{20,12},{12,4},{4,0},{1,9},{9... | collective-permute-start | bytes 221192 | tf_op jit(solution)/shard_map/ppermute | solution.py:75
  248.2 12.3 %collective-permute-start.68 = (bf16[96,768]{1,0:T(8,128)(2,1)S(1)}, bf16[96,768]{1,0:T(8,128)(2,1)S(1)}, u32[]{:S(2)}, u32[]{:S(2)}) collective-permute-start(bf16[96,768]{1,0:T(8,128)(2,1)S(1)} %get-tuple-element.403), channel_id=1, source_target_pairs={{0,8},{8,16},{16,24},{24,28},{28,20},{20,12},{12,4},{4,0},{1,9},{9... | collective-permute-start | bytes 442376 | tf_op jit(solution)/shard_map/ppermute | solution.py:75
  268.8 11.6 %collective-permute-start.71 = (bf16[768,1536]{1,0:T(8,128)(2,1)S(1)}, bf16[768,1536]{1,0:T(8,128)(2,1)S(1)}, u32[]{:S(2)}, u32[]{:S(2)}) collective-permute-start(bf16[768,1536]{1,0:T(8,128)(2,1)S(1)} %shard_map.351), channel_id=1, source_target_pairs={{0,1},{1,0},{2,3},{3,2},{4,5},{5,4},{6,7},{7,6},{8,9},{9,8},{10,11... | collective-permute-start | bytes 7077896 | tf_op jit(solution)/shard_map/ppermute | solution.py:22
  268.9 11.5 %collective-permute-start.70 = (bf16[256,768]{1,0:T(8,128)(2,1)S(1)}, bf16[256,768]{1,0:T(8,128)(2,1)S(1)}, u32[]{:S(2)}, u32[]{:S(2)}) collective-permute-start(bf16[256,768]{1,0:T(8,128)(2,1)S(1)} %get-tuple-element.409.part_ref), channel_id=1, source_target_pairs={{0,2},{2,0},{1,3},{3,1},{4,6},{6,4},{5,7},{7,5},{8,10},{10,8},{9,1... | collective-permute-start | bytes 1179656 | tf_op jit(solution)/shard_map/ppermute | solution.py:26
  286.8 13.3 %collective-permute-start.74 = (bf16[512,768]{1,0:T(8,128)(2,1)S(1)}, bf16[512,768]{1,0:T(8,128)(2,1)S(1)}, u32[]{:S(2)}, u32[]{:S(2)}) collective-permute-start(bf16[512,768]{1,0:T(8,128)(2,1)S(1)} %get-tuple-element.431), channel_id=1, source_target_pairs={{0,1},{1,0},{2,3},{3,2},{4,5},{5,4},{6,7},{7,6},{8,9},{9,8},{10,11... | collective-permute-start | bytes 2359304 | tf_op jit(solution)/shard_map/ppermute | solution.py:22
  303.3 15.5 %collective-permute-start.81 = (bf16[768,768]{1,0:T(8,128)(2,1)S(1)}, bf16[768,768]{1,0:T(8,128)(2,1)S(1)}, u32[]{:S(2)}, u32[]{:S(2)}) collective-permute-start(bf16[768,768]{1,0:T(8,128)(2,1)S(1)} %shard_map.359), channel_id=1, source_target_pairs={{0,1},{1,0},{2,3},{3,2},{4,5},{5,4},{6,7},{7,6},{8,9},{9,8},{10,11... | collective-permute-start | bytes 3538952 | tf_op jit(solution)/shard_map/ppermute | solution.py:22
  303.4 12.0 %collective-permute-start.80 = (bf16[256,768]{1,0:T(8,128)(2,1)S(1)}, bf16[256,768]{1,0:T(8,128)(2,1)S(1)}, u32[]{:S(2)}, u32[]{:S(2)}) collective-permute-start(bf16[256,768]{1,0:T(8,128)(2,1)S(1)} %get-tuple-element.444), channel_id=1, source_target_pairs={{0,2},{2,0},{1,3},{3,1},{4,6},{6,4},{5,7},{7,5},{8,10},{10,8},{9,1... | collective-permute-start | bytes 1179656 | tf_op jit(solution)/shard_map/ppermute | solution.py:26
  306.5 36.8 %collective-permute-start.57 = (bf16[256,768]{1,0:T(8,128)(2,1)S(1)}, bf16[256,768]{1,0:T(8,128)(2,1)S(1)}, u32[]{:S(2)}, u32[]{:S(2)}) collective-permute-start(bf16[256,768]{1,0:T(8,128)(2,1)S(1)} %get-tuple-element.371), channel_id=1, source_target_pairs={{0,2},{2,0},{1,3},{3,1},{4,6},{6,4},{5,7},{7,5},{8,10},{10,8},{9,1... | collective-permute-start | bytes 1179656 | tf_op jit(solution)/shard_map/ppermute | solution.py:26
  322.3 18.2 %collective-permute-start.90 = (bf16[96,1536]{1,0:T(8,128)(2,1)S(1)}, bf16[96,1536]{1,0:T(8,128)(2,1)S(1)}, u32[]{:S(2)}, u32[]{:S(2)}) collective-permute-start(bf16[96,1536]{1,0:T(8,128)(2,1)S(1)} %get-tuple-element.480), channel_id=1, source_target_pairs={{0,8},{8,16},{16,24},{24,28},{28,20},{20,12},{12,4},{4,0},{1,9},{9... | collective-permute-start | bytes 884744 | tf_op jit(solution)/shard_map/ppermute | solution.py:75
  323.8 16.6 %collective-permute-start.91 = (bf16[96,1536]{1,0:T(8,128)(2,1)S(1)}, bf16[96,1536]{1,0:T(8,128)(2,1)S(1)}, u32[]{:S(2)}, u32[]{:S(2)}) collective-permute-start(bf16[96,1536]{1,0:T(8,128)(2,1)S(1)} %get-tuple-element.481), channel_id=1, source_target_pairs={{0,4},{8,0},{16,8},{24,16},{28,24},{20,28},{12,20},{4,12},{1,5},{9... | collective-permute-start | bytes 884744 | tf_op jit(solution)/shard_map/ppermute | solution.py:75
  341.2 13.2 %collective-permute-start.95 = (bf16[96,1536]{1,0:T(8,128)(2,1)S(1)}, bf16[96,1536]{1,0:T(8,128)(2,1)S(1)}, u32[]{:S(2)}, u32[]{:S(2)}) collective-permute-start(bf16[96,1536]{1,0:T(8,128)(2,1)S(1)} %get-tuple-element.490), channel_id=1, source_target_pairs={{0,8},{8,16},{16,24},{24,28},{28,20},{20,12},{12,4},{4,0},{1,9},{9... | collective-permute-start | bytes 884744 | tf_op jit(solution)/shard_map/ppermute | solution.py:75
  342.8 11.7 %collective-permute-start.96 = (bf16[96,1536]{1,0:T(8,128)(2,1)S(1)}, bf16[96,1536]{1,0:T(8,128)(2,1)S(1)}, u32[]{:S(2)}, u32[]{:S(2)}) collective-permute-start(bf16[96,1536]{1,0:T(8,128)(2,1)S(1)} %get-tuple-element.491), channel_id=1, source_target_pairs={{0,4},{8,0},{16,8},{24,16},{28,24},{20,28},{12,20},{4,12},{1,5},{9... | collective-permute-start | bytes 884744 | tf_op jit(solution)/shard_map/ppermute | solution.py:75
  (191 other events, 2115.8 us)
where the time goes:
time: 373 us; the launch traced here: 366 us
  waiting for transfers between devices  127 us (34%)
  Pallas kernels  117 us (31%)
  starting transfers between devices  86.1 us (23%)
  local copies, waits for them, and re-layouts  33.1 us (9%)
    pallas_call x61, Pallas kernels, kernel_call(): pl.pallas_call(kernel, in_specs=[word] * scalars + [inside] * (len(operan...  117 us
    ppermute x16, waiting for transfers between devices, split_send(): return lax.ppermute(value, ('fsdp', 'tensor'), self.split)  44 us
    ppermute x17, waiting for transfers between devices, swap_y(): return lax.ppermute(value, 'tensor', SWAP_Y)  43.1 us
    ppermute x16, starting transfers between devices, split_send(): return lax.ppermute(value, ('fsdp', 'tensor'), self.split)  26.3 us
    ppermute x16, starting transfers between devices, send_both(): lax.ppermute(ahead, 'fsdp', self.pairs[0])  21.9 us
    unnamed x245, local copies, waits for them, and re-layouts  20.4 us
    ppermute x17, starting transfers between devices, swap_y(): return lax.ppermute(value, 'tensor', SWAP_Y)  19.3 us
    ppermute x16, waiting for transfers between devices, send_both(): lax.ppermute(ahead, 'fsdp', self.pairs[0])  17.7 us
  transfers between devices with their start and end apart: 101, of which 43 were waited for; matrix products, arithmetic and copies ran while one was open for 4% of the time, Pallas kernels for 20%

commit v1 on v0

--- a/solution.py
+++ b/solution.py
@@ -85,10 +85,10 @@
         self.rows, self.columns = piece.shape
         self.todo = []
         self.done = 0
+        self.current = piece
         if ring.use:
             self.whole = jnp.zeros((ring.count * self.rows, self.columns), piece.dtype)
             self.put(piece, lax.axis_index("fsdp"))
-            self.current = piece
         else:
             self.whole = lax.all_gather(piece, "fsdp", axis=0, tiled=True)
 
@@ -136,6 +136,7 @@
         self.ring = ring
         self.owns, self.gots = owns, gots
         self.done = 0
+        self.made = owns
         if ring.use:
             self.rows = owns[0].shape[0] // ring.count
         else:
@@ -144,25 +145,33 @@
             )
             self.result = lax.psum_scatter(total, "fsdp", scatter_dimension=0, tiled=True)
 
-    def step(self, main=None):
+    def step(self, main=None, token=None):
         ring = self.ring
-        if not ring.use or self.done == ring.far:
+        if not ring.use or self.done > ring.far:
             return main
-        moving = self.moving if self.done else None
-        ahead, behind = ring.send_both(
-            *passing(ring.blocks, self.owns, self.gots, ring.far - self.done, ring.count, moving)
-        )
+        moving = None
+        if self.done:
+            moving = self.flying
+            if main is not None:
+                main, *moving = tie(main, *moving)
+        if self.done == ring.far:
+            self.done += 1
+            self.result = passing(ring.blocks, self.owns, self.gots, 0, ring.count, moving)[0]
+            return main
+        owns = self.owns
+        if main is None and token is not None:
+            owns, _ = tie(owns, token)
+        made = passing(ring.blocks, owns, self.gots, ring.far - self.done, ring.count, moving)
         if main is not None:
-            main, ahead, behind = tie(main, ahead, behind)
-        self.moving = (ahead, behind)
+            main, *made = tie(main, *made)
+        self.made = made
+        self.flying = ring.send_both(*made)
         self.done += 1
-        if self.done == ring.far:
-            self.result = passing(ring.blocks, self.owns, self.gots, 0, ring.count, self.moving)[0]
         return main
 
     def finish(self):
         if self.ring.use:
-            while self.done < self.ring.far:
+            while self.done <= self.ring.far:
                 self.step()
         return self.result
 
@@ -177,7 +186,6 @@
     return moves
 
 
-ROOM = 16 << 20
 NEVER = -1e30
 
 
@@ -185,20 +193,32 @@
     return jax.ShapeDtypeStruct(shape, dtype)
 
 
-def kernel_call(kernel, operands, outs, scratch=(), scalars=0, cost=1.0):
+def kernel_call(kernel, operands, outs, scratch=(), scalars=0, cost=1.0, room=8, apart=0):
     inside = pl.BlockSpec(memory_space=pltpu.VMEM)
     word = pl.BlockSpec(memory_space=pltpu.SMEM)
     return pl.pallas_call(
         kernel,
-        in_specs=[word] * scalars + [inside] * (len(operands) - scalars),
+        in_specs=[word] * scalars
+        + [inside] * (len(operands) - scalars - apart)
+        + [pl.BlockSpec(memory_space=pl.ANY)] * apart,
         out_specs=[inside] * len(outs),
         out_shape=outs,
         scratch_shapes=scratch,
-        compiler_params=pltpu.CompilerParams(vmem_limit_bytes=ROOM),
+        compiler_params=pltpu.CompilerParams(vmem_limit_bytes=room << 20),
         cost_estimate=pl.CostEstimate(
             flops=int(cost * 1e9), bytes_accessed=1024, transcendentals=0
         ),
     )(*operands)
+
+
+def start_copies(pairs, sems):
+    copies = [
+        pltpu.make_async_copy(source, target, sems.at[index])
+        for index, (source, target) in enumerate(pairs)
+    ]
+    for copy in copies:
+        copy.start()
+    return copies
 
 
 def norm_parts(rows):
@@ -233,13 +253,15 @@
     scale = HEAD_DIM ** (-0.5)
     at = slice(layer, layer + 1)
 
-    def kernel(base_ref, part_ref, arrived_ref, bias_ref, gain_ref, shift_ref, w_ref, qb_ref, vb_ref,
-               state_ref, first_ref, q_ref, kv_ref):
+    def kernel(base_ref, part_ref, arrived_ref, bias_ref, gain_ref, shift_ref, qb_ref, vb_ref, w_far,
+               state_ref, first_ref, q_ref, kv_ref, w_ref, sems):
+        (copy,) = start_copies([(w_far.at[:, : 3 * width], w_ref)], sems)
         state = base_ref[...] + (part_ref[...].astype(WIDE) + arrived_ref[...].astype(WIDE))
         state += bias_ref[layer - 1 : layer, :]
         first = (norm_parts(state)[0] * gain_ref[at, :] + shift_ref[at, :]).astype(LOW)
         state_ref[...] = state
         first_ref[...] = first
+        copy.wait()
         query = (dot(first, w_ref[:, :width]) + qb_ref[at, :]).astype(LOW)
         q_ref[...] = query * jnp.asarray(scale, LOW)
         kv_ref[:, :width] = dot(first, w_ref[:, width : 2 * width]).astype(LOW)
@@ -247,13 +269,16 @@
 
     return kernel_call(
         kernel,
-        (base, part, arrived, bias, gain, shift, weights, q_bias, v_bias),
+        (base, part, arrived, bias, gain, shift, q_bias, v_bias, weights),
         [
             out((rows, depth), WIDE),
             out((rows, depth)),
             out((rows, width)),
             out((rows, 2 * width)),
-        ], cost=1.2)
+        ], scratch=[pltpu.VMEM((depth, 3 * width), LOW), pltpu.SemaphoreType.DMA((1,))],
+        cost=1.2,
+        apart=1,
+    )
 
 
 def feed(layer, state, part, arrived, out_bias, gain, shift, weights, up_bias, lows=None):
@@ -358,27 +383,28 @@
     return value.astype(WIDE).T.astype(LOW)
 
 
-def outer_feed(core, seconds, g_pres, lows, acts, which):
+def outer_feed(core, seconds, g_pres, lows, acts):
     depth = seconds[0].shape[1]
     size = acts[0].shape[1] // 2
 
-    def kernel(core_ref, s0, s1, g0, g1, l0, l1, a0, a1, out_ref):
-        start = jnp.where(core_ref[0] == which, 0, size)
+    def kernel(core_ref, s0, s1, g0, g1, l0, l1, a0, a1, *out_refs):
         for index, (left_refs, right_refs) in enumerate((((s0, s1), (g0, g1)), ((l0, l1), (a0, a1)))):
             left = jnp.concatenate([turned(ref[...]) for ref in left_refs], axis=1)
-            for at in range(0, size, 384):
-                columns = pl.ds(pl.multiple_of(start + at, 128), 384)
-                right = jnp.concatenate([ref[:, columns] for ref in right_refs])
-                base = index * size + at
-                out_ref[:, base : base + 384] = dot(left, right).astype(LOW)
+            for which, out_ref in ((1, out_refs[0]), (0, out_refs[1])):
+                start = jnp.where(core_ref[0] == which, 0, size)
+                for at in range(0, size, 384):
+                    columns = pl.ds(pl.multiple_of(start + at, 128), 384)
+                    right = jnp.concatenate([ref[:, columns] for ref in right_refs])
+                    base = index * size + at
+                    out_ref[:, base : base + 384] = dot(left, right).astype(LOW)
 
     return kernel_call(
         kernel,
         (core, *seconds, *g_pres, *lows, *acts),
-        [out((depth, 2 * size))],
+        [out((depth, 2 * size))] * 2,
         scalars=1,
-        cost=2.0,
-    )[0]
+        cost=3.4,
+    )
 
 
 def outer_heads(core, firsts, g_qkv, m_lows, mixeds, which):
@@ -415,29 +441,44 @@
     partial_in = not first and moving[0].shape[0] == half
 
     def kernel(blocks_ref, *refs):
+        if first:
+            moving_refs, refs = (), refs
+        else:
+            moving_refs, refs = refs[:2], refs[2:]
         own_refs, got_refs = refs[:parts], refs[parts : 2 * parts]
-        rest = refs[2 * parts :]
-        moving_refs, out_refs = (rest[:2], rest[2:]) if not first else ((), rest)
-
-        def here(index, offset=0, size=rows):
-            start = pl.multiple_of(blocks_ref[index] * rows + offset, 16)
-            at = pl.ds(start, size)
+        out_refs, held, sems = refs[2 * parts : -1 - 2 * parts], refs[-1 - 2 * parts : -1], refs[-1]
+        if first:
+            wanted = [(step, 0, half), (step, half, half)]
+        elif last:
+            wanted = [(0, 0, rows)]
+        else:
+            wanted = [(step, 0, rows), ((count - step) % count, 0, rows)]
+        pairs = []
+        for index, (block, offset, size) in enumerate(wanted):
+            start = pl.multiple_of(blocks_ref[block] * rows + offset, 16)
+            for ref, target in zip((*own_refs, *got_refs), held):
+                pairs.append((ref.at[pl.ds(start, size), :], target.at[index, pl.ds(0, size), :]))
+        copies = start_copies(pairs, sems)
+        for copy in copies:
+            copy.wait()
+
+        def here(index, size=rows):
             return jnp.concatenate(
                 [
-                    own[at, :].astype(WIDE) + got[at, :].astype(WIDE)
-                    for own, got in zip(own_refs, got_refs)
+                    held[k][index, :size].astype(WIDE) + held[parts + k][index, :size].astype(WIDE)
+                    for k in range(parts)
                 ],
                 axis=1,
             )
 
         if first:
-            out_refs[0][...] = here(step, 0, half).astype(LOW)
-            out_refs[1][...] = here(step, half, half).astype(LOW)
+            out_refs[0][...] = here(0, half).astype(LOW)
+            out_refs[1][...] = here(1, half).astype(LOW)
         elif last:
             total = here(0) + moving_refs[0][...].astype(WIDE) + moving_refs[1][...].astype(WIDE)
             out_refs[0][...] = total
         else:
-            ahead, behind = here(step), here((count - step) % count)
+            ahead, behind = here(0), here(1)
             a, b = moving_refs[0][...].astype(WIDE), moving_refs[1][...].astype(WIDE)
             if partial_in:
                 out_refs[0][:half, :] = (ahead[:half] + a).astype(LOW)
@@ -452,20 +493,47 @@
         outs = [out((rows, columns), WIDE)]
     else:
         outs = [out((half if first else rows, columns))] * 2
-    operands = (blocks, *owns, *gots) + (() if first else tuple(moving))
-    return kernel_call(kernel, operands, outs, scalars=1, cost=0.8)
+    operands = (blocks, *(() if first else moving), *owns, *gots)
+    return kernel_call(
+        kernel,
+        operands,
+        outs,
+        [pltpu.VMEM((2, rows, own.shape[1]), LOW) for own in (*owns, *gots)]
+        + [pltpu.SemaphoreType.DMA((4 * parts,))],
+        scalars=1,
+        cost=0.8,
+        apart=2 * parts,
+    )
 
 
 def pack_near(weights):
     layers, rows, size = weights[0].shape
 
-    def kernel(q_ref, k_ref, v_ref, o_ref, out_ref):
+    def kernel(*refs):
+        out_ref, held, sems = refs[4], refs[5:9], refs[9]
+        copies = [
+            pltpu.make_async_copy(refs[i], held[i], sems.at[i]) for i in range(4)
+        ]
+        for copy in copies:
+            copy.start()
+        for copy in copies:
+            copy.wait()
+        q_ref, k_ref, v_ref, o_ref = held
         for layer in range(layers):
             out_ref[layer] = jnp.concatenate(
                 [q_ref[layer], k_ref[layer], v_ref[layer], turned(o_ref[layer])], axis=1
             )
 
-    return kernel_call(kernel, weights, [out((layers, rows, 4 * size))])[0]
+    return pl.pallas_call(
+        kernel,
+        in_specs=[pl.BlockSpec(memory_space=pl.ANY)] * 4,
+        out_specs=pl.BlockSpec(memory_space=pltpu.VMEM),
+        out_shape=out((layers, rows, 4 * size)),
+        scratch_shapes=[pltpu.VMEM(w.shape, LOW) for w in weights]
+        + [pltpu.SemaphoreType.DMA((4,))],
+        compiler_params=pltpu.CompilerParams(vmem_limit_bytes=8 << 20),
+        cost_estimate=pl.CostEstimate(flops=1000, bytes_accessed=1024, transcendentals=0),
+    )(*weights)
 
 
 def weave_near(core, own, peer):
@@ -487,30 +555,20 @@
     )
 
 
-def pack_far(up, down):
-    layers, rows, size = up.shape
-
-    def kernel(up_ref, down_ref, *out_refs):
+def weave_far(core, own, peer):
+    layers, rows, columns = own[0].shape
+
+    def kernel(core_ref, u_own, d_own, u_peer, d_peer, *out_refs):
+        first = core_ref[0] == 0
         for layer, out_ref in enumerate(out_refs):
-            out_ref[:, :size] = up_ref[layer]
-            out_ref[:, size:] = turned(down_ref[layer])
-
-    return kernel_call(kernel, (up, down), [out((rows, 2 * size))] * layers)
-
-
-def weave_far(core, own, peer):
-    rows, columns = own[0].shape
-
-    def kernel(core_ref, *refs):
-        first = core_ref[0] == 0
-        count = len(own)
-        for index in range(count):
-            a, b = refs[index][...], refs[count + index][...]
-            refs[2 * count + index][:, :columns] = jnp.where(first, a, b)
-            refs[2 * count + index][:, columns:] = jnp.where(first, b, a)
-
-    return kernel_call(
-        kernel, (core, *own, *peer), [out((rows, 2 * columns))] * len(own), scalars=1
+            for index, (own_ref, peer_ref) in enumerate(((u_own, u_peer), (d_own, d_peer))):
+                a, b = own_ref[layer], peer_ref[layer]
+                low, high = index * columns, (2 + index) * columns
+                out_ref[:, low : low + columns] = jnp.where(first, a, b)
+                out_ref[:, high : high + columns] = jnp.where(first, b, a)
+
+    return kernel_call(
+        kernel, (core, *own, *peer), [out((rows, 4 * columns))] * layers, scalars=1
     )
 
 
@@ -583,7 +641,9 @@
     width = q_bias.shape[1]
     scale = HEAD_DIM ** (-0.5)
 
-    def kernel(side_ref, own_ref, other_ref, embed_ref, gain_ref, shift_ref, w_ref, qb_ref, vb_ref, *refs):
+    def kernel(side_ref, own_ref, other_ref, embed_ref, gain_ref, shift_ref, qb_ref, vb_ref, w_far, *refs):
+        w_ref, sems = refs[8:]
+        (copy,) = start_copies([(w_far.at[:, : 3 * width], w_ref)], sems)
         firsts = []
         for j in range(2):
             rows_in = jnp.where(side_ref[0] == j, own_ref[...], other_ref[...])
@@ -593,6 +653,7 @@
             refs[2 + j][...] = first
             firsts.append(first)
         first = jnp.concatenate(firsts)
+        copy.wait()
         query = (dot(first, w_ref[:, :width]) + qb_ref[0:1, :]).astype(LOW)
         query = query * jnp.asarray(scale, LOW)
         key = dot(first, w_ref[:, width : 2 * width]).astype(LOW)
@@ -605,12 +666,15 @@
 
     made = kernel_call(
         kernel,
-        (side, own, other, embed, gain, shift, weights, q_bias, v_bias),
+        (side, own, other, embed, gain, shift, q_bias, v_bias, weights),
         [out((rows, depth), WIDE)] * 2
         + [out((rows, depth))] * 2
         + [out((rows, width))] * 2
         + [out((rows, 2 * width))] * 2,
-        scalars=1, cost=1.8)
+        scalars=1, scratch=[pltpu.VMEM((depth, 3 * width), LOW), pltpu.SemaphoreType.DMA((1,))],
+        cost=1.8,
+        apart=1,
+    )
     return [made[2 * i : 2 * i + 2] for i in range(4)]
 
 
@@ -619,18 +683,26 @@
     depth = weights.shape[0]
     size = hidden // 2
 
-    def kernel(side_ref, a0, a1, w_ref, away_ref, here_ref):
+    def kernel(side_ref, a0, a1, w_far, away_ref, here_ref, w_ref, sems):
+        copies = start_copies(
+            [(w_far.at[:, (2 * i + 1) * size : (2 * i + 2) * size], w_ref.at[i]) for i in range(2)], sems
+        )
+        for copy in copies:
+            copy.wait()
         for flip, ref in ((1, away_ref), (0, here_ref)):
             act = jnp.where(side_ref[0] == flip, a0[...], a1[...])
-            total = dot_nt(act[:, :size], w_ref[:, size : 2 * size])
-            total += dot_nt(act[:, size:], w_ref[:, 3 * size :])
+            total = dot_nt(act[:, :size], w_ref[0])
+            total += dot_nt(act[:, size:], w_ref[1])
             ref[...] = total.astype(ref.dtype)
 
     return kernel_call(
         kernel,
         (side, *acts, weights),
         [out((rows, depth)), out((rows, depth), WIDE)],
-        scalars=1, cost=1.4)
+        scalars=1, scratch=[pltpu.VMEM((2, depth, size), LOW), pltpu.SemaphoreType.DMA((2,))],
+        cost=1.4,
+        apart=1,
+    )
 
 
 def last_rows(side, middles, here, crossed, bias, layer):
@@ -650,7 +722,8 @@
     rows, width = dqs[0].shape
     depth = weights.shape[0]
 
-    def kernel(side_ref, dq0, dq1, own0, own1, away0, away1, w_ref, g_ref, part0, part1, sums_ref):
+    def kernel(side_ref, dq0, dq1, own0, own1, away0, away1, w_far, g_ref, part0, part1, sums_ref, w_ref, sems):
+        (copy,) = start_copies([(w_far.at[:, : 3 * width], w_ref)], sems)
         pair = (
             own0[...].astype(WIDE)
             + own1[...].astype(WIDE)
@@ -660,7 +733,8 @@
         g_ref[rows:, :width] = dq1[...]
         g_ref[:, width:] = pair
         g = g_ref[...]
-        total = dot_nt(g, w_ref[:, : 3 * width])
+        copy.wait()
+        total = dot_nt(g, w_ref[...])
         low, high = total[:rows], total[rows:]
         if last:
             part0[...] = jnp.where(side_ref[0] == 0, high, low).astype(LOW)
@@ -680,7 +754,10 @@
             out((rows, depth), WIDE if last else LOW),
             out((8, width), WIDE),
         ],
-        scalars=1, cost=1.6)
+        scalars=1, scratch=[pltpu.VMEM((depth, 3 * width), LOW), pltpu.SemaphoreType.DMA((1,))],
+        cost=1.6,
+        apart=1,
+    )
 
 
 def first_rows(side, here, arrived, states, g_middles, gain):
@@ -764,7 +841,7 @@
     )
 
 
-def matrix_outputs(results, size):
+def matrix_outputs(results, size, turn):
     layers = len(results)
     rows, columns = results[0].shape
     count = columns // size
@@ -774,12 +851,13 @@
             value = refs[layer][...].astype(WIDE)
             for i in range(count):
                 part = value[:, i * size : (i + 1) * size]
-                refs[layers + i][layer] = part.T if i == count - 1 else part
+                refs[layers + i][layer] = part.T if turn and i == count - 1 else part
 
     return kernel_call(
         kernel,
         results,
-        [out((layers, rows, size), WIDE)] * (count - 1) + [out((layers, size, rows), WIDE)],
+        [out((layers, rows, size), WIDE)] * (count - 1)
+        + [out((layers, size, rows) if turn else (layers, rows, size), WIDE)],
     )
 
 
@@ -804,7 +882,8 @@
 
     def kernel(q_ref, qm_ref, *refs):
         kv_refs, km_refs = refs[:blocks], refs[blocks : 2 * blocks]
-        w_ref, mixed_ref, norm_ref, part_ref, held = refs[2 * blocks :]
+        w_far, mixed_ref, norm_ref, part_ref, held, w_ref, sems = refs[2 * blocks :]
+        (copy,) = start_copies([(w_far.at[:, 3 * width :], w_ref)], sems)
         parts = []
         for pair in range(heads // 2):
             at = slice(pair * 128, pair * 128 + 128)
@@ -835,13 +914,20 @@
                 norm_ref[row : row + 1, :] = top + jnp.log(bulk)
         mixed = jnp.concatenate(parts).T.astype(LOW)
         mixed_ref[...] = mixed
-        part_ref[...] = dot_nt(mixed, w_ref[:, 3 * width :]).astype(LOW)
+        copy.wait()
+        part_ref[...] = dot_nt(mixed, w_ref[...]).astype(LOW)
 
     return kernel_call(
         kernel,
         (query, q_marks, *pairs, *k_marks, weights),
         [out((rows, width)), out((8, rows), WIDE), out((rows, weights.shape[0]))],
-        [pltpu.VMEM((blocks, size, rows), WIDE)], cost=4.0)
+        [
+            pltpu.VMEM((blocks, size, rows), WIDE),
+            pltpu.VMEM((weights.shape[0], width), LOW),
+            pltpu.SemaphoreType.DMA((1,)),
+        ], cost=4.0,
+        apart=1,
+    )
 
 
 def attend_back(layer, grads, part, arrived, middle, gain, weights, query, q_marks, norms, pairs, k_marks):
@@ -853,9 +939,12 @@
     scale = HEAD_DIM ** (-0.5)
     near = blocks // 2
 
-    def kernel(grads_ref, part_ref, arrived_ref, middle_ref, gain_ref, weight_ref, q_ref, qm_ref, norm_ref, *refs):
+    def kernel(grads_ref, part_ref, arrived_ref, middle_ref, gain_ref, q_ref, qm_ref, norm_ref, *refs):
         kv_refs, km_refs = refs[:blocks], refs[blocks : 2 * blocks]
-        gm_ref, low_ref, sums_ref, dq_ref, own_ref, away_ref, p_wide, w_wide, p_all, s_all = refs[2 * blocks :]
+        w_far, *refs = refs[2 * blocks :]
+        gm_ref, low_ref, sums_ref, dq_ref, own_ref, away_ref, *refs = refs
+        p_wide, w_wide, p_all, s_all, weight_ref, sems = refs
+        (copy,) = start_copies([(w_far.at[:, 3 * width :], weight_ref)], sems)
         incoming = part_ref[...].astype(WIDE) + arrived_ref[...].astype(WIDE)
         gain_grad, shift_grad, through = norm_backward(
             incoming, middle_ref[...], gain_ref[layer : layer + 1, :]
@@ -867,7 +956,8 @@
         sums_ref[0:1, :] = gain_grad
         sums_ref[1:2, :] = shift_grad
         sums_ref[2:3, :] = jnp.sum(g_middle, axis=0, keepdims=True)
-        g_mixed = dot(low, weight_ref[:, 3 * width :]).astype(LOW)
+        copy.wait()
+        g_mixed = dot(low, weight_ref[...]).astype(LOW)
         dqs = []
         for pair in range(heads // 2):
             at = slice(pair * 128, pair * 128 + 128)
@@ -912,7 +1002,7 @@
     length = blocks * size
     return kernel_call(
         kernel,
-        (grads, part, arrived, middle, gain, weights, query, q_marks, norms, *pairs, *k_marks),
+        (grads, part, arrived, middle, gain, query, q_marks, norms, *pairs, *k_marks, weights),
         [
             out((rows, depth), WIDE),
             out((rows, depth)),
@@ -926,7 +1016,12 @@
             pltpu.VMEM((blocks, size, rows), WIDE),
             pltpu.VMEM((length, 2 * rows), LOW),
             pltpu.VMEM((length, 2 * rows), LOW),
-        ], cost=6.4)
+            pltpu.VMEM((depth, width), LOW),
+            pltpu.SemaphoreType.DMA((1,)),
+        ], cost=1.0,
+        room=14,
+        apart=1,
+    )
 
 
 def local(
@@ -977,11 +1072,12 @@
             up_weight,
             down_weight,
         )
-    far_own = pack_far(up_weight, down_weight)
+    far_own = (up_weight, jnp.swapaxes(down_weight, 1, 2))
     far_pieces = weave_far(core, far_own, [swap_core(piece) for piece in far_own])
     near[0].step()
     near[0].step()
     token = near[0].current if ring.use else None
+    cotangent_other = swap_y(tie(cotangent, token)[0] if ring.use else cotangent)
     near[0].finish()
     far = [Gather(ring, far_pieces[0])]
     far[0].step(token)
@@ -992,10 +1088,9 @@
     far.append(Gather(ring, far_pieces[1]))
 
     def exchange(parts):
-        first = swap_y(parts[0])
-        second = swap_y(tie(parts[1], first)[0])
-        first, _ = tie(first, parts[1])
-        return [first, second]
+        arrived = [swap_y(part) for part in parts]
+        arrived[0], parts[1] = tie(arrived[0], parts[1])
+        return arrived
 
     kept = []
     for layer in range(layers):
@@ -1024,21 +1119,24 @@
             states, firsts, queries, pairs = ([m[i] for m in made] for i in range(4))
         pairs = list(pairs) + [swap_core(pair) for pair in pairs]
         mixeds, norms, parts = [], [], []
+        far[layer].step(queries[1])
         for j in range(2):
             mixed, norm, part = attend(queries[j], q_marks[j], pairs, k_marks, w_near)
             mixeds.append(mixed)
             norms.append(norm)
             parts.append(part)
-            far[layer].step(part)
-        arrived = exchange(parts)
+        far[layer].step(parts[1])
+        arrived = [swap_y(part) for part in parts]
         if layer == 0:
             token = far[0].current if ring.use else None
             near[1].step(token)
         far[layer].finish()
+        if layer == 0:
+            near[1].step(far[0].current)
         w_far = far[layer].whole
+        arrived[0], w_far = tie(arrived[0], w_far)
         if layer == 0:
-            cotangent, _ = tie(cotangent, parts[1])
-            seed0, seed1, seed_sums = seed_rows(side, cotangent, swap_y(cotangent), k_marks[:2])
+            seed0, seed1, seed_sums = seed_rows(side, cotangent, cotangent_other, k_marks[:2])
             seeds = [seed0, seed1]
         made = []
         for j in range(2):
@@ -1056,7 +1154,7 @@
                     seeds[j] if layer == last else None,
                 )
             )
-            if layer == 0:
+            if layer == 0 and j == 0:
                 near[1].step(made[j][4])
         middles, seconds, acts, others, branches = ([m[i] for m in made] for i in range(5))
         kept.append((states, firsts, queries, pairs, norms, mixeds, middles, seconds, acts, others))
@@ -1107,16 +1205,22 @@
         arrived = exchange(parts)
         if layer < last:
             arrived[0] = advance(arrived[0])
+            feed_away, feed_own = outer_feed(core, seconds, g_pres, lows, acts)
+            arrived[0], feed_own = tie(arrived[0], feed_own)
+            got = swap_core(feed_away)
         made = []
         for j in range(2):
             if j == 1:
-                feed_away = outer_feed(core, seconds, g_pres, lows, acts, 1)
-                got = swap_core(feed_away)
-                feed_own = outer_feed(core, seconds, g_pres, lows, acts, 0)
+                if layer == last:
+                    feed_away, feed_own = outer_feed(core, seconds, g_pres, lows, acts)
+                    got = swap_core(feed_away)
                 arrived[1], feed_own, got = tie(arrived[1], feed_own, got)
-                arrived[1] = advance(arrived[1])
                 under_way.append(Scatter(ring, [feed_own], [got]))
                 results[layer, "feed"] = under_way[-1]
+                arrived[1] = advance(arrived[1])
+                if layer == last:
+                    acts_after, _ = tie(acts, arrived[1])
+                    away_rows, here_rows = last_branch(side, acts_after, w_far)
             made.append(
                 attend_back(
                     layer,
@@ -1142,7 +1246,10 @@
             (base + 4, ("own", 2), sums),
         ]
         aways = [swap_core(away) for away in aways]
-        aways[1] = advance(aways[1])
+        if layer == last:
+            aways[1] = advance(aways[1])
+            aways[1], away_rows = tie(aways[1], away_rows)
+            crossed = swap_y(away_rows)
         g_qkv, part0, part1, sums = project_back(side, dqs, owns, aways, w_near, layer == 0)
         entries += [(base + 6, ("half", 0), (sums,)), (base + 7, ("half", 1), (sums,))]
         if layer > 0:
@@ -1154,20 +1261,21 @@
         near_away = outer_heads(core, firsts, g_qkv, m_lows, mixeds, 1)
         near_got = swap_core(near_away)
         near_own = outer_heads(core, firsts, g_qkv, m_lows, mixeds, 0)
+        results[layer, "near"] = Scatter(ring, [near_own], [near_got])
+        under_way.append(results[layer, "near"])
         if layer == last:
             arrived[0], near_own, near_got = tie(arrived[0], near_own, near_got)
             arrived[0] = advance(arrived[0])
-        under_way.append(Scatter(ring, [near_own], [near_got]))
-        results[layer, "near"] = under_way[-1]
+        else:
+            results[0, "near"].step()
+            first_message = results[0, "near"].made[0]
+            results[0, "feed"].step(token=first_message)
+            arrived, _ = tie(arrived, first_message)
         if layer == last:
-            acts_after, _ = tie(acts, near_own)
-            away_rows, here_rows = last_branch(side, acts_after, w_far)
-            crossed = swap_y(away_rows)
             denoised = last_rows(side, middles, here_rows, crossed, down_bias, layer)
     input_grad, sums = first_rows(side, part1, arrived, states, g_middles, first_gain)
     entries += [(0, ("one", 0), (sums,)), (1, ("one", 1), (sums,))]
     total = vector_rows(place, entries, layers, depth)
-    results[0, "near"].step()
     if ring.use:
         for move_by in exchanges(ring.count):
             total = total + move_by(total)
@@ -1176,9 +1284,10 @@
         total = lax.psum(total, ("fsdp", "tensor"))
     vectors = vector_outputs(place, total, layers, head_width)
     up_out, down_out = matrix_outputs(
-        [results[layer, "feed"].finish() for layer in range(layers)], hidden_width
-    )
-    heads = matrix_outputs([results[layer, "near"].finish() for layer in range(layers)], head_width)
+        [results[layer, "feed"].finish() for layer in range(layers)], hidden_width, False
+    )
+    down_out = jnp.swapaxes(down_out, 1, 2)
+    heads = matrix_outputs([results[layer, "near"].finish() for layer in range(layers)], head_width, True)
     return (denoised, input_grad, *heads, up_out, down_out, *vectors)
 
 

time: 373 us -> 358 us (0.960)
  waiting for transfers between devices: 127 us -> 111 us
  Pallas kernels: 117 us -> 128 us
  local copies, waits for them, and re-layouts: 33.1 us -> 23 us
    pallas_call x61 -> x57, Pallas kernels: 117 us -> 128 us  [kernel_call(): pl.pallas_call(kernel, in_specs=[word] * scalars + [inside] * (len(operan...]
    unnamed x245 -> x264, local copies, waits for them, and re-layouts: 20.4 us -> 11.1 us
    ppermute x16, starting transfers between devices: 11.2 us -> 19.2 us  [send_both(): lax.ppermute(behind, 'fsdp', self.pairs[1])]
    ppermute x16, starting transfers between devices: 21.9 us -> 14.4 us  [send_both(): lax.ppermute(ahead, 'fsdp', self.pairs[0])]
    ppermute x17, waiting for transfers between devices: 43.1 us -> 35.9 us  [swap_y(): return lax.ppermute(value, 'tensor', SWAP_Y)]
    ppermute x16, waiting for transfers between devices: 17.7 us -> 13.2 us  [send_both(): lax.ppermute(ahead, 'fsdp', self.pairs[0])]
    ppermute x16, waiting for transfers between devices: 44 us -> 39.5 us  [split_send(): return lax.ppermute(value, ('fsdp', 'tensor'), self.split)]
    ppermute x33, waiting for transfers between devices: 3.74 us -> 7.52 us  [swap_core(): return lax.ppermute(value, 'tensor', SWAP_CORE)]
  transfers between devices with their start and end apart: 101 -> 101, of which waited for: 43 -> 39; matrix products, arithmetic and copies ran while one was open for 4% -> 3% of each run, Pallas kernels for 20% -> 25%
where the time goes in v1:
time: 358 us; the launch traced here: 353 us
  Pallas kernels  128 us (36%)
  waiting for transfers between devices  111 us (31%)
  starting transfers between devices  87.8 us (25%)
  local copies, waits for them, and re-layouts  23 us (6%)
  between operations  3.6 us (1%)
    pallas_call x57, Pallas kernels, kernel_call(): pl.pallas_call(kernel, in_specs=[word] * scalars + [inside] * (len(operan...  128 us
    ppermute x16, waiting for transfers between devices, split_send(): return lax.ppermute(value, ('fsdp', 'tensor'), self.split)  39.5 us
    ppermute x17, waiting for transfers between devices, swap_y(): return lax.ppermute(value, 'tensor', SWAP_Y)  35.9 us
    ppermute x16, starting transfers between devices, split_send(): return lax.ppermute(value, ('fsdp', 'tensor'), self.split)  26.2 us
    ppermute x17, starting transfers between devices, swap_y(): return lax.ppermute(value, 'tensor', SWAP_Y)  20.3 us
    ppermute x16, starting transfers between devices, send_both(): lax.ppermute(behind, 'fsdp', self.pairs[1])  19.2 us
    ppermute x16, starting transfers between devices, send_both(): lax.ppermute(ahead, 'fsdp', self.pairs[0])  14.4 us
    ppermute x16, waiting for transfers between devices, send_both(): lax.ppermute(ahead, 'fsdp', self.pairs[0])  13.2 us
  transfers between devices with their start and end apart: 101, of which 39 were waited for; matrix products, arithmetic and copies ran while one was open for 3% of the time, Pallas kernels for 25%

profile of v1, /device:TPU:0, one launch (start us, length us, event | category | flops | bytes accessed | tf_op | source)
XLA Modules:
  0.0 353.4 jit_solution(2531739998387781486)
XLA Ops:
  12.5 2.7 collective-permute-done.2
  18.9 3.9 %collective-permute-done.5 = bf16[96,1536]{1,0:T(8,128)(2,1)S(1)} collective-permute-done((bf16[96,1536]{1,0:T(8,128)(2,1)}, bf16[96,1536]{1,0:T(8,128)(2,1)S(1)}, u32[]{:S(2)}, u32[]{:S(2)}) %collective-permute-start.5) | collective-permute-done | bytes 294944 | tf_op jit(solution)/shard_map/ppermute | solution.py:72
  25.3 4.2 %collective-permute-done.7 = bf16[96,1536]{1,0:T(8,128)(2,1)S(1)} collective-permute-done((bf16[96,1536]{1,0:T(8,128)(2,1)S(1)}, bf16[96,1536]{1,0:T(8,128)(2,1)S(1)}, u32[]{:S(2)}, u32[]{:S(2)}) %collective-permute-start.7) | collective-permute-done | bytes 294944 | tf_op jit(solution)/shard_map/ppermute | solution.py:72
  44.3 4.1 %shard_map.321 = (bf16[256,384]{1,0:T(8,128)(2,1)S(1)}, f32[8,256]{1,0:T(8,128)S(1)}, bf16[256,768]{1,0:T(8,128)(2,1)S(1)}) custom-call(bf16[256,384]{1,0:T(8,128)(2,1)S(1)} %get-tuple-element.336.q_ref, bf16[256,128]{1,0:T(8,128)(2,1)S(1)} %get-tuple-element.338.qm_ref, bf16[256,768]{1,0:T(8,128)(2,1)S(1)} %get-tuple-element.325.refs_0_, ...), custom_call_target="tpu_custom_call" | custom-call | flops 4000000000 | bytes 1024 | tf_op jit(solution)/shard_map/pallas_call | solution.py:199
  50.2 4.1 %shard_map.319 = (bf16[256,384]{1,0:T(8,128)(2,1)S(1)}, f32[8,256]{1,0:T(8,128)S(1)}, bf16[256,768]{1,0:T(8,128)(2,1)S(1)}) custom-call(bf16[256,384]{1,0:T(8,128)(2,1)S(1)} %get-tuple-element.322.q_ref, bf16[256,128]{1,0:T(8,128)(2,1)S(1)} %get-tuple-element.324.qm_ref, bf16[256,768]{1,0:T(8,128)(2,1)S(1)} %get-tuple-element.325.refs_0_, ...), custom_call_target="tpu_custom_call" | custom-call | flops 4000000000 | bytes 1024 | tf_op jit(solution)/shard_map/pallas_call | solution.py:199
  56.7 8.2 %collective-permute-done.20 = bf16[96,3072]{1,0:T(8,128)(2,1)S(1)} collective-permute-done((bf16[96,3072]{1,0:T(8,128)(2,1)S(1)}, bf16[96,3072]{1,0:T(8,128)(2,1)S(1)}, u32[]{:S(2)}, u32[]{:S(2)}) %collective-permute-start.20) | collective-permute-done | bytes 589856 | tf_op jit(solution)/shard_map/ppermute | solution.py:72
  68.2 3.4 collective-permute-done.22
  81.2 2.8 shard_map.322
  89.3 2.8 shard_map.323
  105.8 2.8 shard_map.324
  110.8 4.1 %shard_map.327 = (bf16[256,384]{1,0:T(8,128)(2,1)S(1)}, f32[8,256]{1,0:T(8,128)S(1)}, bf16[256,768]{1,0:T(8,128)(2,1)S(1)}) custom-call(bf16[256,384]{1,0:T(8,128)(2,1)S(1)} %get-tuple-element.362.q_ref, bf16[256,128]{1,0:T(8,128)(2,1)S(1)} %get-tuple-element.338.qm_ref, bf16[256,768]{1,0:T(8,128)(2,1)S(1)} %get-tuple-element.355.refs_0_, ...), custom_call_target="tpu_custom_call" | custom-call | flops 4000000000 | bytes 1024 | tf_op jit(solution)/shard_map/pallas_call | solution.py:199
  117.0 4.1 %shard_map.326 = (bf16[256,384]{1,0:T(8,128)(2,1)S(1)}, f32[8,256]{1,0:T(8,128)S(1)}, bf16[256,768]{1,0:T(8,128)(2,1)S(1)}) custom-call(bf16[256,384]{1,0:T(8,128)(2,1)S(1)} %get-tuple-element.354.q_ref, bf16[256,128]{1,0:T(8,128)(2,1)S(1)} %get-tuple-element.324.qm_ref, bf16[256,768]{1,0:T(8,128)(2,1)S(1)} %get-tuple-element.355.refs_0_, ...), custom_call_target="tpu_custom_call" | custom-call | flops 4000000000 | bytes 1024 | tf_op jit(solution)/shard_map/pallas_call | solution.py:199
  123.4 8.2 %collective-permute-done.42 = bf16[96,3072]{1,0:T(8,128)(2,1)S(1)} collective-permute-done((bf16[96,3072]{1,0:T(8,128)(2,1)S(1)}, bf16[96,3072]{1,0:T(8,128)(2,1)S(1)}, u32[]{:S(2)}, u32[]{:S(2)}) %collective-permute-start.42) | collective-permute-done | bytes 589856 | tf_op jit(solution)/shard_map/ppermute | solution.py:72
  133.5 5.1 %collective-permute-done.44 = bf16[48,3072]{1,0:T(8,128)(2,1)S(1)} collective-permute-done((bf16[48,3072]{1,0:T(8,128)(2,1)S(1)}, bf16[48,3072]{1,0:T(8,128)(2,1)S(1)}, u32[]{:S(2)}, u32[]{:S(2)}) %collective-permute-start.44) | collective-permute-done | bytes 294944 | tf_op jit(solution)/shard_map/ppermute | solution.py:72
  140.2 3.7 %shard_map.329 = (f32[256,768]{1,0:T(8,128)S(1)}, bf16[256,768]{1,0:T(8,128)(2,1)S(1)}, bf16[256,1536]{1,0:T(8,128)(2,1)S(1)}, bf16[256,1536]{1,0:T(8,128)(2,1)S...) custom-call(f32[256,768]{1,0:T(8,128)S(1)} %get-tuple-element.353.refs_0_.state_ref, ...), custom_call_target="tpu_custom_call" | custom-call | flops 4000000000 | bytes 1024 | tf_op jit(solution)/shard_map/pallas_call | solution.py:199
  146.1 4.5 %shard_map.330 = (f32[256,768]{1,0:T(8,128)S(1)}, bf16[256,768]{1,0:T(8,128)(2,1)S(1)}, bf16[256,1536]{1,0:T(8,128)(2,1)S(1)}, bf16[256,1536]{1,0:T(8,128)(2,1)S...) custom-call(f32[256,768]{1,0:T(8,128)S(1)} %get-tuple-element.372.refs_0_.state_ref, ...), custom_call_target="tpu_custom_call" | custom-call | flops 4000000000 | bytes 1024 | tf_op jit(solution)/shard_map/pallas_call | solution.py:199
  151.4 4.3 %collective-permute-done.49.arrived_ref = bf16[256,768]{1,0:T(8,128)(2,1)S(1)} collective-permute-done((bf16[256,768]{1,0:T(8,128)(2,1)S(1)}, bf16[256,768]{1,0:T(8,128)(2,1)S(1)}, u32[]{:S(2)}, u32[]{:S(2)}) %collective-permute-start.49) | collective-permute-done | bytes 393248 | tf_op jit(solution)/shard_map/ppermute | solution.py:26
  155.8 7.5 %shard_map.331 = (f32[256,768]{1,0:T(8,128)S(1)}, bf16[256,768]{1,0:T(8,128)(2,1)S(1)}, f32[8,768]{1,0:T(8,128)S(1)}, bf16[256,384]{1,0:T(8,128)(2,1)S(1)}, bf16...) custom-call(bf16[256,768]{1,0:T(8,128)(2,1)S(1)} %get-tuple-element.370.refs_8_.grads_ref.l0, ...), custom_call_target="tpu_custom_call" | custom-call | flops 1000000000 | bytes 1024 | tf_op jit(solution)/shard_map/pallas_call | solution.py:199
  163.5 4.1 %shard_map.332 = (bf16[768,1536]{1,0:T(8,128)(2,1)}, bf16[768,1536]{1,0:T(8,128)(2,1)S(1)}) custom-call(s32[1]{0:T(128)} %bitcast.1.core_ref, bf16[256,768]{1,0:T(8,128)(2,1)S(1)} %get-tuple-element.378.s0, bf16[256,768]{1,0:T(8,128)(2,1)S(1)} %get-tuple-element.379.s1, bf16[256,1536]{1,0:T(8,128)(2,1)S(1)} %get-tuple-element.386.g0, ...), custom_call_target="tpu_custom_call" | custom-call | flops 3400000000 | bytes 1024 | tf_op jit(solution)/shard_map/pallas_call | solution.py:199
  169.3 10.2 %collective-permute-done.48.arrived_ref = bf16[256,768]{1,0:T(8,128)(2,1)} collective-permute-done((bf16[256,768]{1,0:T(8,128)(2,1)}, bf16[256,768]{1,0:T(8,128)(2,1)}, u32[]{:S(2)}, u32[]{:S(2)}) %collective-permute-start.48) | collective-permute-done | bytes 393248 | tf_op jit(solution)/shard_map/ppermute | solution.py:26
  182.0 9.0 %shard_map.335 = (f32[256,768]{1,0:T(8,128)S(1)}, bf16[256,768]{1,0:T(8,128)(2,1)S(1)}, f32[8,768]{1,0:T(8,128)S(1)}, bf16[256,384]{1,0:T(8,128)(2,1)S(1)}, bf16...) custom-call(bf16[256,768]{1,0:T(8,128)(2,1)S(1)} %copy-done.40, bf16[256,768]{1,0:T(8,128)(2,1)} %get-tuple-element.399.part_ref, ...), custom_call_target="tpu_custom_call" | custom-call | flops 1000000000 | bytes 1024 | tf_op jit(solution)/shard_map/pallas_call | solution.py:199
  201.0 2.8 shard_map.338
  211.3 6.2 %collective-permute-done.56.arrived_ref = bf16[256,768]{1,0:T(8,128)(2,1)S(1)} collective-permute-done((bf16[256,768]{1,0:T(8,128)(2,1)S(1)}, bf16[256,768]{1,0:T(8,128)(2,1)S(1)}, u32[]{:S(2)}, u32[]{:S(2)}) %collective-permute-start.56) | collective-permute-done | bytes 393248 | tf_op jit(solution)/shard_map/ppermute | solution.py:26
  227.5 3.6 %collective-permute-done.62.refs_0_ = bf16[96,1536]{1,0:T(8,128)(2,1)S(1)} collective-permute-done((bf16[96,1536]{1,0:T(8,128)(2,1)S(1)}, bf16[96,1536]{1,0:T(8,128)(2,1)S(1)}, u32[]{:S(2)}, u32[]{:S(2)}) %collective-permute-start.62) | collective-permute-done | bytes 294944 | tf_op jit(solution)/shard_map/ppermute | solution.py:75
  238.2 3.5 shard_map.348
  245.9 7.9 %collective-permute-done.60.arrived_ref = bf16[256,768]{1,0:T(8,128)(2,1)S(1)} collective-permute-done((bf16[256,768]{1,0:T(8,128)(2,1)S(1)}, bf16[256,768]{1,0:T(8,128)(2,1)S(1)}, u32[]{:S(2)}, u32[]{:S(2)}) %collective-permute-start.60) | collective-permute-done | bytes 393248 | tf_op jit(solution)/shard_map/ppermute | solution.py:26
  255.8 3.1 collective-permute-done.68.refs_0_
  263.8 6.5 %shard_map.349 = (f32[256,768]{1,0:T(8,128)S(1)}, bf16[256,768]{1,0:T(8,128)(2,1)S(1)}, f32[8,768]{1,0:T(8,128)S(1)}, bf16[256,384]{1,0:T(8,128)(2,1)S(1)}, bf16...) custom-call(f32[256,768]{1,0:T(8,128)S(1)} %get-tuple-element.441.grads_ref, ...), custom_call_target="tpu_custom_call" | custom-call | flops 1000000000 | bytes 1024 | tf_op jit(solution)/shard_map/pallas_call | solution.py:199
  273.3 6.7 %shard_map.352 = (f32[256,768]{1,0:T(8,128)S(1)}, bf16[256,768]{1,0:T(8,128)(2,1)S(1)}, f32[8,768]{1,0:T(8,128)S(1)}, bf16[256,384]{1,0:T(8,128)(2,1)S(1)}, bf16...) custom-call(f32[256,768]{1,0:T(8,128)S(1)} %get-tuple-element.487.grads_ref, ...), custom_call_target="tpu_custom_call" | custom-call | flops 1000000000 | bytes 1024 | tf_op jit(solution)/shard_map/pallas_call | solution.py:199
  303.9 2.9 collective-permute-done.79.refs_0_
  312.2 4.3 %collective-permute-done.86.refs_1_ = bf16[48,768]{1,0:T(8,128)(2,1)S(1)} collective-permute-done((bf16[48,768]{1,0:T(8,128)(2,1)S(1)}, bf16[48,768]{1,0:T(8,128)(2,1)S(1)}, u32[]{:S(2)}, u32[]{:S(2)}) %collective-permute-start.86) | collective-permute-done | bytes 73760 | tf_op jit(solution)/shard_map/ppermute | solution.py:75
  319.1 3.3 collective-permute-done.87
  (544 shorter events, 195.3 us)
Async XLA Ops:
  5.4 30.7 %collective-permute-start = (bf16[256,768]{1,0:T(8,128)(2,1)}, bf16[256,768]{1,0:T(8,128)(2,1)S(1)}, u32[]{:S(2)}, u32[]{:S(2)}) collective-permute-start(bf16[256,768]{1,0:T(8,128)(2,1)} %own_ref.1), channel_id=1, source_target_pairs={{0,2},{2,0},{1,3},{3,1},{4,6},{6,4},{5,7},{7,5},{8,10},{10,8},{9,1... | collective-permute-start | bytes 1179656 | tf_op jit(solution)/shard_map/ppermute | solution.py:26
  31.1 11.3 %collective-permute-start.16 = (bf16[96,3072]{1,0:T(8,128)(2,1)S(1)}, bf16[96,3072]{1,0:T(8,128)(2,1)S(1)}, u32[]{:S(2)}, u32[]{:S(2)}) collective-permute-start(bf16[96,3072]{1,0:T(8,128)(2,1)S(1)} %get-tuple-element.335), channel_id=1, source_target_pairs={{0,8},{8,16},{16,24},{24,28},{28,20},{20,12},{12,4},{4,0},{1,5},{9... | collective-permute-start | bytes 1769480 | tf_op jit(solution)/shard_map/ppermute | solution.py:72
  40.9 67.8 %collective-permute-start.46 = (bf16[256,768]{1,0:T(8,128)(2,1)S(1)}, bf16[256,768]{1,0:T(8,128)(2,1)S(1)}, u32[]{:S(2)}, u32[]{:S(2)}) collective-permute-start(bf16[256,768]{1,0:T(8,128)(2,1)S(1)} %copy-done.73), channel_id=1, source_target_pairs={{0,2},{2,0},{1,3},{3,1},{4,6},{6,4},{5,7},{7,5},{8,10},{10,8},{9,1... | collective-permute-start | bytes 1179656 | tf_op jit(solution)/shard_map/ppermute | solution.py:26
  42.4 12.5 %collective-permute-start.18 = (bf16[96,3072]{1,0:T(8,128)(2,1)S(1)}, bf16[96,3072]{1,0:T(8,128)(2,1)S(1)}, u32[]{:S(2)}, u32[]{:S(2)}) collective-permute-start(bf16[96,3072]{1,0:T(8,128)(2,1)S(1)} %collective-permute-done.16), channel_id=1, source_target_pairs={{0,8},{8,16},{16,24},{24,28},{28,20},{20,12},{12,4},{4,0},{1,5},{9... | collective-permute-start | bytes 1769480 | tf_op jit(solution)/shard_map/ppermute | solution.py:72
  44.2 12.3 %collective-permute-start.17 = (bf16[96,3072]{1,0:T(8,128)(2,1)S(1)}, bf16[96,3072]{1,0:T(8,128)(2,1)S(1)}, u32[]{:S(2)}, u32[]{:S(2)}) collective-permute-start(bf16[96,3072]{1,0:T(8,128)(2,1)S(1)} %collective-permute-done.16), channel_id=1, source_target_pairs={{0,1},{1,0},{2,3},{3,2},{4,5},{5,4},{6,7},{7,6},{8,9},{9,8},{10,11... | collective-permute-start | bytes 1769480 | tf_op jit(solution)/shard_map/ppermute | solution.py:22
  49.7 39.6 %collective-permute-start.25 = (bf16[256,768]{1,0:T(8,128)(2,1)S(1)}, bf16[256,768]{1,0:T(8,128)(2,1)S(1)}, u32[]{:S(2)}, u32[]{:S(2)}) collective-permute-start(bf16[256,768]{1,0:T(8,128)(2,1)S(1)} %get-tuple-element.339.refs_1_), channel_id=1, source_target_pairs={{0,2},{2,0},{1,3},{3,1},{4,6},{6,4},{5,7},{7,5},{8,10},{10,8},{9,1... | collective-permute-start | bytes 1179656 | tf_op jit(solution)/shard_map/ppermute | solution.py:26
  56.5 11.5 %collective-permute-start.19 = (bf16[96,3072]{1,0:T(8,128)(2,1)S(1)}, bf16[96,3072]{1,0:T(8,128)(2,1)S(1)}, u32[]{:S(2)}, u32[]{:S(2)}) collective-permute-start(bf16[96,3072]{1,0:T(8,128)(2,1)S(1)} %collective-permute-done.18), channel_id=1, source_target_pairs={{0,1},{1,0},{2,3},{3,2},{4,5},{5,4},{6,7},{7,6},{8,9},{9,8},{10,11... | collective-permute-start | bytes 1769480 | tf_op jit(solution)/shard_map/ppermute | solution.py:22
  74.8 12.5 %collective-permute-start.28 = (bf16[96,1536]{1,0:T(8,128)(2,1)S(1)}, bf16[96,1536]{1,0:T(8,128)(2,1)S(1)}, u32[]{:S(2)}, u32[]{:S(2)}) collective-permute-start(bf16[96,1536]{1,0:T(8,128)(2,1)S(1)} %collective-permute-done.26), channel_id=1, source_target_pairs={{0,8},{8,16},{16,24},{24,28},{28,20},{20,12},{12,4},{4,0},{1,5},{9... | collective-permute-start | bytes 884744 | tf_op jit(solution)/shard_map/ppermute | solution.py:72
  78.7 14.1 %collective-permute-start.27 = (bf16[96,1536]{1,0:T(8,128)(2,1)S(1)}, bf16[96,1536]{1,0:T(8,128)(2,1)S(1)}, u32[]{:S(2)}, u32[]{:S(2)}) collective-permute-start(bf16[96,1536]{1,0:T(8,128)(2,1)S(1)} %collective-permute-done.26), channel_id=1, source_target_pairs={{0,1},{1,0},{2,3},{3,2},{4,5},{5,4},{6,7},{7,6},{8,9},{9,8},{10,11... | collective-permute-start | bytes 884744 | tf_op jit(solution)/shard_map/ppermute | solution.py:22
  85.8 12.1 %collective-permute-start.24 = (bf16[256,768]{1,0:T(8,128)(2,1)S(1)}, bf16[256,768]{1,0:T(8,128)(2,1)S(1)}, u32[]{:S(2)}, u32[]{:S(2)}) collective-permute-start(bf16[256,768]{1,0:T(8,128)(2,1)S(1)} %get-tuple-element.345.part_ref), channel_id=1, source_target_pairs={{0,2},{2,0},{1,3},{3,1},{4,6},{6,4},{5,7},{7,5},{8,10},{10,8},{9,1... | collective-permute-start | bytes 1179656 | tf_op jit(solution)/shard_map/ppermute | solution.py:26
  109.0 12.7 %collective-permute-start.40 = (bf16[96,3072]{1,0:T(8,128)(2,1)S(1)}, bf16[96,3072]{1,0:T(8,128)(2,1)S(1)}, u32[]{:S(2)}, u32[]{:S(2)}) collective-permute-start(bf16[96,3072]{1,0:T(8,128)(2,1)S(1)} %collective-permute-done.38), channel_id=1, source_target_pairs={{0,8},{8,16},{16,24},{24,28},{28,20},{20,12},{12,4},{4,0},{1,5},{9... | collective-permute-start | bytes 1769480 | tf_op jit(solution)/shard_map/ppermute | solution.py:72
  110.6 12.6 %collective-permute-start.39 = (bf16[96,3072]{1,0:T(8,128)(2,1)S(1)}, bf16[96,3072]{1,0:T(8,128)(2,1)S(1)}, u32[]{:S(2)}, u32[]{:S(2)}) collective-permute-start(bf16[96,3072]{1,0:T(8,128)(2,1)S(1)} %collective-permute-done.38), channel_id=1, source_target_pairs={{0,1},{1,0},{2,3},{3,2},{4,5},{5,4},{6,7},{7,6},{8,9},{9,8},{10,11... | collective-permute-start | bytes 1769480 | tf_op jit(solution)/shard_map/ppermute | solution.py:22
  115.5 30.6 %collective-permute-start.47 = (bf16[256,768]{1,0:T(8,128)(2,1)S(1)}, bf16[256,768]{1,0:T(8,128)(2,1)S(1)}, u32[]{:S(2)}, u32[]{:S(2)}) collective-permute-start(bf16[256,768]{1,0:T(8,128)(2,1)S(1)} %get-tuple-element.364.refs_1_), channel_id=1, source_target_pairs={{0,2},{2,0},{1,3},{3,1},{4,6},{6,4},{5,7},{7,5},{8,10},{10,8},{9,1... | collective-permute-start | bytes 1179656 | tf_op jit(solution)/shard_map/ppermute | solution.py:26
  121.2 19.1 %collective-permute-start.37 = (bf16[256,768]{1,0:T(8,128)(2,1)S(1)}, bf16[256,768]{1,0:T(8,128)(2,1)S(1)}, u32[]{:S(2)}, u32[]{:S(2)}) collective-permute-start(bf16[256,768]{1,0:T(8,128)(2,1)S(1)} %get-tuple-element.359.refs_1_), channel_id=1, source_target_pairs={{0,2},{2,0},{1,3},{3,1},{4,6},{6,4},{5,7},{7,5},{8,10},{10,8},{9,1... | collective-permute-start | bytes 1179656 | tf_op jit(solution)/shard_map/ppermute | solution.py:26
  167.6 11.9 %collective-permute-start.50 = (bf16[768,1536]{1,0:T(8,128)(2,1)}, bf16[768,1536]{1,0:T(8,128)(2,1)}, u32[]{:S(2)}, u32[]{:S(2)}) collective-permute-start(bf16[768,1536]{1,0:T(8,128)(2,1)} %get-tuple-element.389), channel_id=1, source_target_pairs={{0,1},{1,0},{2,3},{3,2},{4,5},{5,4},{6,7},{7,6},{8,9},{9,8},{10,11... | collective-permute-start | bytes 7077896 | tf_op jit(solution)/shard_map/ppermute | solution.py:22
  167.7 11.8 %collective-permute-start.48 = (bf16[256,768]{1,0:T(8,128)(2,1)}, bf16[256,768]{1,0:T(8,128)(2,1)}, u32[]{:S(2)}, u32[]{:S(2)}) collective-permute-start(bf16[256,768]{1,0:T(8,128)(2,1)} %get-tuple-element.399.part_ref), channel_id=1, source_target_pairs={{0,2},{2,0},{1,3},{3,1},{4,6},{6,4},{5,7},{7,5},{8,10},{10,8},{9,1... | collective-permute-start | bytes 1179656 | tf_op jit(solution)/shard_map/ppermute | solution.py:26
  205.5 12.1 %collective-permute-start.57 = (bf16[768,768]{1,0:T(8,128)(2,1)S(1)}, bf16[768,768]{1,0:T(8,128)(2,1)S(1)}, u32[]{:S(2)}, u32[]{:S(2)}) collective-permute-start(bf16[768,768]{1,0:T(8,128)(2,1)S(1)} %shard_map.340), channel_id=1, source_target_pairs={{0,1},{1,0},{2,3},{3,2},{4,5},{5,4},{6,7},{7,6},{8,9},{9,8},{10,11... | collective-permute-start | bytes 3538952 | tf_op jit(solution)/shard_map/ppermute | solution.py:22
  205.6 12.0 %collective-permute-start.56 = (bf16[256,768]{1,0:T(8,128)(2,1)S(1)}, bf16[256,768]{1,0:T(8,128)(2,1)S(1)}, u32[]{:S(2)}, u32[]{:S(2)}) collective-permute-start(bf16[256,768]{1,0:T(8,128)(2,1)S(1)} %get-tuple-element.419.part_ref), channel_id=1, source_target_pairs={{0,2},{2,0},{1,3},{3,1},{4,6},{6,4},{5,7},{7,5},{8,10},{10,8},{9,1... | collective-permute-start | bytes 1179656 | tf_op jit(solution)/shard_map/ppermute | solution.py:26
  209.2 18.3 %collective-permute-start.61 = (bf16[256,768]{1,0:T(8,128)(2,1)S(1)}, bf16[256,768]{1,0:T(8,128)(2,1)S(1)}, u32[]{:S(2)}, u32[]{:S(2)}) collective-permute-start(bf16[256,768]{1,0:T(8,128)(2,1)S(1)} %get-tuple-element.444.part_ref), channel_id=1, source_target_pairs={{0,2},{2,0},{1,3},{3,1},{4,6},{6,4},{5,7},{7,5},{8,10},{10,8},{9,1... | collective-permute-start | bytes 1179656 | tf_op jit(solution)/shard_map/ppermute | solution.py:26
  220.6 13.4 %collective-permute-start.64 = (bf16[48,768]{1,0:T(8,128)(2,1)S(1)}, bf16[48,768]{1,0:T(8,128)(2,1)S(1)}, u32[]{:S(2)}, u32[]{:S(2)}) collective-permute-start(bf16[48,768]{1,0:T(8,128)(2,1)S(1)} %get-tuple-element.453), channel_id=1, source_target_pairs={{0,8},{8,16},{16,24},{24,28},{28,20},{20,12},{12,4},{4,0},{1,9},{9... | collective-permute-start | bytes 221192 | tf_op jit(solution)/shard_map/ppermute | solution.py:75
  221.8 12.2 %collective-permute-start.65 = (bf16[48,768]{1,0:T(8,128)(2,1)S(1)}, bf16[48,768]{1,0:T(8,128)(2,1)S(1)}, u32[]{:S(2)}, u32[]{:S(2)}) collective-permute-start(bf16[48,768]{1,0:T(8,128)(2,1)S(1)} %get-tuple-element.454), channel_id=1, source_target_pairs={{0,4},{8,0},{16,8},{24,16},{28,24},{20,28},{12,20},{4,12},{1,5},{9... | collective-permute-start | bytes 221192 | tf_op jit(solution)/shard_map/ppermute | solution.py:75
  241.7 28.6 %collective-permute-start.71 = (bf16[768,1536]{1,0:T(8,128)(2,1)S(1)}, bf16[768,1536]{1,0:T(8,128)(2,1)S(1)}, u32[]{:S(2)}, u32[]{:S(2)}) collective-permute-start(bf16[768,1536]{1,0:T(8,128)(2,1)S(1)} %get-tuple-element.490), channel_id=1, source_target_pairs={{0,1},{1,0},{2,3},{3,2},{4,5},{5,4},{6,7},{7,6},{8,9},{9,8},{10,11... | collective-permute-start | bytes 7077896 | tf_op jit(solution)/shard_map/ppermute | solution.py:22
  241.8 12.0 %collective-permute-start.60 = (bf16[256,768]{1,0:T(8,128)(2,1)S(1)}, bf16[256,768]{1,0:T(8,128)(2,1)S(1)}, u32[]{:S(2)}, u32[]{:S(2)}) collective-permute-start(bf16[256,768]{1,0:T(8,128)(2,1)S(1)} %get-tuple-element.442.part_ref), channel_id=1, source_target_pairs={{0,2},{2,0},{1,3},{3,1},{4,6},{6,4},{5,7},{7,5},{8,10},{10,8},{9,1... | collective-permute-start | bytes 1179656 | tf_op jit(solution)/shard_map/ppermute | solution.py:26
  243.3 11.5 %collective-permute-start.66 = (bf16[96,1536]{1,0:T(8,128)(2,1)S(1)}, bf16[96,1536]{1,0:T(8,128)(2,1)S(1)}, u32[]{:S(2)}, u32[]{:S(2)}) collective-permute-start(bf16[96,1536]{1,0:T(8,128)(2,1)S(1)} %get-tuple-element.464), channel_id=1, source_target_pairs={{0,8},{8,16},{16,24},{24,28},{28,20},{20,12},{12,4},{4,0},{1,9},{9... | collective-permute-start | bytes 884744 | tf_op jit(solution)/shard_map/ppermute | solution.py:75
  244.4 11.4 %collective-permute-start.67 = (bf16[96,1536]{1,0:T(8,128)(2,1)S(1)}, bf16[96,1536]{1,0:T(8,128)(2,1)S(1)}, u32[]{:S(2)}, u32[]{:S(2)}) collective-permute-start(bf16[96,1536]{1,0:T(8,128)(2,1)S(1)} %get-tuple-element.465), channel_id=1, source_target_pairs={{0,4},{8,0},{16,8},{24,16},{28,24},{20,28},{12,20},{4,12},{1,5},{9... | collective-permute-start | bytes 884744 | tf_op jit(solution)/shard_map/ppermute | solution.py:75
  245.4 25.0 %collective-permute-start.70 = (bf16[256,768]{1,0:T(8,128)(2,1)S(1)}, bf16[256,768]{1,0:T(8,128)(2,1)S(1)}, u32[]{:S(2)}, u32[]{:S(2)}) collective-permute-start(bf16[256,768]{1,0:T(8,128)(2,1)S(1)} %get-tuple-element.488.part_ref), channel_id=1, source_target_pairs={{0,2},{2,0},{1,3},{3,1},{4,6},{6,4},{5,7},{7,5},{8,10},{10,8},{9,1... | collective-permute-start | bytes 1179656 | tf_op jit(solution)/shard_map/ppermute | solution.py:26
  287.0 13.3 %collective-permute-start.76 = (bf16[256,768]{1,0:T(8,128)(2,1)S(1)}, bf16[256,768]{1,0:T(8,128)(2,1)S(1)}, u32[]{:S(2)}, u32[]{:S(2)}) collective-permute-start(bf16[256,768]{1,0:T(8,128)(2,1)S(1)} %get-tuple-element.512), channel_id=1, source_target_pairs={{0,2},{2,0},{1,3},{3,1},{4,6},{6,4},{5,7},{7,5},{8,10},{10,8},{9,1... | collective-permute-start | bytes 1179656 | tf_op jit(solution)/shard_map/ppermute | solution.py:26
  303.3 23.7 %collective-permute-start.54 = (bf16[256,768]{1,0:T(8,128)(2,1)S(1)}, bf16[256,768]{1,0:T(8,128)(2,1)S(1)}, u32[]{:S(2)}, u32[]{:S(2)}) collective-permute-start(bf16[256,768]{1,0:T(8,128)(2,1)S(1)} %get-tuple-element.411), channel_id=1, source_target_pairs={{0,2},{2,0},{1,3},{3,1},{4,6},{6,4},{5,7},{7,5},{8,10},{10,8},{9,1... | collective-permute-start | bytes 1179656 | tf_op jit(solution)/shard_map/ppermute | solution.py:26
  308.1 15.7 %collective-permute-start.88 = (bf16[96,1536]{1,0:T(8,128)(2,1)S(1)}, bf16[96,1536]{1,0:T(8,128)(2,1)S(1)}, u32[]{:S(2)}, u32[]{:S(2)}) collective-permute-start(bf16[96,1536]{1,0:T(8,128)(2,1)S(1)} %get-tuple-element.560), channel_id=1, source_target_pairs={{0,8},{8,16},{16,24},{24,28},{28,20},{20,12},{12,4},{4,0},{1,9},{9... | collective-permute-start | bytes 884744 | tf_op jit(solution)/shard_map/ppermute | solution.py:75
  308.7 15.2 %collective-permute-start.89 = (bf16[96,1536]{1,0:T(8,128)(2,1)S(1)}, bf16[96,1536]{1,0:T(8,128)(2,1)S(1)}, u32[]{:S(2)}, u32[]{:S(2)}) collective-permute-start(bf16[96,1536]{1,0:T(8,128)(2,1)S(1)} %get-tuple-element.561), channel_id=1, source_target_pairs={{0,4},{8,0},{16,8},{24,16},{28,24},{20,28},{12,20},{4,12},{1,5},{9... | collective-permute-start | bytes 884744 | tf_op jit(solution)/shard_map/ppermute | solution.py:75
  325.0 13.2 %collective-permute-start.93 = (bf16[96,1536]{1,0:T(8,128)(2,1)S(1)}, bf16[96,1536]{1,0:T(8,128)(2,1)S(1)}, u32[]{:S(2)}, u32[]{:S(2)}) collective-permute-start(bf16[96,1536]{1,0:T(8,128)(2,1)S(1)} %get-tuple-element.576), channel_id=1, source_target_pairs={{0,8},{8,16},{16,24},{24,28},{28,20},{20,12},{12,4},{4,0},{1,9},{9... | collective-permute-start | bytes 884744 | tf_op jit(solution)/shard_map/ppermute | solution.py:75
  325.6 12.6 %collective-permute-start.94 = (bf16[96,1536]{1,0:T(8,128)(2,1)S(1)}, bf16[96,1536]{1,0:T(8,128)(2,1)S(1)}, u32[]{:S(2)}, u32[]{:S(2)}) collective-permute-start(bf16[96,1536]{1,0:T(8,128)(2,1)S(1)} %get-tuple-element.577), channel_id=1, source_target_pairs={{0,4},{8,0},{16,8},{24,16},{28,24},{20,28},{12,20},{4,12},{1,5},{9... | collective-permute-start | bytes 884744 | tf_op jit(solution)/shard_map/ppermute | solution.py:75
  (201 other events, 2416.3 us)

commit v2 on v1

--- a/solution.py
+++ b/solution.py
@@ -526,7 +526,7 @@
 
     return pl.pallas_call(
         kernel,
-        in_specs=[pl.BlockSpec(memory_space=pl.ANY)] * 4,
+        in_specs=[pl.BlockSpec(memory_space=pltpu.HBM)] * 4,
         out_specs=pl.BlockSpec(memory_space=pltpu.VMEM),
         out_shape=out((layers, rows, 4 * size)),
         scratch_shapes=[pltpu.VMEM(w.shape, LOW) for w in weights]
@@ -1268,9 +1268,10 @@
             arrived[0] = advance(arrived[0])
         else:
             results[0, "near"].step()
-            first_message = results[0, "near"].made[0]
-            results[0, "feed"].step(token=first_message)
-            arrived, _ = tie(arrived, first_message)
+            flight = results[0, "near"].flying[0] if ring.use else near_own
+            results[0, "near"].step(token=flight)
+            results[0, "feed"].step(token=results[0, "near"].made[0])
+            arrived, _ = tie(arrived, flight)
         if layer == last:
             denoised = last_rows(side, middles, here_rows, crossed, down_bias, layer)
     input_grad, sums = first_rows(side, part1, arrived, states, g_middles, first_gain)
@@ -1279,7 +1280,6 @@
     if ring.use:
         for move_by in exchanges(ring.count):
             total = total + move_by(total)
-            total = advance(total)
     else:
         total = lax.psum(total, ("fsdp", "tensor"))
     vectors = vector_outputs(place, total, layers, head_width)

time: 358 us -> 352 us (0.983)
  waiting for transfers between devices: 111 us -> 104 us
    ppermute x16, waiting for transfers between devices: 10.8 us -> 5.84 us  [send_both(): lax.ppermute(behind, 'fsdp', self.pairs[1])]
  transfers between devices with their start and end apart: 101 -> 101, of which waited for: 39 -> 36; matrix products, arithmetic and copies ran while one was open for 3% -> 3% of each run, Pallas kernels for 25% -> 25%
where the time goes in v2:
time: 352 us; the launch traced here: 347 us
  Pallas kernels  129 us (37%)
  waiting for transfers between devices  104 us (30%)
  starting transfers between devices  87.8 us (25%)
  local copies, waits for them, and re-layouts  23 us (7%)
  between operations  3.6 us (1%)
    pallas_call x57, Pallas kernels, kernel_call(): pl.pallas_call(kernel, in_specs=[word] * scalars + [inside] * (len(operan...  128 us
    ppermute x16, waiting for transfers between devices, split_send(): return lax.ppermute(value, ('fsdp', 'tensor'), self.split)  39.5 us
    ppermute x17, waiting for transfers between devices, swap_y(): return lax.ppermute(value, 'tensor', SWAP_Y)  36.8 us
    ppermute x16, starting transfers between devices, split_send(): return lax.ppermute(value, ('fsdp', 'tensor'), self.split)  26.2 us
    ppermute x17, starting transfers between devices, swap_y(): return lax.ppermute(value, 'tensor', SWAP_Y)  21.3 us
    ppermute x16, starting transfers between devices, send_both(): lax.ppermute(behind, 'fsdp', self.pairs[1])  17.1 us
    ppermute x16, starting transfers between devices, send_both(): lax.ppermute(ahead, 'fsdp', self.pairs[0])  16.6 us
    ppermute x16, waiting for transfers between devices, send_both(): lax.ppermute(ahead, 'fsdp', self.pairs[0])  11.4 us
  transfers between devices with their start and end apart: 101, of which 36 were waited for; matrix products, arithmetic and copies ran while one was open for 3% of the time, Pallas kernels for 25%

profile of v2, /device:TPU:0, one launch (start us, length us, event | category | flops | bytes accessed | tf_op | source)
XLA Modules:
  0.0 346.5 jit_solution(12341053469419928851)
XLA Ops:
  5.4 2.6 collective-permute-start
  12.5 2.7 collective-permute-done.2
  18.9 3.9 %collective-permute-done.5 = bf16[96,1536]{1,0:T(8,128)(2,1)S(1)} collective-permute-done((bf16[96,1536]{1,0:T(8,128)(2,1)}, bf16[96,1536]{1,0:T(8,128)(2,1)S(1)}, u32[]{:S(2)}, u32[]{:S(2)}) %collective-permute-start.5) | collective-permute-done | bytes 294944 | tf_op jit(solution)/shard_map/ppermute | solution.py:72
  25.3 4.2 %collective-permute-done.7 = bf16[96,1536]{1,0:T(8,128)(2,1)S(1)} collective-permute-done((bf16[96,1536]{1,0:T(8,128)(2,1)S(1)}, bf16[96,1536]{1,0:T(8,128)(2,1)S(1)}, u32[]{:S(2)}, u32[]{:S(2)}) %collective-permute-start.7) | collective-permute-done | bytes 294944 | tf_op jit(solution)/shard_map/ppermute | solution.py:72
  44.3 4.1 %shard_map.321 = (bf16[256,384]{1,0:T(8,128)(2,1)S(1)}, f32[8,256]{1,0:T(8,128)S(1)}, bf16[256,768]{1,0:T(8,128)(2,1)S(1)}) custom-call(bf16[256,384]{1,0:T(8,128)(2,1)S(1)} %get-tuple-element.298.q_ref, bf16[256,128]{1,0:T(8,128)(2,1)S(1)} %get-tuple-element.300.qm_ref, bf16[256,768]{1,0:T(8,128)(2,1)S(1)} %get-tuple-element.287.refs_0_, ...), custom_call_target="tpu_custom_call" | custom-call | flops 4000000000 | bytes 1024 | tf_op jit(solution)/shard_map/pallas_call | solution.py:199
  50.2 4.1 %shard_map.319 = (bf16[256,384]{1,0:T(8,128)(2,1)S(1)}, f32[8,256]{1,0:T(8,128)S(1)}, bf16[256,768]{1,0:T(8,128)(2,1)S(1)}) custom-call(bf16[256,384]{1,0:T(8,128)(2,1)S(1)} %get-tuple-element.284.q_ref, bf16[256,128]{1,0:T(8,128)(2,1)S(1)} %get-tuple-element.286.qm_ref, bf16[256,768]{1,0:T(8,128)(2,1)S(1)} %get-tuple-element.287.refs_0_, ...), custom_call_target="tpu_custom_call" | custom-call | flops 4000000000 | bytes 1024 | tf_op jit(solution)/shard_map/pallas_call | solution.py:199
  56.7 8.2 %collective-permute-done.20 = bf16[96,3072]{1,0:T(8,128)(2,1)S(1)} collective-permute-done((bf16[96,3072]{1,0:T(8,128)(2,1)S(1)}, bf16[96,3072]{1,0:T(8,128)(2,1)S(1)}, u32[]{:S(2)}, u32[]{:S(2)}) %collective-permute-start.20) | collective-permute-done | bytes 589856 | tf_op jit(solution)/shard_map/ppermute | solution.py:72
  68.2 3.4 collective-permute-done.22
  81.2 2.8 shard_map.322
  89.3 2.8 shard_map.323
  105.8 2.8 shard_map.324
  110.8 4.1 %shard_map.327 = (bf16[256,384]{1,0:T(8,128)(2,1)S(1)}, f32[8,256]{1,0:T(8,128)S(1)}, bf16[256,768]{1,0:T(8,128)(2,1)S(1)}) custom-call(bf16[256,384]{1,0:T(8,128)(2,1)S(1)} %get-tuple-element.324.q_ref, bf16[256,128]{1,0:T(8,128)(2,1)S(1)} %get-tuple-element.300.qm_ref, bf16[256,768]{1,0:T(8,128)(2,1)S(1)} %get-tuple-element.317.refs_0_, ...), custom_call_target="tpu_custom_call" | custom-call | flops 4000000000 | bytes 1024 | tf_op jit(solution)/shard_map/pallas_call | solution.py:199
  117.0 4.1 %shard_map.326 = (bf16[256,384]{1,0:T(8,128)(2,1)S(1)}, f32[8,256]{1,0:T(8,128)S(1)}, bf16[256,768]{1,0:T(8,128)(2,1)S(1)}) custom-call(bf16[256,384]{1,0:T(8,128)(2,1)S(1)} %get-tuple-element.316.q_ref, bf16[256,128]{1,0:T(8,128)(2,1)S(1)} %get-tuple-element.286.qm_ref, bf16[256,768]{1,0:T(8,128)(2,1)S(1)} %get-tuple-element.317.refs_0_, ...), custom_call_target="tpu_custom_call" | custom-call | flops 4000000000 | bytes 1024 | tf_op jit(solution)/shard_map/pallas_call | solution.py:199
  123.4 8.2 %collective-permute-done.42 = bf16[96,3072]{1,0:T(8,128)(2,1)S(1)} collective-permute-done((bf16[96,3072]{1,0:T(8,128)(2,1)S(1)}, bf16[96,3072]{1,0:T(8,128)(2,1)S(1)}, u32[]{:S(2)}, u32[]{:S(2)}) %collective-permute-start.42) | collective-permute-done | bytes 589856 | tf_op jit(solution)/shard_map/ppermute | solution.py:72
  133.5 5.1 %collective-permute-done.44 = bf16[48,3072]{1,0:T(8,128)(2,1)S(1)} collective-permute-done((bf16[48,3072]{1,0:T(8,128)(2,1)S(1)}, bf16[48,3072]{1,0:T(8,128)(2,1)S(1)}, u32[]{:S(2)}, u32[]{:S(2)}) %collective-permute-start.44) | collective-permute-done | bytes 294944 | tf_op jit(solution)/shard_map/ppermute | solution.py:72
  140.2 3.7 %shard_map.329 = (f32[256,768]{1,0:T(8,128)S(1)}, bf16[256,768]{1,0:T(8,128)(2,1)S(1)}, bf16[256,1536]{1,0:T(8,128)(2,1)S(1)}, bf16[256,1536]{1,0:T(8,128)(2,1)S...) custom-call(f32[256,768]{1,0:T(8,128)S(1)} %get-tuple-element.315.refs_0_.state_ref, ...), custom_call_target="tpu_custom_call" | custom-call | flops 4000000000 | bytes 1024 | tf_op jit(solution)/shard_map/pallas_call | solution.py:199
  146.1 4.5 %shard_map.330 = (f32[256,768]{1,0:T(8,128)S(1)}, bf16[256,768]{1,0:T(8,128)(2,1)S(1)}, bf16[256,1536]{1,0:T(8,128)(2,1)S(1)}, bf16[256,1536]{1,0:T(8,128)(2,1)S...) custom-call(f32[256,768]{1,0:T(8,128)S(1)} %get-tuple-element.334.refs_0_.state_ref, ...), custom_call_target="tpu_custom_call" | custom-call | flops 4000000000 | bytes 1024 | tf_op jit(solution)/shard_map/pallas_call | solution.py:199
  151.4 4.3 %collective-permute-done.49.arrived_ref = bf16[256,768]{1,0:T(8,128)(2,1)S(1)} collective-permute-done((bf16[256,768]{1,0:T(8,128)(2,1)S(1)}, bf16[256,768]{1,0:T(8,128)(2,1)S(1)}, u32[]{:S(2)}, u32[]{:S(2)}) %collective-permute-start.49) | collective-permute-done | bytes 393248 | tf_op jit(solution)/shard_map/ppermute | solution.py:26
  155.8 7.5 %shard_map.331 = (f32[256,768]{1,0:T(8,128)S(1)}, bf16[256,768]{1,0:T(8,128)(2,1)S(1)}, f32[8,768]{1,0:T(8,128)S(1)}, bf16[256,384]{1,0:T(8,128)(2,1)S(1)}, bf16...) custom-call(bf16[256,768]{1,0:T(8,128)(2,1)S(1)} %get-tuple-element.332.refs_8_.grads_ref.l0, ...), custom_call_target="tpu_custom_call" | custom-call | flops 1000000000 | bytes 1024 | tf_op jit(solution)/shard_map/pallas_call | solution.py:199
  163.5 4.1 %shard_map.332 = (bf16[768,1536]{1,0:T(8,128)(2,1)}, bf16[768,1536]{1,0:T(8,128)(2,1)S(1)}) custom-call(s32[1]{0:T(128)} %bitcast.1.core_ref, bf16[256,768]{1,0:T(8,128)(2,1)S(1)} %get-tuple-element.340.s0, bf16[256,768]{1,0:T(8,128)(2,1)S(1)} %get-tuple-element.341.s1, bf16[256,1536]{1,0:T(8,128)(2,1)S(1)} %get-tuple-element.348.g0, ...), custom_call_target="tpu_custom_call" | custom-call | flops 3400000000 | bytes 1024 | tf_op jit(solution)/shard_map/pallas_call | solution.py:199
  169.3 10.2 %collective-permute-done.48.arrived_ref = bf16[256,768]{1,0:T(8,128)(2,1)} collective-permute-done((bf16[256,768]{1,0:T(8,128)(2,1)}, bf16[256,768]{1,0:T(8,128)(2,1)}, u32[]{:S(2)}, u32[]{:S(2)}) %collective-permute-start.48) | collective-permute-done | bytes 393248 | tf_op jit(solution)/shard_map/ppermute | solution.py:26
  182.0 9.0 %shard_map.335 = (f32[256,768]{1,0:T(8,128)S(1)}, bf16[256,768]{1,0:T(8,128)(2,1)S(1)}, f32[8,768]{1,0:T(8,128)S(1)}, bf16[256,384]{1,0:T(8,128)(2,1)S(1)}, bf16...) custom-call(bf16[256,768]{1,0:T(8,128)(2,1)S(1)} %copy-done.40, bf16[256,768]{1,0:T(8,128)(2,1)} %get-tuple-element.361.part_ref, ...), custom_call_target="tpu_custom_call" | custom-call | flops 1000000000 | bytes 1024 | tf_op jit(solution)/shard_map/pallas_call | solution.py:199
  201.0 2.8 shard_map.338
  211.3 6.2 %collective-permute-done.56.arrived_ref = bf16[256,768]{1,0:T(8,128)(2,1)S(1)} collective-permute-done((bf16[256,768]{1,0:T(8,128)(2,1)S(1)}, bf16[256,768]{1,0:T(8,128)(2,1)S(1)}, u32[]{:S(2)}, u32[]{:S(2)}) %collective-permute-start.56) | collective-permute-done | bytes 393248 | tf_op jit(solution)/shard_map/ppermute | solution.py:26
  224.9 2.6 shard_map.343
  227.5 3.6 %collective-permute-done.62.refs_0_ = bf16[96,1536]{1,0:T(8,128)(2,1)S(1)} collective-permute-done((bf16[96,1536]{1,0:T(8,128)(2,1)S(1)}, bf16[96,1536]{1,0:T(8,128)(2,1)S(1)}, u32[]{:S(2)}, u32[]{:S(2)}) %collective-permute-start.62) | collective-permute-done | bytes 294944 | tf_op jit(solution)/shard_map/ppermute | solution.py:75
  235.5 2.6 shard_map.346
  238.2 3.5 %shard_map.348 = (bf16[768,1536]{1,0:T(8,128)(2,1)S(1)}, bf16[768,1536]{1,0:T(8,128)(2,1)S(1)}) custom-call(s32[1]{0:T(128)} %bitcast.1.core_ref, bf16[256,768]{1,0:T(8,128)(2,1)S(1)} %copy-done.118, bf16[256,768]{1,0:T(8,128)(2,1)S(1)} %copy-done.120, bf16[256,1536]{1,0:T(8,128)(2,1)S(1)} %get-tuple-element.439.g0, ...), custom_call_target="tpu_custom_call" | custom-call | flops 3400000000 | bytes 1024 | tf_op jit(solution)/shard_map/pallas_call | solution.py:199
  245.9 7.9 %collective-permute-done.60.arrived_ref = bf16[256,768]{1,0:T(8,128)(2,1)S(1)} collective-permute-done((bf16[256,768]{1,0:T(8,128)(2,1)S(1)}, bf16[256,768]{1,0:T(8,128)(2,1)S(1)}, u32[]{:S(2)}, u32[]{:S(2)}) %collective-permute-start.60) | collective-permute-done | bytes 393248 | tf_op jit(solution)/shard_map/ppermute | solution.py:26
  255.8 3.1 collective-permute-done.68.refs_0_
  263.8 6.5 %shard_map.349 = (f32[256,768]{1,0:T(8,128)S(1)}, bf16[256,768]{1,0:T(8,128)(2,1)S(1)}, f32[8,768]{1,0:T(8,128)S(1)}, bf16[256,384]{1,0:T(8,128)(2,1)S(1)}, bf16...) custom-call(f32[256,768]{1,0:T(8,128)S(1)} %get-tuple-element.403.grads_ref, ...), custom_call_target="tpu_custom_call" | custom-call | flops 1000000000 | bytes 1024 | tf_op jit(solution)/shard_map/pallas_call | solution.py:199
  273.3 6.7 %shard_map.352 = (f32[256,768]{1,0:T(8,128)S(1)}, bf16[256,768]{1,0:T(8,128)(2,1)S(1)}, f32[8,768]{1,0:T(8,128)S(1)}, bf16[256,384]{1,0:T(8,128)(2,1)S(1)}, bf16...) custom-call(f32[256,768]{1,0:T(8,128)S(1)} %get-tuple-element.449.grads_ref, ...), custom_call_target="tpu_custom_call" | custom-call | flops 1000000000 | bytes 1024 | tf_op jit(solution)/shard_map/pallas_call | solution.py:199
  (544 shorter events, 191.2 us)
Async XLA Ops:
  5.4 30.7 %collective-permute-start = (bf16[256,768]{1,0:T(8,128)(2,1)}, bf16[256,768]{1,0:T(8,128)(2,1)S(1)}, u32[]{:S(2)}, u32[]{:S(2)}) collective-permute-start(bf16[256,768]{1,0:T(8,128)(2,1)} %own_ref.1), channel_id=1, source_target_pairs={{0,2},{2,0},{1,3},{3,1},{4,6},{6,4},{5,7},{7,5},{8,10},{10,8},{9,1... | collective-permute-start | bytes 1179656 | tf_op jit(solution)/shard_map/ppermute | solution.py:26
  31.1 11.3 %collective-permute-start.16 = (bf16[96,3072]{1,0:T(8,128)(2,1)S(1)}, bf16[96,3072]{1,0:T(8,128)(2,1)S(1)}, u32[]{:S(2)}, u32[]{:S(2)}) collective-permute-start(bf16[96,3072]{1,0:T(8,128)(2,1)S(1)} %get-tuple-element.297), channel_id=1, source_target_pairs={{0,8},{8,16},{16,24},{24,28},{28,20},{20,12},{12,4},{4,0},{1,5},{9... | collective-permute-start | bytes 1769480 | tf_op jit(solution)/shard_map/ppermute | solution.py:72
  40.9 67.8 %collective-permute-start.46 = (bf16[256,768]{1,0:T(8,128)(2,1)S(1)}, bf16[256,768]{1,0:T(8,128)(2,1)S(1)}, u32[]{:S(2)}, u32[]{:S(2)}) collective-permute-start(bf16[256,768]{1,0:T(8,128)(2,1)S(1)} %copy-done.73), channel_id=1, source_target_pairs={{0,2},{2,0},{1,3},{3,1},{4,6},{6,4},{5,7},{7,5},{8,10},{10,8},{9,1... | collective-permute-start | bytes 1179656 | tf_op jit(solution)/shard_map/ppermute | solution.py:26
  42.4 12.5 %collective-permute-start.18 = (bf16[96,3072]{1,0:T(8,128)(2,1)S(1)}, bf16[96,3072]{1,0:T(8,128)(2,1)S(1)}, u32[]{:S(2)}, u32[]{:S(2)}) collective-permute-start(bf16[96,3072]{1,0:T(8,128)(2,1)S(1)} %collective-permute-done.16), channel_id=1, source_target_pairs={{0,8},{8,16},{16,24},{24,28},{28,20},{20,12},{12,4},{4,0},{1,5},{9... | collective-permute-start | bytes 1769480 | tf_op jit(solution)/shard_map/ppermute | solution.py:72
  44.2 12.3 %collective-permute-start.17 = (bf16[96,3072]{1,0:T(8,128)(2,1)S(1)}, bf16[96,3072]{1,0:T(8,128)(2,1)S(1)}, u32[]{:S(2)}, u32[]{:S(2)}) collective-permute-start(bf16[96,3072]{1,0:T(8,128)(2,1)S(1)} %collective-permute-done.16), channel_id=1, source_target_pairs={{0,1},{1,0},{2,3},{3,2},{4,5},{5,4},{6,7},{7,6},{8,9},{9,8},{10,11... | collective-permute-start | bytes 1769480 | tf_op jit(solution)/shard_map/ppermute | solution.py:22
  49.7 39.6 %collective-permute-start.25 = (bf16[256,768]{1,0:T(8,128)(2,1)S(1)}, bf16[256,768]{1,0:T(8,128)(2,1)S(1)}, u32[]{:S(2)}, u32[]{:S(2)}) collective-permute-start(bf16[256,768]{1,0:T(8,128)(2,1)S(1)} %get-tuple-element.301.refs_1_), channel_id=1, source_target_pairs={{0,2},{2,0},{1,3},{3,1},{4,6},{6,4},{5,7},{7,5},{8,10},{10,8},{9,1... | collective-permute-start | bytes 1179656 | tf_op jit(solution)/shard_map/ppermute | solution.py:26
  56.5 11.5 %collective-permute-start.19 = (bf16[96,3072]{1,0:T(8,128)(2,1)S(1)}, bf16[96,3072]{1,0:T(8,128)(2,1)S(1)}, u32[]{:S(2)}, u32[]{:S(2)}) collective-permute-start(bf16[96,3072]{1,0:T(8,128)(2,1)S(1)} %collective-permute-done.18), channel_id=1, source_target_pairs={{0,1},{1,0},{2,3},{3,2},{4,5},{5,4},{6,7},{7,6},{8,9},{9,8},{10,11... | collective-permute-start | bytes 1769480 | tf_op jit(solution)/shard_map/ppermute | solution.py:22
  74.8 12.5 %collective-permute-start.28 = (bf16[96,1536]{1,0:T(8,128)(2,1)S(1)}, bf16[96,1536]{1,0:T(8,128)(2,1)S(1)}, u32[]{:S(2)}, u32[]{:S(2)}) collective-permute-start(bf16[96,1536]{1,0:T(8,128)(2,1)S(1)} %collective-permute-done.26), channel_id=1, source_target_pairs={{0,8},{8,16},{16,24},{24,28},{28,20},{20,12},{12,4},{4,0},{1,5},{9... | collective-permute-start | bytes 884744 | tf_op jit(solution)/shard_map/ppermute | solution.py:72
  78.7 14.1 %collective-permute-start.27 = (bf16[96,1536]{1,0:T(8,128)(2,1)S(1)}, bf16[96,1536]{1,0:T(8,128)(2,1)S(1)}, u32[]{:S(2)}, u32[]{:S(2)}) collective-permute-start(bf16[96,1536]{1,0:T(8,128)(2,1)S(1)} %collective-permute-done.26), channel_id=1, source_target_pairs={{0,1},{1,0},{2,3},{3,2},{4,5},{5,4},{6,7},{7,6},{8,9},{9,8},{10,11... | collective-permute-start | bytes 884744 | tf_op jit(solution)/shard_map/ppermute | solution.py:22
  85.8 12.1 %collective-permute-start.24 = (bf16[256,768]{1,0:T(8,128)(2,1)S(1)}, bf16[256,768]{1,0:T(8,128)(2,1)S(1)}, u32[]{:S(2)}, u32[]{:S(2)}) collective-permute-start(bf16[256,768]{1,0:T(8,128)(2,1)S(1)} %get-tuple-element.307.part_ref), channel_id=1, source_target_pairs={{0,2},{2,0},{1,3},{3,1},{4,6},{6,4},{5,7},{7,5},{8,10},{10,8},{9,1... | collective-permute-start | bytes 1179656 | tf_op jit(solution)/shard_map/ppermute | solution.py:26
  97.8 11.2 %collective-permute-start.38 = (bf16[96,3072]{1,0:T(8,128)(2,1)S(1)}, bf16[96,3072]{1,0:T(8,128)(2,1)S(1)}, u32[]{:S(2)}, u32[]{:S(2)}) collective-permute-start(bf16[96,3072]{1,0:T(8,128)(2,1)S(1)} %get-tuple-element.323), channel_id=1, source_target_pairs={{0,8},{8,16},{16,24},{24,28},{28,20},{20,12},{12,4},{4,0},{1,5},{9... | collective-permute-start | bytes 1769480 | tf_op jit(solution)/shard_map/ppermute | solution.py:72
  109.0 12.7 %collective-permute-start.40 = (bf16[96,3072]{1,0:T(8,128)(2,1)S(1)}, bf16[96,3072]{1,0:T(8,128)(2,1)S(1)}, u32[]{:S(2)}, u32[]{:S(2)}) collective-permute-start(bf16[96,3072]{1,0:T(8,128)(2,1)S(1)} %collective-permute-done.38), channel_id=1, source_target_pairs={{0,8},{8,16},{16,24},{24,28},{28,20},{20,12},{12,4},{4,0},{1,5},{9... | collective-permute-start | bytes 1769480 | tf_op jit(solution)/shard_map/ppermute | solution.py:72
  110.6 12.6 %collective-permute-start.39 = (bf16[96,3072]{1,0:T(8,128)(2,1)S(1)}, bf16[96,3072]{1,0:T(8,128)(2,1)S(1)}, u32[]{:S(2)}, u32[]{:S(2)}) collective-permute-start(bf16[96,3072]{1,0:T(8,128)(2,1)S(1)} %collective-permute-done.38), channel_id=1, source_target_pairs={{0,1},{1,0},{2,3},{3,2},{4,5},{5,4},{6,7},{7,6},{8,9},{9,8},{10,11... | collective-permute-start | bytes 1769480 | tf_op jit(solution)/shard_map/ppermute | solution.py:22
  115.5 30.6 %collective-permute-start.47 = (bf16[256,768]{1,0:T(8,128)(2,1)S(1)}, bf16[256,768]{1,0:T(8,128)(2,1)S(1)}, u32[]{:S(2)}, u32[]{:S(2)}) collective-permute-start(bf16[256,768]{1,0:T(8,128)(2,1)S(1)} %get-tuple-element.326.refs_1_), channel_id=1, source_target_pairs={{0,2},{2,0},{1,3},{3,1},{4,6},{6,4},{5,7},{7,5},{8,10},{10,8},{9,1... | collective-permute-start | bytes 1179656 | tf_op jit(solution)/shard_map/ppermute | solution.py:26
  121.2 19.1 %collective-permute-start.37 = (bf16[256,768]{1,0:T(8,128)(2,1)S(1)}, bf16[256,768]{1,0:T(8,128)(2,1)S(1)}, u32[]{:S(2)}, u32[]{:S(2)}) collective-permute-start(bf16[256,768]{1,0:T(8,128)(2,1)S(1)} %get-tuple-element.321.refs_1_), channel_id=1, source_target_pairs={{0,2},{2,0},{1,3},{3,1},{4,6},{6,4},{5,7},{7,5},{8,10},{10,8},{9,1... | collective-permute-start | bytes 1179656 | tf_op jit(solution)/shard_map/ppermute | solution.py:26
  144.6 11.2 %collective-permute-start.49 = (bf16[256,768]{1,0:T(8,128)(2,1)S(1)}, bf16[256,768]{1,0:T(8,128)(2,1)S(1)}, u32[]{:S(2)}, u32[]{:S(2)}) collective-permute-start(bf16[256,768]{1,0:T(8,128)(2,1)S(1)} %get-tuple-element.344.part_ref), channel_id=1, source_target_pairs={{0,2},{2,0},{1,3},{3,1},{4,6},{6,4},{5,7},{7,5},{8,10},{10,8},{9,1... | collective-permute-start | bytes 1179656 | tf_op jit(solution)/shard_map/ppermute | solution.py:26
  167.6 11.9 %collective-permute-start.50 = (bf16[768,1536]{1,0:T(8,128)(2,1)}, bf16[768,1536]{1,0:T(8,128)(2,1)}, u32[]{:S(2)}, u32[]{:S(2)}) collective-permute-start(bf16[768,1536]{1,0:T(8,128)(2,1)} %get-tuple-element.351), channel_id=1, source_target_pairs={{0,1},{1,0},{2,3},{3,2},{4,5},{5,4},{6,7},{7,6},{8,9},{9,8},{10,11... | collective-permute-start | bytes 7077896 | tf_op jit(solution)/shard_map/ppermute | solution.py:22
  167.7 11.8 %collective-permute-start.48 = (bf16[256,768]{1,0:T(8,128)(2,1)}, bf16[256,768]{1,0:T(8,128)(2,1)}, u32[]{:S(2)}, u32[]{:S(2)}) collective-permute-start(bf16[256,768]{1,0:T(8,128)(2,1)} %get-tuple-element.361.part_ref), channel_id=1, source_target_pairs={{0,2},{2,0},{1,3},{3,1},{4,6},{6,4},{5,7},{7,5},{8,10},{10,8},{9,1... | collective-permute-start | bytes 1179656 | tf_op jit(solution)/shard_map/ppermute | solution.py:26
  205.5 12.1 %collective-permute-start.57 = (bf16[768,768]{1,0:T(8,128)(2,1)S(1)}, bf16[768,768]{1,0:T(8,128)(2,1)S(1)}, u32[]{:S(2)}, u32[]{:S(2)}) collective-permute-start(bf16[768,768]{1,0:T(8,128)(2,1)S(1)} %shard_map.340), channel_id=1, source_target_pairs={{0,1},{1,0},{2,3},{3,2},{4,5},{5,4},{6,7},{7,6},{8,9},{9,8},{10,11... | collective-permute-start | bytes 3538952 | tf_op jit(solution)/shard_map/ppermute | solution.py:22
  205.6 12.0 %collective-permute-start.56 = (bf16[256,768]{1,0:T(8,128)(2,1)S(1)}, bf16[256,768]{1,0:T(8,128)(2,1)S(1)}, u32[]{:S(2)}, u32[]{:S(2)}) collective-permute-start(bf16[256,768]{1,0:T(8,128)(2,1)S(1)} %get-tuple-element.381.part_ref), channel_id=1, source_target_pairs={{0,2},{2,0},{1,3},{3,1},{4,6},{6,4},{5,7},{7,5},{8,10},{10,8},{9,1... | collective-permute-start | bytes 1179656 | tf_op jit(solution)/shard_map/ppermute | solution.py:26
  209.2 18.3 %collective-permute-start.61 = (bf16[256,768]{1,0:T(8,128)(2,1)S(1)}, bf16[256,768]{1,0:T(8,128)(2,1)S(1)}, u32[]{:S(2)}, u32[]{:S(2)}) collective-permute-start(bf16[256,768]{1,0:T(8,128)(2,1)S(1)} %get-tuple-element.406.part_ref), channel_id=1, source_target_pairs={{0,2},{2,0},{1,3},{3,1},{4,6},{6,4},{5,7},{7,5},{8,10},{10,8},{9,1... | collective-permute-start | bytes 1179656 | tf_op jit(solution)/shard_map/ppermute | solution.py:26
  220.6 13.4 %collective-permute-start.64 = (bf16[48,768]{1,0:T(8,128)(2,1)S(1)}, bf16[48,768]{1,0:T(8,128)(2,1)S(1)}, u32[]{:S(2)}, u32[]{:S(2)}) collective-permute-start(bf16[48,768]{1,0:T(8,128)(2,1)S(1)} %get-tuple-element.415), channel_id=1, source_target_pairs={{0,8},{8,16},{16,24},{24,28},{28,20},{20,12},{12,4},{4,0},{1,9},{9... | collective-permute-start | bytes 221192 | tf_op jit(solution)/shard_map/ppermute | solution.py:75
  221.8 12.2 %collective-permute-start.65 = (bf16[48,768]{1,0:T(8,128)(2,1)S(1)}, bf16[48,768]{1,0:T(8,128)(2,1)S(1)}, u32[]{:S(2)}, u32[]{:S(2)}) collective-permute-start(bf16[48,768]{1,0:T(8,128)(2,1)S(1)} %get-tuple-element.416), channel_id=1, source_target_pairs={{0,4},{8,0},{16,8},{24,16},{28,24},{20,28},{12,20},{4,12},{1,5},{9... | collective-permute-start | bytes 221192 | tf_op jit(solution)/shard_map/ppermute | solution.py:75
  241.7 28.6 %collective-permute-start.71 = (bf16[768,1536]{1,0:T(8,128)(2,1)S(1)}, bf16[768,1536]{1,0:T(8,128)(2,1)S(1)}, u32[]{:S(2)}, u32[]{:S(2)}) collective-permute-start(bf16[768,1536]{1,0:T(8,128)(2,1)S(1)} %get-tuple-element.452), channel_id=1, source_target_pairs={{0,1},{1,0},{2,3},{3,2},{4,5},{5,4},{6,7},{7,6},{8,9},{9,8},{10,11... | collective-permute-start | bytes 7077896 | tf_op jit(solution)/shard_map/ppermute | solution.py:22
  241.8 12.0 %collective-permute-start.60 = (bf16[256,768]{1,0:T(8,128)(2,1)S(1)}, bf16[256,768]{1,0:T(8,128)(2,1)S(1)}, u32[]{:S(2)}, u32[]{:S(2)}) collective-permute-start(bf16[256,768]{1,0:T(8,128)(2,1)S(1)} %get-tuple-element.404.part_ref), channel_id=1, source_target_pairs={{0,2},{2,0},{1,3},{3,1},{4,6},{6,4},{5,7},{7,5},{8,10},{10,8},{9,1... | collective-permute-start | bytes 1179656 | tf_op jit(solution)/shard_map/ppermute | solution.py:26
  243.3 11.5 %collective-permute-start.66 = (bf16[96,1536]{1,0:T(8,128)(2,1)S(1)}, bf16[96,1536]{1,0:T(8,128)(2,1)S(1)}, u32[]{:S(2)}, u32[]{:S(2)}) collective-permute-start(bf16[96,1536]{1,0:T(8,128)(2,1)S(1)} %get-tuple-element.426), channel_id=1, source_target_pairs={{0,8},{8,16},{16,24},{24,28},{28,20},{20,12},{12,4},{4,0},{1,9},{9... | collective-permute-start | bytes 884744 | tf_op jit(solution)/shard_map/ppermute | solution.py:75
  244.4 11.4 %collective-permute-start.67 = (bf16[96,1536]{1,0:T(8,128)(2,1)S(1)}, bf16[96,1536]{1,0:T(8,128)(2,1)S(1)}, u32[]{:S(2)}, u32[]{:S(2)}) collective-permute-start(bf16[96,1536]{1,0:T(8,128)(2,1)S(1)} %get-tuple-element.427), channel_id=1, source_target_pairs={{0,4},{8,0},{16,8},{24,16},{28,24},{20,28},{12,20},{4,12},{1,5},{9... | collective-permute-start | bytes 884744 | tf_op jit(solution)/shard_map/ppermute | solution.py:75
  245.4 24.9 %collective-permute-start.70 = (bf16[256,768]{1,0:T(8,128)(2,1)S(1)}, bf16[256,768]{1,0:T(8,128)(2,1)S(1)}, u32[]{:S(2)}, u32[]{:S(2)}) collective-permute-start(bf16[256,768]{1,0:T(8,128)(2,1)S(1)} %get-tuple-element.450.part_ref), channel_id=1, source_target_pairs={{0,2},{2,0},{1,3},{3,1},{4,6},{6,4},{5,7},{7,5},{8,10},{10,8},{9,1... | collective-permute-start | bytes 1179656 | tf_op jit(solution)/shard_map/ppermute | solution.py:26
  287.0 12.0 %collective-permute-start.76 = (bf16[256,768]{1,0:T(8,128)(2,1)S(1)}, bf16[256,768]{1,0:T(8,128)(2,1)S(1)}, u32[]{:S(2)}, u32[]{:S(2)}) collective-permute-start(bf16[256,768]{1,0:T(8,128)(2,1)S(1)} %get-tuple-element.474), channel_id=1, source_target_pairs={{0,2},{2,0},{1,3},{3,1},{4,6},{6,4},{5,7},{7,5},{8,10},{10,8},{9,1... | collective-permute-start | bytes 1179656 | tf_op jit(solution)/shard_map/ppermute | solution.py:26
  296.0 24.0 %collective-permute-start.54 = (bf16[256,768]{1,0:T(8,128)(2,1)S(1)}, bf16[256,768]{1,0:T(8,128)(2,1)S(1)}, u32[]{:S(2)}, u32[]{:S(2)}) collective-permute-start(bf16[256,768]{1,0:T(8,128)(2,1)S(1)} %get-tuple-element.373), channel_id=1, source_target_pairs={{0,2},{2,0},{1,3},{3,1},{4,6},{6,4},{5,7},{7,5},{8,10},{10,8},{9,1... | collective-permute-start | bytes 1179656 | tf_op jit(solution)/shard_map/ppermute | solution.py:26
  314.5 17.5 %collective-permute-start.92 = (bf16[96,1536]{1,0:T(8,128)(2,1)S(1)}, bf16[96,1536]{1,0:T(8,128)(2,1)S(1)}, u32[]{:S(2)}, u32[]{:S(2)}) collective-permute-start(bf16[96,1536]{1,0:T(8,128)(2,1)S(1)} %get-tuple-element.506), channel_id=1, source_target_pairs={{0,8},{8,16},{16,24},{24,28},{28,20},{20,12},{12,4},{4,0},{1,9},{9... | collective-permute-start | bytes 884744 | tf_op jit(solution)/shard_map/ppermute | solution.py:75
  315.6 17.1 %collective-permute-start.93 = (bf16[96,1536]{1,0:T(8,128)(2,1)S(1)}, bf16[96,1536]{1,0:T(8,128)(2,1)S(1)}, u32[]{:S(2)}, u32[]{:S(2)}) collective-permute-start(bf16[96,1536]{1,0:T(8,128)(2,1)S(1)} %get-tuple-element.507), channel_id=1, source_target_pairs={{0,4},{8,0},{16,8},{24,16},{28,24},{20,28},{12,20},{4,12},{1,5},{9... | collective-permute-start | bytes 884744 | tf_op jit(solution)/shard_map/ppermute | solution.py:75
  (201 other events, 2412.9 us)

commit v3 on v2

--- a/solution.py
+++ b/solution.py
@@ -1247,7 +1247,6 @@
         ]
         aways = [swap_core(away) for away in aways]
         if layer == last:
-            aways[1] = advance(aways[1])
             aways[1], away_rows = tie(aways[1], away_rows)
             crossed = swap_y(away_rows)
         g_qkv, part0, part1, sums = project_back(side, dqs, owns, aways, w_near, layer == 0)

time: 352 us -> 346 us (0.983)
  waiting for transfers between devices: 104 us -> 98.2 us
    ppermute x16, waiting for transfers between devices: 11.4 us -> 6.23 us  [send_both(): lax.ppermute(ahead, 'fsdp', self.pairs[0])]
    ppermute x16, starting transfers between devices: 17.1 us -> 13.4 us  [send_both(): lax.ppermute(behind, 'fsdp', self.pairs[1])]
  transfers between devices with their start and end apart: 101 -> 101, of which waited for: 36 -> 34; matrix products, arithmetic and copies ran while one was open for 3% -> 3% of each run, Pallas kernels for 25% -> 25%
where the time goes in v3:
time: 346 us; the launch traced here: 341 us
  Pallas kernels  128 us (37%)
  waiting for transfers between devices  98.2 us (28%)
  starting transfers between devices  87.7 us (25%)
  local copies, waits for them, and re-layouts  23 us (7%)
  between operations  3.5 us (1%)
    pallas_call x57, Pallas kernels, kernel_call(): pl.pallas_call(kernel, in_specs=[word] * scalars + [inside] * (len(operan...  128 us
    ppermute x16, waiting for transfers between devices, split_send(): return lax.ppermute(value, ('fsdp', 'tensor'), self.split)  39.5 us
    ppermute x17, waiting for transfers between devices, swap_y(): return lax.ppermute(value, 'tensor', SWAP_Y)  36.7 us
    ppermute x16, starting transfers between devices, split_send(): return lax.ppermute(value, ('fsdp', 'tensor'), self.split)  26.2 us
    ppermute x17, starting transfers between devices, swap_y(): return lax.ppermute(value, 'tensor', SWAP_Y)  21.3 us
    ppermute x16, starting transfers between devices, send_both(): lax.ppermute(ahead, 'fsdp', self.pairs[0])  19.8 us
    ppermute x16, starting transfers between devices, send_both(): lax.ppermute(behind, 'fsdp', self.pairs[1])  13.4 us
    unnamed x264, local copies, waits for them, and re-layouts  11.1 us
  transfers between devices with their start and end apart: 101, of which 34 were waited for; matrix products, arithmetic and copies ran while one was open for 3% of the time, Pallas kernels for 25%

profile of v3, /device:TPU:0, one launch (start us, length us, event | category | flops | bytes accessed | tf_op | source)
XLA Modules:
  0.0 340.9 jit_solution(8341635410577637829)
XLA Ops:
  5.4 2.6 collective-permute-start
  12.5 2.7 collective-permute-done.2
  18.9 3.9 %collective-permute-done.5 = bf16[96,1536]{1,0:T(8,128)(2,1)S(1)} collective-permute-done((bf16[96,1536]{1,0:T(8,128)(2,1)}, bf16[96,1536]{1,0:T(8,128)(2,1)S(1)}, u32[]{:S(2)}, u32[]{:S(2)}) %collective-permute-start.5) | collective-permute-done | bytes 294944 | tf_op jit(solution)/shard_map/ppermute | solution.py:72
  25.3 4.2 %collective-permute-done.7 = bf16[96,1536]{1,0:T(8,128)(2,1)S(1)} collective-permute-done((bf16[96,1536]{1,0:T(8,128)(2,1)S(1)}, bf16[96,1536]{1,0:T(8,128)(2,1)S(1)}, u32[]{:S(2)}, u32[]{:S(2)}) %collective-permute-start.7) | collective-permute-done | bytes 294944 | tf_op jit(solution)/shard_map/ppermute | solution.py:72
  44.3 4.1 %shard_map.321 = (bf16[256,384]{1,0:T(8,128)(2,1)S(1)}, f32[8,256]{1,0:T(8,128)S(1)}, bf16[256,768]{1,0:T(8,128)(2,1)S(1)}) custom-call(bf16[256,384]{1,0:T(8,128)(2,1)S(1)} %get-tuple-element.298.q_ref, bf16[256,128]{1,0:T(8,128)(2,1)S(1)} %get-tuple-element.300.qm_ref, bf16[256,768]{1,0:T(8,128)(2,1)S(1)} %get-tuple-element.287.refs_0_, ...), custom_call_target="tpu_custom_call" | custom-call | flops 4000000000 | bytes 1024 | tf_op jit(solution)/shard_map/pallas_call | solution.py:199
  50.2 4.1 %shard_map.319 = (bf16[256,384]{1,0:T(8,128)(2,1)S(1)}, f32[8,256]{1,0:T(8,128)S(1)}, bf16[256,768]{1,0:T(8,128)(2,1)S(1)}) custom-call(bf16[256,384]{1,0:T(8,128)(2,1)S(1)} %get-tuple-element.284.q_ref, bf16[256,128]{1,0:T(8,128)(2,1)S(1)} %get-tuple-element.286.qm_ref, bf16[256,768]{1,0:T(8,128)(2,1)S(1)} %get-tuple-element.287.refs_0_, ...), custom_call_target="tpu_custom_call" | custom-call | flops 4000000000 | bytes 1024 | tf_op jit(solution)/shard_map/pallas_call | solution.py:199
  56.7 8.2 %collective-permute-done.20 = bf16[96,3072]{1,0:T(8,128)(2,1)S(1)} collective-permute-done((bf16[96,3072]{1,0:T(8,128)(2,1)S(1)}, bf16[96,3072]{1,0:T(8,128)(2,1)S(1)}, u32[]{:S(2)}, u32[]{:S(2)}) %collective-permute-start.20) | collective-permute-done | bytes 589856 | tf_op jit(solution)/shard_map/ppermute | solution.py:72
  68.2 3.4 collective-permute-done.22
  81.2 2.8 shard_map.322
  89.3 2.8 shard_map.323
  105.8 2.8 shard_map.324
  110.8 4.1 %shard_map.327 = (bf16[256,384]{1,0:T(8,128)(2,1)S(1)}, f32[8,256]{1,0:T(8,128)S(1)}, bf16[256,768]{1,0:T(8,128)(2,1)S(1)}) custom-call(bf16[256,384]{1,0:T(8,128)(2,1)S(1)} %get-tuple-element.324.q_ref, bf16[256,128]{1,0:T(8,128)(2,1)S(1)} %get-tuple-element.300.qm_ref, bf16[256,768]{1,0:T(8,128)(2,1)S(1)} %get-tuple-element.317.refs_0_, ...), custom_call_target="tpu_custom_call" | custom-call | flops 4000000000 | bytes 1024 | tf_op jit(solution)/shard_map/pallas_call | solution.py:199
  117.0 4.1 %shard_map.326 = (bf16[256,384]{1,0:T(8,128)(2,1)S(1)}, f32[8,256]{1,0:T(8,128)S(1)}, bf16[256,768]{1,0:T(8,128)(2,1)S(1)}) custom-call(bf16[256,384]{1,0:T(8,128)(2,1)S(1)} %get-tuple-element.316.q_ref, bf16[256,128]{1,0:T(8,128)(2,1)S(1)} %get-tuple-element.286.qm_ref, bf16[256,768]{1,0:T(8,128)(2,1)S(1)} %get-tuple-element.317.refs_0_, ...), custom_call_target="tpu_custom_call" | custom-call | flops 4000000000 | bytes 1024 | tf_op jit(solution)/shard_map/pallas_call | solution.py:199
  123.4 8.2 %collective-permute-done.42 = bf16[96,3072]{1,0:T(8,128)(2,1)S(1)} collective-permute-done((bf16[96,3072]{1,0:T(8,128)(2,1)S(1)}, bf16[96,3072]{1,0:T(8,128)(2,1)S(1)}, u32[]{:S(2)}, u32[]{:S(2)}) %collective-permute-start.42) | collective-permute-done | bytes 589856 | tf_op jit(solution)/shard_map/ppermute | solution.py:72
  133.5 5.1 %collective-permute-done.44 = bf16[48,3072]{1,0:T(8,128)(2,1)S(1)} collective-permute-done((bf16[48,3072]{1,0:T(8,128)(2,1)S(1)}, bf16[48,3072]{1,0:T(8,128)(2,1)S(1)}, u32[]{:S(2)}, u32[]{:S(2)}) %collective-permute-start.44) | collective-permute-done | bytes 294944 | tf_op jit(solution)/shard_map/ppermute | solution.py:72
  140.2 3.7 %shard_map.329 = (f32[256,768]{1,0:T(8,128)S(1)}, bf16[256,768]{1,0:T(8,128)(2,1)S(1)}, bf16[256,1536]{1,0:T(8,128)(2,1)S(1)}, bf16[256,1536]{1,0:T(8,128)(2,1)S...) custom-call(f32[256,768]{1,0:T(8,128)S(1)} %get-tuple-element.315.refs_0_.state_ref, ...), custom_call_target="tpu_custom_call" | custom-call | flops 4000000000 | bytes 1024 | tf_op jit(solution)/shard_map/pallas_call | solution.py:199
  146.1 4.5 %shard_map.330 = (f32[256,768]{1,0:T(8,128)S(1)}, bf16[256,768]{1,0:T(8,128)(2,1)S(1)}, bf16[256,1536]{1,0:T(8,128)(2,1)S(1)}, bf16[256,1536]{1,0:T(8,128)(2,1)S...) custom-call(f32[256,768]{1,0:T(8,128)S(1)} %get-tuple-element.334.refs_0_.state_ref, ...), custom_call_target="tpu_custom_call" | custom-call | flops 4000000000 | bytes 1024 | tf_op jit(solution)/shard_map/pallas_call | solution.py:199
  151.4 4.3 %collective-permute-done.49.arrived_ref = bf16[256,768]{1,0:T(8,128)(2,1)S(1)} collective-permute-done((bf16[256,768]{1,0:T(8,128)(2,1)S(1)}, bf16[256,768]{1,0:T(8,128)(2,1)S(1)}, u32[]{:S(2)}, u32[]{:S(2)}) %collective-permute-start.49) | collective-permute-done | bytes 393248 | tf_op jit(solution)/shard_map/ppermute | solution.py:26
  155.8 7.7 %shard_map.331 = (f32[256,768]{1,0:T(8,128)S(1)}, bf16[256,768]{1,0:T(8,128)(2,1)S(1)}, f32[8,768]{1,0:T(8,128)S(1)}, bf16[256,384]{1,0:T(8,128)(2,1)S(1)}, bf16...) custom-call(bf16[256,768]{1,0:T(8,128)(2,1)S(1)} %get-tuple-element.332.refs_8_.grads_ref.l0, ...), custom_call_target="tpu_custom_call" | custom-call | flops 1000000000 | bytes 1024 | tf_op jit(solution)/shard_map/pallas_call | solution.py:199
  163.7 4.1 %shard_map.332 = (bf16[768,1536]{1,0:T(8,128)(2,1)}, bf16[768,1536]{1,0:T(8,128)(2,1)S(1)}) custom-call(s32[1]{0:T(128)} %bitcast.1.core_ref, bf16[256,768]{1,0:T(8,128)(2,1)S(1)} %get-tuple-element.340.s0, bf16[256,768]{1,0:T(8,128)(2,1)S(1)} %get-tuple-element.341.s1, bf16[256,1536]{1,0:T(8,128)(2,1)S(1)} %get-tuple-element.348.g0, ...), custom_call_target="tpu_custom_call" | custom-call | flops 3400000000 | bytes 1024 | tf_op jit(solution)/shard_map/pallas_call | solution.py:199
  169.5 10.2 %collective-permute-done.48.arrived_ref = bf16[256,768]{1,0:T(8,128)(2,1)} collective-permute-done((bf16[256,768]{1,0:T(8,128)(2,1)}, bf16[256,768]{1,0:T(8,128)(2,1)}, u32[]{:S(2)}, u32[]{:S(2)}) %collective-permute-start.48) | collective-permute-done | bytes 393248 | tf_op jit(solution)/shard_map/ppermute | solution.py:26
  182.2 9.0 %shard_map.335 = (f32[256,768]{1,0:T(8,128)S(1)}, bf16[256,768]{1,0:T(8,128)(2,1)S(1)}, f32[8,768]{1,0:T(8,128)S(1)}, bf16[256,384]{1,0:T(8,128)(2,1)S(1)}, bf16...) custom-call(bf16[256,768]{1,0:T(8,128)(2,1)S(1)} %copy-done.40, bf16[256,768]{1,0:T(8,128)(2,1)} %get-tuple-element.361.part_ref, ...), custom_call_target="tpu_custom_call" | custom-call | flops 1000000000 | bytes 1024 | tf_op jit(solution)/shard_map/pallas_call | solution.py:199
  194.7 2.8 shard_map.337
  205.3 6.1 %collective-permute-done.54.arrived_ref = bf16[256,768]{1,0:T(8,128)(2,1)S(1)} collective-permute-done((bf16[256,768]{1,0:T(8,128)(2,1)S(1)}, bf16[256,768]{1,0:T(8,128)(2,1)S(1)}, u32[]{:S(2)}, u32[]{:S(2)}) %collective-permute-start.54) | collective-permute-done | bytes 393248 | tf_op jit(solution)/shard_map/ppermute | solution.py:26
  218.5 2.6 shard_map.342
  221.1 3.5 %collective-permute-done.60.refs_0_ = bf16[96,1536]{1,0:T(8,128)(2,1)S(1)} collective-permute-done((bf16[96,1536]{1,0:T(8,128)(2,1)S(1)}, bf16[96,1536]{1,0:T(8,128)(2,1)S(1)}, u32[]{:S(2)}, u32[]{:S(2)}) %collective-permute-start.60) | collective-permute-done | bytes 294944 | tf_op jit(solution)/shard_map/ppermute | solution.py:75
  229.3 2.5 shard_map.345
  231.9 3.5 %shard_map.348 = (bf16[768,1536]{1,0:T(8,128)(2,1)S(1)}, bf16[768,1536]{1,0:T(8,128)(2,1)S(1)}) custom-call(s32[1]{0:T(128)} %bitcast.1.core_ref, bf16[256,768]{1,0:T(8,128)(2,1)S(1)} %copy-done.118, bf16[256,768]{1,0:T(8,128)(2,1)S(1)} %copy-done.120, bf16[256,1536]{1,0:T(8,128)(2,1)S(1)} %get-tuple-element.436.g0, ...), custom_call_target="tpu_custom_call" | custom-call | flops 3400000000 | bytes 1024 | tf_op jit(solution)/shard_map/pallas_call | solution.py:199
  239.6 7.9 %collective-permute-done.58.arrived_ref = bf16[256,768]{1,0:T(8,128)(2,1)S(1)} collective-permute-done((bf16[256,768]{1,0:T(8,128)(2,1)S(1)}, bf16[256,768]{1,0:T(8,128)(2,1)S(1)}, u32[]{:S(2)}, u32[]{:S(2)}) %collective-permute-start.58) | collective-permute-done | bytes 393248 | tf_op jit(solution)/shard_map/ppermute | solution.py:26
  257.6 6.5 %shard_map.349 = (f32[256,768]{1,0:T(8,128)S(1)}, bf16[256,768]{1,0:T(8,128)(2,1)S(1)}, f32[8,768]{1,0:T(8,128)S(1)}, bf16[256,384]{1,0:T(8,128)(2,1)S(1)}, bf16...) custom-call(f32[256,768]{1,0:T(8,128)S(1)} %get-tuple-element.395.grads_ref, ...), custom_call_target="tpu_custom_call" | custom-call | flops 1000000000 | bytes 1024 | tf_op jit(solution)/shard_map/pallas_call | solution.py:199
  267.1 6.5 %shard_map.352 = (f32[256,768]{1,0:T(8,128)S(1)}, bf16[256,768]{1,0:T(8,128)(2,1)S(1)}, f32[8,768]{1,0:T(8,128)S(1)}, bf16[256,384]{1,0:T(8,128)(2,1)S(1)}, bf16...) custom-call(f32[256,768]{1,0:T(8,128)S(1)} %get-tuple-element.446.grads_ref, ...), custom_call_target="tpu_custom_call" | custom-call | flops 1000000000 | bytes 1024 | tf_op jit(solution)/shard_map/pallas_call | solution.py:199
  276.1 2.4 shard_map.353
  (544 shorter events, 186.6 us)
Async XLA Ops:
  5.4 30.7 %collective-permute-start = (bf16[256,768]{1,0:T(8,128)(2,1)}, bf16[256,768]{1,0:T(8,128)(2,1)S(1)}, u32[]{:S(2)}, u32[]{:S(2)}) collective-permute-start(bf16[256,768]{1,0:T(8,128)(2,1)} %own_ref.1), channel_id=1, source_target_pairs={{0,2},{2,0},{1,3},{3,1},{4,6},{6,4},{5,7},{7,5},{8,10},{10,8},{9,1... | collective-permute-start | bytes 1179656 | tf_op jit(solution)/shard_map/ppermute | solution.py:26
  31.1 11.3 %collective-permute-start.16 = (bf16[96,3072]{1,0:T(8,128)(2,1)S(1)}, bf16[96,3072]{1,0:T(8,128)(2,1)S(1)}, u32[]{:S(2)}, u32[]{:S(2)}) collective-permute-start(bf16[96,3072]{1,0:T(8,128)(2,1)S(1)} %get-tuple-element.297), channel_id=1, source_target_pairs={{0,8},{8,16},{16,24},{24,28},{28,20},{20,12},{12,4},{4,0},{1,5},{9... | collective-permute-start | bytes 1769480 | tf_op jit(solution)/shard_map/ppermute | solution.py:72
  40.9 67.8 %collective-permute-start.46 = (bf16[256,768]{1,0:T(8,128)(2,1)S(1)}, bf16[256,768]{1,0:T(8,128)(2,1)S(1)}, u32[]{:S(2)}, u32[]{:S(2)}) collective-permute-start(bf16[256,768]{1,0:T(8,128)(2,1)S(1)} %copy-done.73), channel_id=1, source_target_pairs={{0,2},{2,0},{1,3},{3,1},{4,6},{6,4},{5,7},{7,5},{8,10},{10,8},{9,1... | collective-permute-start | bytes 1179656 | tf_op jit(solution)/shard_map/ppermute | solution.py:26
  42.4 12.5 %collective-permute-start.18 = (bf16[96,3072]{1,0:T(8,128)(2,1)S(1)}, bf16[96,3072]{1,0:T(8,128)(2,1)S(1)}, u32[]{:S(2)}, u32[]{:S(2)}) collective-permute-start(bf16[96,3072]{1,0:T(8,128)(2,1)S(1)} %collective-permute-done.16), channel_id=1, source_target_pairs={{0,8},{8,16},{16,24},{24,28},{28,20},{20,12},{12,4},{4,0},{1,5},{9... | collective-permute-start | bytes 1769480 | tf_op jit(solution)/shard_map/ppermute | solution.py:72
  44.2 12.3 %collective-permute-start.17 = (bf16[96,3072]{1,0:T(8,128)(2,1)S(1)}, bf16[96,3072]{1,0:T(8,128)(2,1)S(1)}, u32[]{:S(2)}, u32[]{:S(2)}) collective-permute-start(bf16[96,3072]{1,0:T(8,128)(2,1)S(1)} %collective-permute-done.16), channel_id=1, source_target_pairs={{0,1},{1,0},{2,3},{3,2},{4,5},{5,4},{6,7},{7,6},{8,9},{9,8},{10,11... | collective-permute-start | bytes 1769480 | tf_op jit(solution)/shard_map/ppermute | solution.py:22
  49.7 39.6 %collective-permute-start.25 = (bf16[256,768]{1,0:T(8,128)(2,1)S(1)}, bf16[256,768]{1,0:T(8,128)(2,1)S(1)}, u32[]{:S(2)}, u32[]{:S(2)}) collective-permute-start(bf16[256,768]{1,0:T(8,128)(2,1)S(1)} %get-tuple-element.301.refs_1_), channel_id=1, source_target_pairs={{0,2},{2,0},{1,3},{3,1},{4,6},{6,4},{5,7},{7,5},{8,10},{10,8},{9,1... | collective-permute-start | bytes 1179656 | tf_op jit(solution)/shard_map/ppermute | solution.py:26
  56.5 11.5 %collective-permute-start.19 = (bf16[96,3072]{1,0:T(8,128)(2,1)S(1)}, bf16[96,3072]{1,0:T(8,128)(2,1)S(1)}, u32[]{:S(2)}, u32[]{:S(2)}) collective-permute-start(bf16[96,3072]{1,0:T(8,128)(2,1)S(1)} %collective-permute-done.18), channel_id=1, source_target_pairs={{0,1},{1,0},{2,3},{3,2},{4,5},{5,4},{6,7},{7,6},{8,9},{9,8},{10,11... | collective-permute-start | bytes 1769480 | tf_op jit(solution)/shard_map/ppermute | solution.py:22
  74.8 12.5 %collective-permute-start.28 = (bf16[96,1536]{1,0:T(8,128)(2,1)S(1)}, bf16[96,1536]{1,0:T(8,128)(2,1)S(1)}, u32[]{:S(2)}, u32[]{:S(2)}) collective-permute-start(bf16[96,1536]{1,0:T(8,128)(2,1)S(1)} %collective-permute-done.26), channel_id=1, source_target_pairs={{0,8},{8,16},{16,24},{24,28},{28,20},{20,12},{12,4},{4,0},{1,5},{9... | collective-permute-start | bytes 884744 | tf_op jit(solution)/shard_map/ppermute | solution.py:72
  78.7 14.1 %collective-permute-start.27 = (bf16[96,1536]{1,0:T(8,128)(2,1)S(1)}, bf16[96,1536]{1,0:T(8,128)(2,1)S(1)}, u32[]{:S(2)}, u32[]{:S(2)}) collective-permute-start(bf16[96,1536]{1,0:T(8,128)(2,1)S(1)} %collective-permute-done.26), channel_id=1, source_target_pairs={{0,1},{1,0},{2,3},{3,2},{4,5},{5,4},{6,7},{7,6},{8,9},{9,8},{10,11... | collective-permute-start | bytes 884744 | tf_op jit(solution)/shard_map/ppermute | solution.py:22
  85.8 12.1 %collective-permute-start.24 = (bf16[256,768]{1,0:T(8,128)(2,1)S(1)}, bf16[256,768]{1,0:T(8,128)(2,1)S(1)}, u32[]{:S(2)}, u32[]{:S(2)}) collective-permute-start(bf16[256,768]{1,0:T(8,128)(2,1)S(1)} %get-tuple-element.307.part_ref), channel_id=1, source_target_pairs={{0,2},{2,0},{1,3},{3,1},{4,6},{6,4},{5,7},{7,5},{8,10},{10,8},{9,1... | collective-permute-start | bytes 1179656 | tf_op jit(solution)/shard_map/ppermute | solution.py:26
  109.0 12.7 %collective-permute-start.40 = (bf16[96,3072]{1,0:T(8,128)(2,1)S(1)}, bf16[96,3072]{1,0:T(8,128)(2,1)S(1)}, u32[]{:S(2)}, u32[]{:S(2)}) collective-permute-start(bf16[96,3072]{1,0:T(8,128)(2,1)S(1)} %collective-permute-done.38), channel_id=1, source_target_pairs={{0,8},{8,16},{16,24},{24,28},{28,20},{20,12},{12,4},{4,0},{1,5},{9... | collective-permute-start | bytes 1769480 | tf_op jit(solution)/shard_map/ppermute | solution.py:72
  110.6 12.6 %collective-permute-start.39 = (bf16[96,3072]{1,0:T(8,128)(2,1)S(1)}, bf16[96,3072]{1,0:T(8,128)(2,1)S(1)}, u32[]{:S(2)}, u32[]{:S(2)}) collective-permute-start(bf16[96,3072]{1,0:T(8,128)(2,1)S(1)} %collective-permute-done.38), channel_id=1, source_target_pairs={{0,1},{1,0},{2,3},{3,2},{4,5},{5,4},{6,7},{7,6},{8,9},{9,8},{10,11... | collective-permute-start | bytes 1769480 | tf_op jit(solution)/shard_map/ppermute | solution.py:22
  115.5 30.6 %collective-permute-start.47 = (bf16[256,768]{1,0:T(8,128)(2,1)S(1)}, bf16[256,768]{1,0:T(8,128)(2,1)S(1)}, u32[]{:S(2)}, u32[]{:S(2)}) collective-permute-start(bf16[256,768]{1,0:T(8,128)(2,1)S(1)} %get-tuple-element.326.refs_1_), channel_id=1, source_target_pairs={{0,2},{2,0},{1,3},{3,1},{4,6},{6,4},{5,7},{7,5},{8,10},{10,8},{9,1... | collective-permute-start | bytes 1179656 | tf_op jit(solution)/shard_map/ppermute | solution.py:26
  121.2 19.1 %collective-permute-start.37 = (bf16[256,768]{1,0:T(8,128)(2,1)S(1)}, bf16[256,768]{1,0:T(8,128)(2,1)S(1)}, u32[]{:S(2)}, u32[]{:S(2)}) collective-permute-start(bf16[256,768]{1,0:T(8,128)(2,1)S(1)} %get-tuple-element.321.refs_1_), channel_id=1, source_target_pairs={{0,2},{2,0},{1,3},{3,1},{4,6},{6,4},{5,7},{7,5},{8,10},{10,8},{9,1... | collective-permute-start | bytes 1179656 | tf_op jit(solution)/shard_map/ppermute | solution.py:26
  167.8 11.9 %collective-permute-start.50 = (bf16[768,1536]{1,0:T(8,128)(2,1)}, bf16[768,1536]{1,0:T(8,128)(2,1)}, u32[]{:S(2)}, u32[]{:S(2)}) collective-permute-start(bf16[768,1536]{1,0:T(8,128)(2,1)} %get-tuple-element.351), channel_id=1, source_target_pairs={{0,1},{1,0},{2,3},{3,2},{4,5},{5,4},{6,7},{7,6},{8,9},{9,8},{10,11... | collective-permute-start | bytes 7077896 | tf_op jit(solution)/shard_map/ppermute | solution.py:22
  167.9 11.8 %collective-permute-start.48 = (bf16[256,768]{1,0:T(8,128)(2,1)}, bf16[256,768]{1,0:T(8,128)(2,1)}, u32[]{:S(2)}, u32[]{:S(2)}) collective-permute-start(bf16[256,768]{1,0:T(8,128)(2,1)} %get-tuple-element.361.part_ref), channel_id=1, source_target_pairs={{0,2},{2,0},{1,3},{3,1},{4,6},{6,4},{5,7},{7,5},{8,10},{10,8},{9,1... | collective-permute-start | bytes 1179656 | tf_op jit(solution)/shard_map/ppermute | solution.py:26
  199.2 12.1 %collective-permute-start.55 = (bf16[768,768]{1,0:T(8,128)(2,1)S(1)}, bf16[768,768]{1,0:T(8,128)(2,1)S(1)}, u32[]{:S(2)}, u32[]{:S(2)}) collective-permute-start(bf16[768,768]{1,0:T(8,128)(2,1)S(1)} %shard_map.339), channel_id=1, source_target_pairs={{0,1},{1,0},{2,3},{3,2},{4,5},{5,4},{6,7},{7,6},{8,9},{9,8},{10,11... | collective-permute-start | bytes 3538952 | tf_op jit(solution)/shard_map/ppermute | solution.py:22
  199.4 11.9 %collective-permute-start.54 = (bf16[256,768]{1,0:T(8,128)(2,1)S(1)}, bf16[256,768]{1,0:T(8,128)(2,1)S(1)}, u32[]{:S(2)}, u32[]{:S(2)}) collective-permute-start(bf16[256,768]{1,0:T(8,128)(2,1)S(1)} %get-tuple-element.373.part_ref), channel_id=1, source_target_pairs={{0,2},{2,0},{1,3},{3,1},{4,6},{6,4},{5,7},{7,5},{8,10},{10,8},{9,1... | collective-permute-start | bytes 1179656 | tf_op jit(solution)/shard_map/ppermute | solution.py:26
  203.1 17.9 %collective-permute-start.59 = (bf16[256,768]{1,0:T(8,128)(2,1)S(1)}, bf16[256,768]{1,0:T(8,128)(2,1)S(1)}, u32[]{:S(2)}, u32[]{:S(2)}) collective-permute-start(bf16[256,768]{1,0:T(8,128)(2,1)S(1)} %get-tuple-element.398.part_ref), channel_id=1, source_target_pairs={{0,2},{2,0},{1,3},{3,1},{4,6},{6,4},{5,7},{7,5},{8,10},{10,8},{9,1... | collective-permute-start | bytes 1179656 | tf_op jit(solution)/shard_map/ppermute | solution.py:26
  214.3 13.4 %collective-permute-start.62 = (bf16[48,768]{1,0:T(8,128)(2,1)S(1)}, bf16[48,768]{1,0:T(8,128)(2,1)S(1)}, u32[]{:S(2)}, u32[]{:S(2)}) collective-permute-start(bf16[48,768]{1,0:T(8,128)(2,1)S(1)} %get-tuple-element.407), channel_id=1, source_target_pairs={{0,8},{8,16},{16,24},{24,28},{28,20},{20,12},{12,4},{4,0},{1,9},{9... | collective-permute-start | bytes 221192 | tf_op jit(solution)/shard_map/ppermute | solution.py:75
  215.9 11.9 %collective-permute-start.63 = (bf16[48,768]{1,0:T(8,128)(2,1)S(1)}, bf16[48,768]{1,0:T(8,128)(2,1)S(1)}, u32[]{:S(2)}, u32[]{:S(2)}) collective-permute-start(bf16[48,768]{1,0:T(8,128)(2,1)S(1)} %get-tuple-element.408), channel_id=1, source_target_pairs={{0,4},{8,0},{16,8},{24,16},{28,24},{20,28},{12,20},{4,12},{1,5},{9... | collective-permute-start | bytes 221192 | tf_op jit(solution)/shard_map/ppermute | solution.py:75
  235.4 28.7 %collective-permute-start.69 = (bf16[768,1536]{1,0:T(8,128)(2,1)S(1)}, bf16[768,1536]{1,0:T(8,128)(2,1)S(1)}, u32[]{:S(2)}, u32[]{:S(2)}) collective-permute-start(bf16[768,1536]{1,0:T(8,128)(2,1)S(1)} %get-tuple-element.449), channel_id=1, source_target_pairs={{0,1},{1,0},{2,3},{3,2},{4,5},{5,4},{6,7},{7,6},{8,9},{9,8},{10,11... | collective-permute-start | bytes 7077896 | tf_op jit(solution)/shard_map/ppermute | solution.py:22
  235.5 12.0 %collective-permute-start.58 = (bf16[256,768]{1,0:T(8,128)(2,1)S(1)}, bf16[256,768]{1,0:T(8,128)(2,1)S(1)}, u32[]{:S(2)}, u32[]{:S(2)}) collective-permute-start(bf16[256,768]{1,0:T(8,128)(2,1)S(1)} %get-tuple-element.396.part_ref), channel_id=1, source_target_pairs={{0,2},{2,0},{1,3},{3,1},{4,6},{6,4},{5,7},{7,5},{8,10},{10,8},{9,1... | collective-permute-start | bytes 1179656 | tf_op jit(solution)/shard_map/ppermute | solution.py:26
  237.0 11.6 %collective-permute-start.64 = (bf16[96,1536]{1,0:T(8,128)(2,1)S(1)}, bf16[96,1536]{1,0:T(8,128)(2,1)S(1)}, u32[]{:S(2)}, u32[]{:S(2)}) collective-permute-start(bf16[96,1536]{1,0:T(8,128)(2,1)S(1)} %get-tuple-element.418), channel_id=1, source_target_pairs={{0,8},{8,16},{16,24},{24,28},{28,20},{20,12},{12,4},{4,0},{1,9},{9... | collective-permute-start | bytes 884744 | tf_op jit(solution)/shard_map/ppermute | solution.py:75
  238.2 11.3 %collective-permute-start.65 = (bf16[96,1536]{1,0:T(8,128)(2,1)S(1)}, bf16[96,1536]{1,0:T(8,128)(2,1)S(1)}, u32[]{:S(2)}, u32[]{:S(2)}) collective-permute-start(bf16[96,1536]{1,0:T(8,128)(2,1)S(1)} %get-tuple-element.419), channel_id=1, source_target_pairs={{0,4},{8,0},{16,8},{24,16},{28,24},{20,28},{12,20},{4,12},{1,5},{9... | collective-permute-start | bytes 884744 | tf_op jit(solution)/shard_map/ppermute | solution.py:75
  239.0 17.4 %collective-permute-start.68 = (bf16[256,768]{1,0:T(8,128)(2,1)S(1)}, bf16[256,768]{1,0:T(8,128)(2,1)S(1)}, u32[]{:S(2)}, u32[]{:S(2)}) collective-permute-start(bf16[256,768]{1,0:T(8,128)(2,1)S(1)} %get-tuple-element.447.part_ref), channel_id=1, source_target_pairs={{0,2},{2,0},{1,3},{3,1},{4,6},{6,4},{5,7},{7,5},{8,10},{10,8},{9,1... | collective-permute-start | bytes 1179656 | tf_op jit(solution)/shard_map/ppermute | solution.py:26
  251.5 12.7 %collective-permute-start.70 = (bf16[96,1536]{1,0:T(8,128)(2,1)S(1)}, bf16[96,1536]{1,0:T(8,128)(2,1)S(1)}, u32[]{:S(2)}, u32[]{:S(2)}) collective-permute-start(bf16[96,1536]{1,0:T(8,128)(2,1)S(1)} %get-tuple-element.451), channel_id=1, source_target_pairs={{0,8},{8,16},{16,24},{24,28},{28,20},{20,12},{12,4},{4,0},{1,9},{9... | collective-permute-start | bytes 884744 | tf_op jit(solution)/shard_map/ppermute | solution.py:75
  252.7 11.5 %collective-permute-start.71 = (bf16[96,1536]{1,0:T(8,128)(2,1)S(1)}, bf16[96,1536]{1,0:T(8,128)(2,1)S(1)}, u32[]{:S(2)}, u32[]{:S(2)}) collective-permute-start(bf16[96,1536]{1,0:T(8,128)(2,1)S(1)} %get-tuple-element.452), channel_id=1, source_target_pairs={{0,4},{8,0},{16,8},{24,16},{28,24},{20,28},{12,20},{4,12},{1,5},{9... | collective-permute-start | bytes 884744 | tf_op jit(solution)/shard_map/ppermute | solution.py:75
  280.6 12.0 %collective-permute-start.76 = (bf16[256,768]{1,0:T(8,128)(2,1)S(1)}, bf16[256,768]{1,0:T(8,128)(2,1)S(1)}, u32[]{:S(2)}, u32[]{:S(2)}) collective-permute-start(bf16[256,768]{1,0:T(8,128)(2,1)S(1)} %get-tuple-element.474), channel_id=1, source_target_pairs={{0,2},{2,0},{1,3},{3,1},{4,6},{6,4},{5,7},{7,5},{8,10},{10,8},{9,1... | collective-permute-start | bytes 1179656 | tf_op jit(solution)/shard_map/ppermute | solution.py:26
  289.6 24.2 %collective-permute-start.52 = (bf16[256,768]{1,0:T(8,128)(2,1)S(1)}, bf16[256,768]{1,0:T(8,128)(2,1)S(1)}, u32[]{:S(2)}, u32[]{:S(2)}) collective-permute-start(bf16[256,768]{1,0:T(8,128)(2,1)S(1)} %get-tuple-element.365), channel_id=1, source_target_pairs={{0,2},{2,0},{1,3},{3,1},{4,6},{6,4},{5,7},{7,5},{8,10},{10,8},{9,1... | collective-permute-start | bytes 1179656 | tf_op jit(solution)/shard_map/ppermute | solution.py:26
  308.1 17.5 %collective-permute-start.92 = (bf16[96,1536]{1,0:T(8,128)(2,1)S(1)}, bf16[96,1536]{1,0:T(8,128)(2,1)S(1)}, u32[]{:S(2)}, u32[]{:S(2)}) collective-permute-start(bf16[96,1536]{1,0:T(8,128)(2,1)S(1)} %get-tuple-element.506), channel_id=1, source_target_pairs={{0,8},{8,16},{16,24},{24,28},{28,20},{20,12},{12,4},{4,0},{1,9},{9... | collective-permute-start | bytes 884744 | tf_op jit(solution)/shard_map/ppermute | solution.py:75
  309.0 18.2 %collective-permute-start.93 = (bf16[96,1536]{1,0:T(8,128)(2,1)S(1)}, bf16[96,1536]{1,0:T(8,128)(2,1)S(1)}, u32[]{:S(2)}, u32[]{:S(2)}) collective-permute-start(bf16[96,1536]{1,0:T(8,128)(2,1)S(1)} %get-tuple-element.507), channel_id=1, source_target_pairs={{0,4},{8,0},{16,8},{24,16},{28,24},{20,28},{12,20},{4,12},{1,5},{9... | collective-permute-start | bytes 884744 | tf_op jit(solution)/shard_map/ppermute | solution.py:75
  (201 other events, 2301.3 us)
